TPU v7x, 32 devices: a whole 2x2x4 slice. The times are simulated.
32 devices in a mesh: group: 2 (over x), expert: 16 (over z, y, core).
Axes of the slice: x: 2, y: 2, z: 4, core: 2. Of those that a mesh axis runs over, the one named last changes fastest.
Arguments:
- tokens: bfloat16 [64, 256, 1024], P(('group', 'expert')), parts along dimension 0, may hold values from -6 to 6
- w_qkv: bfloat16 [1024, 3072], P('expert'), may hold values from -0.1875 to 0.1875
- w_attn_out: bfloat16 [1024, 1024], P('expert'), may hold values from -0.1875 to 0.1875
- slot_keys: bfloat16 [1024, 32], replicated, may hold values from -0.5 to 0.5
- w_expert_in: bfloat16 [16, 1024, 2048], P('expert'), may hold values from -0.375 to 0.375
- w_expert_out: bfloat16 [16, 2048, 1024], P('expert'), may hold values from -0.125 to 0.125
Outputs:
- block_out: bfloat16 [64, 256, 1024], P(('group', 'expert')), parts along dimension 0
There are 2 independent parts, one for each index of `group`. A program takes and returns all parts, laid end to end along the dimension named above; an argument that names none is the same for every part. Nothing has to cross between parts.
All inputs are finite; a program needn't handle non-finite values.
Results may differ from a plain program's by a relative error of at most 0.009.
Values may be sent and summed in bfloat16 or wider, within the bound.
No kernel may reach another device: no remote copies, remote signals or barrier semaphores. Data moves between devices by JAX's collectives and lax.ppermute only.
A program may use at most 64 MiB of HBM per device.

v0:
```python
import math

import jax
import jax.numpy as jnp
from jax import lax
from jax.sharding import PartitionSpec as P

HEADS = 16


def layer_norm(values):
    center = values - jnp.mean(values, axis=-1, keepdims=True)
    spread = jnp.mean(center * center, axis=-1, keepdims=True)
    return center * lax.rsqrt(spread + 1e-06)


def on_device(tokens, w_qkv, w_attn_out, slot_keys, w_expert_in, w_expert_out):
    image_count, length, model_width = tokens.shape
    head_count = HEADS
    head_width = model_width // head_count
    row_count = image_count * length
    normed = (
        layer_norm(tokens.astype(jnp.float32)).astype(jnp.bfloat16).reshape(row_count, model_width)
    )
    full_qkv = lax.all_gather(w_qkv, "expert", axis=0, tiled=True)
    qkv = jnp.dot(normed, full_qkv, preferred_element_type=jnp.float32)
    packed = qkv.astype(jnp.bfloat16).reshape(image_count, length, 3, head_count, head_width)
    query = packed[:, :, 0]
    keys = packed[:, :, 1]
    values = packed[:, :, 2]
    scores = jnp.einsum(
        "bqhd,bkhd->bhqk", query, keys, preferred_element_type=jnp.float32
    ) / math.sqrt(head_width)
    weights = jax.nn.softmax(scores, axis=-1).astype(jnp.bfloat16)
    attended = jnp.einsum(
        "bhqk,bkhd->bqhd", weights, values, preferred_element_type=jnp.float32
    ).astype(jnp.bfloat16)
    attended = attended.reshape(row_count, model_width)
    full_out = lax.all_gather(w_attn_out, "expert", axis=0, tiled=True)
    projected = jnp.dot(attended, full_out, preferred_element_type=jnp.float32)
    resid = tokens.astype(jnp.float32) + projected.reshape(image_count, length, model_width)
    normed_two = layer_norm(resid).astype(jnp.bfloat16)
    slot_count = slot_keys.shape[1]
    logits = jnp.dot(
        normed_two.reshape(row_count, model_width), slot_keys, preferred_element_type=jnp.float32
    )
    logits = logits.reshape(image_count, length, slot_count)
    dispatch = jax.nn.softmax(logits, axis=1).astype(jnp.bfloat16)
    combine = jax.nn.softmax(logits, axis=2).astype(jnp.bfloat16)
    slot_inputs = jnp.einsum(
        "bsn,bsd->bnd", dispatch, normed_two, preferred_element_type=jnp.float32
    ).astype(jnp.bfloat16)
    sources = lax.axis_size("expert")
    expert_here = w_expert_in.shape[0]
    pairs = slot_count // (sources * expert_here)
    block = lax.all_to_all(slot_inputs, "expert", split_axis=1, concat_axis=1, tiled=True)
    batch = block.shape[0]
    arranged = block.reshape(batch, sources, expert_here, pairs, model_width)
    hidden = jnp.einsum(
        "bnepd,edh->bneph", arranged, w_expert_in, preferred_element_type=jnp.float32
    )
    hidden = jax.nn.gelu(hidden, approximate=False).astype(jnp.bfloat16)
    answer = jnp.einsum(
        "bneph,ehd->bnepd", hidden, w_expert_out, preferred_element_type=jnp.float32
    )
    answered = answer.astype(jnp.bfloat16).reshape(batch, slot_count, model_width)
    slot_outputs = lax.all_to_all(answered, "expert", split_axis=1, concat_axis=1, tiled=True)
    mixed = jnp.einsum("bsn,bnd->bsd", combine, slot_outputs, preferred_element_type=jnp.float32)
    return (resid + mixed).astype(jnp.bfloat16)


def solution(mesh):
    placed = (
        P(("group", "expert"), None, None),
        P("expert", None),
        P("expert", None),
        P(),
        P("expert", None, None),
        P("expert", None, None),
    )
    return jax.shard_map(
        on_device,
        mesh=mesh,
        in_specs=placed,
        out_specs=P(("group", "expert"), None, None),
        check_vma=False,
    )
```

profile of v0, /device:TPU:0, one launch (start us, length us, event | category | flops | bytes accessed | tf_op | source)
XLA Modules:
  0.0 159.9 jit_solution(4813306679087702941)
XLA Ops:
  6.5 0.7 all-gather.3.cloned.1.call-update
  7.3 0.7 all-gather.5.cloned.1.call-update
  8.0 1.4 convert_reduce_fusion
  9.5 0.4 fusion.14
  10.2 64.0 %all-gather.3.cloned.1.call-done = bf16[1024,3072]{1,0:T(8,128)(2,1)} async-done(((bf16[64,3072]{1,0:T(8,128)(2,1)}), bf16[1024,3072]{1,0:T(8,128)(2,1)}) %all-gather.3.cloned.1.call-update) | async-done | bytes 6291472 | tf_op jit(solution)/shard_map/all_gather | solution.py:25
  74.2 7.5 %convolution_convert_fusion = bf16[512,3072]{1,0:T(8,128)(2,1)} fusion(bf16[512,1024]{1,0:T(8,128)(2,1)S(1)} %bitcast.133, bf16[1024,3072]{1,0:T(8,128)(2,1)} %all-gather.3.cloned.1.call-done), kind=kOutput, calls=%fused_computation.7 | convolution fusion | flops 3222798336 | bytes 10485760 | tf_op jit(solution)/shard_map/dot_general | solution.py:26
  81.8 8.6 %reshape.80 = bf16[2,256,3,16,64]{4,3,2,1,0:T(8,128)(2,1)} reshape(bf16[512,3072]{1,0:T(8,128)(2,1)} %convolution_convert_fusion) | data formatting | bytes 6291456 | tf_op jit(solution)/shard_map/reshape | solution.py:27
  90.4 6.0 %fusion.110 = (bf16[2,256,1,16,64]{4,3,2,1,0:T(8,128)(2,1)S(1)}, bf16[2,256,1,16,64]{4,3,2,1,0:T(8,128)(2,1)}, bf16[2,256,1,16,64]{4,3,2,1,0:T(8,128)(2,1)}) fusion(bf16[2,256,3,16,64]{4,3,2,1,0:T(8,128)(2,1)} %reshape.80), kind=kLoop, calls=%fused_computation.118 | loop fusion | bytes 6291456 | tf_op jit(solution)/shard_map/slice | solution.py:30
  96.4 3.6 %copy.48 = bf16[2,256,1,16,64]{1,4,3,0,2:T(8,128)(2,1)} copy(bf16[2,256,1,16,64]{4,3,2,1,0:T(8,128)(2,1)} %get-tuple-element.6) | data formatting | bytes 2097152
  99.9 3.5 %copy.49 = bf16[2,256,1,16,64]{1,4,3,0,2:T(8,128)(2,1)} copy(bf16[2,256,1,16,64]{4,3,2,1,0:T(8,128)(2,1)} %get-tuple-element.7) | data formatting | bytes 2097152
  103.5 2.5 %copy.47 = bf16[2,256,1,16,64]{1,4,3,0,2:T(8,128)(2,1)} copy(bf16[2,256,1,16,64]{4,3,2,1,0:T(8,128)(2,1)S(1)} %get-tuple-element.5) | data formatting | bytes 2097152
  106.0 2.8 %fusion.31 = f32[2,16,256,256]{2,3,1,0:T(8,128)S(1)} fusion(bf16[2,256,1,16,64]{1,4,3,0,2:T(8,128)(2,1)} %copy.49, bf16[2,256,1,16,64]{1,4,3,0,2:T(8,128)(2,1)} %copy.48), kind=kOutput, calls=%fused_computation.34 | convolution fusion | flops 268435456 | bytes 10485760 | tf_op jit(solution)/shard_map/bqhd,bkhd->bhqk/dot_general | solution.py:31
  108.8 6.3 %fusion.111 = (f32[2,16,256]{2,1,0:T(8,128)S(1)}, f32[2,16,256,256]{2,3,1,0:T(8,128)S(1)}) fusion(f32[2,16,256,256]{2,3,1,0:T(8,128)S(1)} %fusion.31), kind=kOutput, calls=%fused_computation.119 | output fusion | flops 8388863 | bytes 16809984 | tf_op jit(solution)/shard_map/sub | solution.py:34
  115.1 1.8 %fusion.20 = bf16[2,16,64,256]{3,2,1,0:T(8,128)(2,1)} fusion(f32[2,16,256,256]{2,3,1,0:T(8,128)S(1)} %get-tuple-element.9, f32[2,16,256]{2,1,0:T(8,128)S(1)} %get-tuple-element.8, bf16[2,256,1,16,64]{1,4,3,0,2:T(8,128)(2,1)S(1)} %copy-done.2), kind=kOutput, calls=%fused_computation.26 | convolution fusion | flops 273154048 | bytes 10518528 | tf_op jit(solution)/shard_map/bhqk,bkhd->bqhd/dot_general | solution.py:35
  117.0 3.3 %fusion.112 = (f32[2,256]{1,0:T(2,128)S(1)}, f32[2,256,1024]{2,1,0:T(8,128)S(1)}) fusion(bf16[2,256,1024]{1,2,0:T(8,128)(2,1)} %bitcast.134, bf16[1024,1024]{1,0:T(8,128)(2,1)} %all-gather.5.cloned.1.call-done, bf16[2,256,1024]{2,1,0:T(8,128)(2,1)S(1)} %copy-done.1), kind=kOutput, calls=%fused_computation.120 | convolution fusion | flops 1075314176 | bytes 6293504 | tf_op jit(solution)/shard_map/dot_general | solution.py:40
  120.2 0.4 multiply_reduce_fusion.1
  120.6 0.5 fusion.54
  121.3 0.5 convolution_convert_fusion.1
  122.0 11.3 %all_to_all.10 = bf16[2,32,1024]{2,0,1:T(2,128)(2,1)S(1)} all-to-all(bf16[2,32,1024]{2,0,1:T(2,128)(2,1)S(1)} %copy.37), channel_id=1, replica_groups=mesh['group'=2,'expert'=16] {'expert'}, dimensions={1} | all-to-all | bytes 262144 | tf_op jit(solution)/shard_map/all_to_all | solution.py:56
  133.2 6.1 %fusion.24 = bf16[2,16,1,2,1024]{4,1,3,0,2:T(8,128)(2,1)S(1)} fusion(bf16[1,2048,1024]{2,1,0:T(8,128)(2,1)} %param.11, bf16[1,1024,2048]{2,1,0:T(8,128)(2,1)} %param.10, bf16[2,16,2,1024]{3,0,2,1:T(2,128)(2,1)S(1)} %bitcast.135), kind=kOutput, calls=%fused_computation.29 | convolution fusion | flops 545456128 | bytes 8650752 | tf_op jit(solution)/shard_map/bneph,ehd->bnepd/dot_general | solution.py:63
  139.3 0.8 copy.39
  140.1 3.5 %all-to-all-start.1 = ((bf16[2,32,1024]{2,0,1:T(2,128)(2,1)}), bf16[2,32,1024]{2,0,1:T(2,128)(2,1)S(1)}, u32[]{:S(2)}, u32[]{:S(2)}) async-start(bf16[2,32,1024]{2,0,1:T(2,128)(2,1)} %bitcast.27), calls=%async_computation.1 | async-start | bytes 262144 | tf_op jit(solution)/shard_map/all_to_all | solution.py:67
  143.7 7.9 %all-to-all-done.1 = bf16[2,32,1024]{2,0,1:T(2,128)(2,1)S(1)} async-done(((bf16[2,32,1024]{2,0,1:T(2,128)(2,1)}), bf16[2,32,1024]{2,0,1:T(2,128)(2,1)S(1)}, u32[]{:S(2)}, u32[]{:S(2)}) %all-to-all-start.1) | async-done | bytes 131104 | tf_op jit(solution)/shard_map/all_to_all | solution.py:67
  151.6 1.5 add_convert_fusion
  (17 shorter events, 0.8 us)
Async XLA Ops:
  6.5 114.1 %copy-start = (bf16[1024,32]{0,1:T(8,128)(2,1)S(1)}, bf16[1024,32]{0,1:T(8,128)(2,1)}, u32[]{:S(2)}) copy-start(bf16[1024,32]{0,1:T(8,128)(2,1)} %param.9) | copy-start | bytes 196612
  6.5 2.9 %copy-start.1 = (bf16[2,256,1024]{2,1,0:T(8,128)(2,1)S(1)}, bf16[2,256,1024]{2,1,0:T(8,128)(2,1)}, u32[]{:S(2)}) copy-start(bf16[2,256,1024]{2,1,0:T(8,128)(2,1)} %param.6) | copy-start | bytes 3145732
  6.5 67.7 %all-gather.3.cloned.1.call-start = ((), (), s32[]{:S(2)}) async-start(), calls=%async_computation.2 | async-start | bytes 6684672 | tf_op jit(solution)/shard_map/all_gather | solution.py:25
  7.3 109.7 %all-gather.5.cloned.1.call-start = ((), (), s32[]{:S(2)}) async-start(), calls=%async_computation.3 | async-start | bytes 2228224 | tf_op jit(solution)/shard_map/all_gather | solution.py:39
  108.8 6.3 %copy-start.2 = (bf16[2,256,1,16,64]{1,4,3,0,2:T(8,128)(2,1)S(1)}, bf16[2,256,1,16,64]{1,4,3,0,2:T(8,128)(2,1)}, u32[]{:S(2)}) copy-start(bf16[2,256,1,16,64]{1,4,3,0,2:T(8,128)(2,1)} %copy.47) | copy-start | bytes 3145732
  140.1 11.4 %all-to-all-start.1 = ((bf16[2,32,1024]{2,0,1:T(2,128)(2,1)}), bf16[2,32,1024]{2,0,1:T(2,128)(2,1)S(1)}, u32[]{:S(2)}, u32[]{:S(2)}) async-start(bf16[2,32,1024]{2,0,1:T(2,128)(2,1)} %bitcast.27), calls=%async_computation.1 | async-start | bytes 262144 | tf_op jit(solution)/shard_map/all_to_all | solution.py:67
Sparse Core Ops, SparseCore 0:
  9.6 64.5 all-gather.2
  76.4 39.9 all-gather.4
where the time goes:
time: 160 us
  waiting for transfers between devices  73.3 us (46%)
  local copies, waits for them, and re-layouts  25.1 us (16%)
  matrix products  24 us (15%)
  between operations  13.5 us (8%)
  blocking collectives  11.3 us (7%)
  other arithmetic  9.08 us (6%)
  starting transfers between devices  3.55 us (2%)
    all_gather x1, waiting for transfers between devices, on_device(): full_qkv = lax.all_gather(w_qkv, 'expert', axis=0, tiled=True)  64 us
    all_to_all x1, blocking collectives, on_device(): lax.all_to_all(slot_inputs, 'expert', split_axis=1, concat_axis=1, tiled=...  11.3 us
    unnamed x9, local copies, waits for them, and re-layouts  9.61 us
    reshape x1, local copies, waits for them, and re-layouts, on_device(): qkv.astype(jnp.bfloat16)  8.6 us
    all_to_all x1, waiting for transfers between devices, on_device(): lax.all_to_all(answered, 'expert', split_axis=1, concat_axis=1, tiled=True)  7.85 us
    dot_general x1, matrix products, on_device(): qkv = jnp.dot(normed, full_qkv, preferred_element_type=jnp.float32)  7.53 us
    sub x1, other arithmetic, on_device(): weights = jax.nn.softmax(scores, axis=-1).astype(jnp.bfloat16)  6.31 us
    dot_general x1, matrix products, on_device(): jnp.einsum('bneph,ehd->bnepd', hidden, w_expert_out, preferred_element_ty...  6.09 us
  transfers between devices with their start and end apart: 3, of which 2 were waited for; matrix products, arithmetic and copies ran while one was open for 28% of the time, Pallas kernels for 0%

commit v1 on v0

v1 whole, which is shorter than its diff:
```python
import functools

import jax
import jax.numpy as jnp
from jax import lax
from jax.experimental import pallas as pl
from jax.experimental.pallas import tpu as pltpu
from jax.sharding import PartitionSpec as P

HEADS = 16
AXES = ("group", "expert")
F32 = jnp.float32
BF16 = jnp.bfloat16


def layer_norm(values):
    center = values - jnp.mean(values, axis=-1, keepdims=True)
    spread = jnp.mean(center * center, axis=-1, keepdims=True)
    return center * lax.rsqrt(spread + 1e-06)


def is_grid(groups, experts):
    return groups == 2 and experts == 16


def pairs_of(groups, experts, move):
    result = []
    for group in range(groups):
        mask, flip = move(group)
        for expert in range(experts):
            target = (group ^ flip) * experts + (expert ^ mask)
            result.append((group * experts + expert, target))
    return result


def gather_blocks(own, groups, experts):
    def send(block, move):
        return lax.ppermute(block, AXES, pairs_of(groups, experts, move))

    def over_y(block):
        return send(block, lambda group: (2, 0))

    def over_x(block):
        return send(block, lambda group: (0, 1))

    def in_chip(block):
        return send(block, lambda group: (1, 0))

    far = send(own, lambda group: (12, 0) if group else (8, 0))
    near = send(own, lambda group: (4, 0))
    beside = over_y(own)
    beside_near = over_y(near)
    far_other = over_x(far)
    beside_far = over_y(far)
    beside_far_other = over_x(beside_far)
    blocks = [
        (own, 0, 0),
        (beside, 2, 2),
        (near, 4, 4),
        (beside_near, 6, 6),
        (far, 8, 12),
        (far_other, 12, 8),
        (beside_far, 10, 14),
        (beside_far_other, 14, 10),
    ]
    return blocks + [(in_chip(b), m0 ^ 1, m1 ^ 1) for b, m0, m1 in blocks]


def gather_weight(own, mesh_shape):
    groups, experts = mesh_shape
    rows = own.shape[0]
    if not is_grid(groups, experts):
        return [lax.all_gather(own, "expert", axis=0, tiled=True)], jnp.zeros((1,), jnp.int32)
    blocks = gather_blocks(own, groups, experts)
    masks = jnp.array([[b[1] for b in blocks], [b[2] for b in blocks]], jnp.int32)
    mine = jnp.where(lax.axis_index("group") == 0, masks[0], masks[1])
    starts = jnp.bitwise_xor(mine, lax.axis_index("expert")) * rows
    return [b[0] for b in blocks], starts.astype(jnp.int32)


def load_pieces(starts_ref, pieces, whole, sem):
    copies = []
    for at, piece in enumerate(pieces):
        rows = piece.shape[0]
        start = pl.multiple_of(starts_ref[at], rows)
        copy = pltpu.make_async_copy(piece, whole.at[pl.ds(start, rows)], sem.at[at])
        copy.start()
        copies.append(copy)
    return copies


def attention_kernel(count, images, length, *refs):
    starts_ref, tokens_ref = refs[:2]
    pieces = refs[2 : 2 + count]
    out_ref = refs[2 + count]
    weight, normed, sem = refs[3 + count :]
    copies = load_pieces(starts_ref, pieces, weight, sem)
    width = tokens_ref.shape[1]
    for image in range(images):
        rows = slice(image * length, (image + 1) * length)
        normed[rows] = layer_norm(tokens_ref[rows].astype(F32)).astype(BF16)
    for copy in copies:
        copy.wait()
    head = width // HEADS
    pair = 2 * head
    group = 2 * pair
    scale = head**-0.5
    lane = lax.broadcasted_iota(jnp.int32, (length, pair), 1)
    first = lane < head

    def heads(at, carry):
        base = pl.multiple_of(at * group, group)

        def project(offset):
            return jnp.dot(
                normed[...], weight[:, pl.ds(base + offset, group)], preferred_element_type=F32
            )

        query = (project(0) * scale).astype(BF16)
        keys = project(width).astype(BF16)
        values = project(2 * width).astype(BF16)
        for image in range(images):
            rows = slice(image * length, (image + 1) * length)
            for half in range(2):
                columns = slice(half * pair, (half + 1) * pair)
                q, k, v = query[rows, columns], keys[rows, columns], values[rows, columns]
                result = []
                for mask in (first, ~first):
                    scores = lax.dot_general(
                        jnp.where(mask, q, jnp.zeros_like(q)),
                        k,
                        (((1,), (1,)), ((), ())),
                        preferred_element_type=F32,
                    )
                    top = jnp.max(scores, axis=-1, keepdims=True)
                    weights = jnp.exp(scores - top).astype(BF16)
                    mixed = jnp.dot(
                        weights, jnp.where(mask, v, jnp.ones_like(v)), preferred_element_type=F32
                    )
                    result.append(mixed / pltpu.roll(mixed, head, 1))
                out_ref[rows, pl.ds(base + half * pair, pair)] = jnp.where(
                    first, result[0], result[1]
                ).astype(BF16)
        return carry

    lax.fori_loop(0, width // group, heads, 0)


def attention(tokens, pieces, starts, images, length):
    rows, width = tokens.shape
    count = len(pieces)
    return pl.pallas_call(
        functools.partial(attention_kernel, count, images, length),
        out_shape=jax.ShapeDtypeStruct((rows, width), BF16),
        in_specs=[pl.BlockSpec(memory_space=pltpu.SMEM), pl.BlockSpec(memory_space=pltpu.VMEM)]
        + [pl.BlockSpec(memory_space=pl.ANY)] * count,
        out_specs=pl.BlockSpec(memory_space=pltpu.VMEM),
        scratch_shapes=[
            pltpu.VMEM((width, 3 * width), BF16),
            pltpu.VMEM((rows, width), BF16),
            pltpu.SemaphoreType.DMA((count,)),
        ],
        compiler_params=pltpu.CompilerParams(vmem_limit_bytes=40 << 20),
        cost_estimate=pl.CostEstimate(
            flops=2 * rows * width * (3 * width + 4 * length),
            bytes_accessed=6 * width * width + 4 * rows * width,
            transcendentals=rows * HEADS * length,
        ),
        name="attention",
    )(starts, tokens, *pieces)


def router_kernel(count, images, length, *refs):
    starts_ref, attended_ref, tokens_ref, keys_ref = refs[:4]
    pieces = refs[4 : 4 + count]
    resid_ref, combine_ref, inputs_ref = refs[4 + count : 7 + count]
    weight, sem = refs[7 + count :]
    for copy in load_pieces(starts_ref, pieces, weight, sem):
        copy.wait()
    for image in range(images):
        rows = slice(image * length, (image + 1) * length)
        resid = tokens_ref[rows].astype(F32) + jnp.dot(
            attended_ref[rows], weight[...], preferred_element_type=F32
        )
        resid_ref[rows] = resid
        normed = layer_norm(resid).astype(BF16)
        logits = lax.dot_general(
            keys_ref[...], normed, (((1,), (1,)), ((), ())), preferred_element_type=F32
        )
        dispatch = jax.nn.softmax(logits, axis=1).astype(BF16)
        combine_ref[image] = jax.nn.softmax(logits, axis=0).astype(BF16)
        inputs_ref[image] = jnp.dot(dispatch, normed, preferred_element_type=F32).astype(BF16)


def router(attended, tokens, slot_keys, pieces, starts, images, length):
    rows, width = tokens.shape
    slots = slot_keys.shape[1]
    count = len(pieces)
    vmem = pl.BlockSpec(memory_space=pltpu.VMEM)
    return pl.pallas_call(
        functools.partial(router_kernel, count, images, length),
        out_shape=[
            jax.ShapeDtypeStruct((rows, width), F32),
            jax.ShapeDtypeStruct((images, slots, length), BF16),
            jax.ShapeDtypeStruct((images, slots, width), BF16),
        ],
        in_specs=[pl.BlockSpec(memory_space=pltpu.SMEM)]
        + [vmem] * 3
        + [pl.BlockSpec(memory_space=pl.ANY)] * count,
        out_specs=[vmem] * 3,
        scratch_shapes=[
            pltpu.VMEM((width, width), BF16),
            pltpu.SemaphoreType.DMA((count,)),
        ],
        compiler_params=pltpu.CompilerParams(vmem_limit_bytes=40 << 20),
        cost_estimate=pl.CostEstimate(
            flops=2 * rows * width * (width + 2 * slots),
            bytes_accessed=2 * width * width + 8 * rows * width,
            transcendentals=2 * rows * slots,
        ),
        name="router",
    )(starts, attended, tokens, slot_keys.T, *pieces)


def on_device(mesh_shape, tokens, w_qkv, w_attn_out, slot_keys, w_expert_in, w_expert_out):
    images, length, width = tokens.shape
    flat_tokens = tokens.reshape(images * length, width)
    qkv_pieces, qkv_starts = gather_weight(w_qkv, mesh_shape)
    out_pieces, out_starts = gather_weight(w_attn_out, mesh_shape)
    attended = attention(flat_tokens, qkv_pieces, qkv_starts, images, length)
    resid, combine, slot_inputs = router(
        attended, flat_tokens, slot_keys, out_pieces, out_starts, images, length
    )
    slots = slot_keys.shape[1]
    sources = mesh_shape[1]
    expert_here = w_expert_in.shape[0]
    pairs = slots // (sources * expert_here)
    block = lax.all_to_all(slot_inputs, "expert", split_axis=1, concat_axis=1, tiled=True)
    arranged = block.reshape(images, sources, expert_here, pairs, width)
    hidden = jnp.einsum("bnepd,edh->bneph", arranged, w_expert_in, preferred_element_type=F32)
    hidden = jax.nn.gelu(hidden, approximate=False).astype(BF16)
    answer = jnp.einsum("bneph,ehd->bnepd", hidden, w_expert_out, preferred_element_type=F32)
    answered = answer.astype(BF16).reshape(images, slots, width)
    slot_outputs = lax.all_to_all(answered, "expert", split_axis=1, concat_axis=1, tiled=True)
    mixed = jnp.einsum("bns,bnd->bsd", combine, slot_outputs, preferred_element_type=F32)
    return (resid.reshape(images, length, width) + mixed).astype(BF16)


def solution(mesh):
    placed = (
        P(AXES, None, None),
        P("expert", None),
        P("expert", None),
        P(),
        P("expert", None, None),
        P("expert", None, None),
    )
    return jax.shard_map(
        functools.partial(on_device, (mesh.shape["group"], mesh.shape["expert"])),
        mesh=mesh,
        in_specs=placed,
        out_specs=P(AXES, None, None),
        check_vma=False,
    )
```

time: 160 us -> 124 us (0.78)
  waiting for transfers between devices: 73.3 us -> 43.7 us
  Pallas kernels: 0 us -> 20.9 us
  local copies, waits for them, and re-layouts: 25.1 us -> 6.01 us
  matrix products: 24 us -> 6.56 us
  starting transfers between devices: 3.55 us -> 19.6 us
  between operations: 13.5 us -> 0.14 us
  blocking collectives: 11.3 us -> 24.4 us
  other arithmetic: 9.08 us -> 1.93 us
    all_gather x2 -> x0, waiting for transfers between devices: 64 us -> none  [the longest x1 64 us: on_device(): full_qkv = lax.all_gather(w_qkv, 'expert', axis=0, tiled=True)]
    ppermute x0 -> x30, waiting for transfers between devices: none -> 43.7 us  [send(): return lax.ppermute(block, AXES, pairs_of(groups, experts, move))]
    pallas_call x0 -> x2, Pallas kernels: none -> 20.9 us  [the longest x1 14.1 us: attention(): pl.pallas_call(functools.partial(attention_kernel, count, images, length)...]
    ppermute x0 -> x30, starting transfers between devices: none -> 19.6 us  [send(): return lax.ppermute(block, AXES, pairs_of(groups, experts, move))]
    dot_general x7 -> x1, matrix products: 17.9 us -> 0.47 us  [on_device(): jnp.einsum('bns,bnd->bsd', combine, slot_outputs, preferred_element_type=...]
    all_to_all x0 -> x1, blocking collectives: none -> 10.5 us  [on_device(): lax.all_to_all(answered, 'expert', split_axis=1, concat_axis=1, tiled=True)]
    reshape x1 -> x0, local copies, waits for them, and re-layouts: 8.6 us -> none  [on_device(): qkv.astype(jnp.bfloat16)]
    all_to_all x1 -> x0, waiting for transfers between devices: 7.85 us -> none  [on_device(): lax.all_to_all(answered, 'expert', split_axis=1, concat_axis=1, tiled=True)]
  transfers between devices with their start and end apart: 3 -> 30, of which waited for: 2 -> 9; matrix products, arithmetic and copies ran while one was open for 28% -> 1% of each run, Pallas kernels for 0% -> 11%
where the time goes in v1:
time: 124 us; the launch traced here: 123 us
  waiting for transfers between devices  43.7 us (35%)
  blocking collectives  24.4 us (20%)
  Pallas kernels  20.9 us (17%)
  starting transfers between devices  19.6 us (16%)
  matrix products  6.56 us (5%)
  local copies, waits for them, and re-layouts  6.01 us (5%)
  other arithmetic  1.93 us (2%)
    ppermute x30, waiting for transfers between devices, send(): return lax.ppermute(block, AXES, pairs_of(groups, experts, move))  43.7 us
    ppermute x30, starting transfers between devices, send(): return lax.ppermute(block, AXES, pairs_of(groups, experts, move))  19.6 us
    pallas_call x1, Pallas kernels, attention(): pl.pallas_call(functools.partial(attention_kernel, count, images, length)...  14.1 us
    all_to_all x1, blocking collectives, on_device(): lax.all_to_all(slot_inputs, 'expert', split_axis=1, concat_axis=1, tiled=...  13.9 us
    all_to_all x1, blocking collectives, on_device(): lax.all_to_all(answered, 'expert', split_axis=1, concat_axis=1, tiled=True)  10.5 us
    pallas_call x1, Pallas kernels, router(): pl.pallas_call(functools.partial(router_kernel, count, images, length), o...  6.8 us
    dot_general x1, matrix products, on_device(): jnp.einsum('bneph,ehd->bnepd', hidden, w_expert_out, preferred_element_ty...  6.09 us
    unnamed x16, local copies, waits for them, and re-layouts  5.73 us
  transfers between devices with their start and end apart: 30, of which 9 were waited for; matrix products, arithmetic and copies ran while one was open for 1% of the time, Pallas kernels for 11%

profile of v1, /device:TPU:0, one launch (start us, length us, event | category | flops | bytes accessed | tf_op | source)
XLA Modules:
  0.0 123.3 jit_solution(2546394737583343229)
XLA Ops:
  0.0 4.0 %collective-permute-start.3 = (bf16[64,3072]{1,0:T(8,128)(2,1)}, bf16[64,3072]{1,0:T(8,128)(2,1)S(1)}, u32[]{:S(2)}, u32[]{:S(2)}) collective-permute-start(bf16[64,3072]{1,0:T(8,128)(2,1)} %refs_2_.1), channel_id=1, source_target_pairs={{0,8},{1,9},{2,10},{3,11},{4,12},{5,13},{6,14},{7,15},{8,0},{9,1},... | collective-permute-start | bytes 1179656 | tf_op jit(solution)/shard_map/ppermute | solution.py:38
  4.1 1.9 %collective-permute-start.16 = (bf16[64,1024]{1,0:T(8,128)(2,1)}, bf16[64,1024]{1,0:T(8,128)(2,1)S(1)}, u32[]{:S(2)}, u32[]{:S(2)}) collective-permute-start(bf16[64,1024]{1,0:T(8,128)(2,1)} %refs_4_.1), channel_id=1, source_target_pairs={{0,4},{1,5},{2,6},{3,7},{4,0},{5,1},{6,2},{7,3},{8,12},{9,13},{10,... | collective-permute-start | bytes 393224 | tf_op jit(solution)/shard_map/ppermute | solution.py:38
  6.0 1.5 %collective-permute-start.15 = (bf16[64,1024]{1,0:T(8,128)(2,1)}, bf16[64,1024]{1,0:T(8,128)(2,1)S(1)}, u32[]{:S(2)}, u32[]{:S(2)}) collective-permute-start(bf16[64,1024]{1,0:T(8,128)(2,1)} %refs_4_.1), channel_id=1, source_target_pairs={{0,2},{1,3},{2,0},{3,1},{4,6},{5,7},{6,4},{7,5},{8,10},{9,11},{10,... | collective-permute-start | bytes 393224 | tf_op jit(solution)/shard_map/ppermute | solution.py:38
  7.5 19.9 %collective-permute-done.18.refs_8_ = bf16[64,1024]{1,0:T(8,128)(2,1)S(1)} collective-permute-done((bf16[64,1024]{1,0:T(8,128)(2,1)}, bf16[64,1024]{1,0:T(8,128)(2,1)S(1)}, u32[]{:S(2)}, u32[]{:S(2)}) %collective-permute-start.18) | collective-permute-done | bytes 131104 | tf_op jit(solution)/shard_map/ppermute | solution.py:38
  27.4 1.6 %collective-permute-start.20 = (bf16[64,1024]{1,0:T(8,128)(2,1)S(1)}, bf16[64,1024]{1,0:T(8,128)(2,1)S(1)}, u32[]{:S(2)}, u32[]{:S(2)}) collective-permute-start(bf16[64,1024]{1,0:T(8,128)(2,1)S(1)} %collective-permute-done.18.refs_8_), channel_id=1, source_target_pairs={{0,2},{1,3},{2,0},{3,1},{4,6},{5,7},{6,4},{7,5},{8,10},{9,11},{10,... | collective-permute-start | bytes 393224 | tf_op jit(solution)/shard_map/ppermute | solution.py:38
  29.5 4.0 %collective-permute-done.20.refs_10_ = bf16[64,1024]{1,0:T(8,128)(2,1)S(1)} collective-permute-done((bf16[64,1024]{1,0:T(8,128)(2,1)S(1)}, bf16[64,1024]{1,0:T(8,128)(2,1)S(1)}, u32[]{:S(2)}, u32[]{:S(2)}) %collective-permute-start.20) | collective-permute-done | bytes 131104 | tf_op jit(solution)/shard_map/ppermute | solution.py:38
  33.5 1.1 collective-permute-start.1
  34.6 1.5 %collective-permute-start = (bf16[64,3072]{1,0:T(8,128)(2,1)}, bf16[64,3072]{1,0:T(8,128)(2,1)S(1)}, u32[]{:S(2)}, u32[]{:S(2)}) collective-permute-start(bf16[64,3072]{1,0:T(8,128)(2,1)} %refs_2_.1), channel_id=1, source_target_pairs={{0,2},{1,3},{2,0},{3,1},{4,6},{5,7},{6,4},{7,5},{8,10},{9,11},{10,... | collective-permute-start | bytes 1179656 | tf_op jit(solution)/shard_map/ppermute | solution.py:38
  36.9 1.2 collective-permute-done.24.refs_14_
  38.1 1.0 collective-permute-start.21
  39.1 4.5 %collective-permute-done.21.refs_11_ = bf16[64,1024]{1,0:T(8,128)(2,1)S(1)} collective-permute-done((bf16[64,1024]{1,0:T(8,128)(2,1)S(1)}, bf16[64,1024]{1,0:T(8,128)(2,1)S(1)}, u32[]{:S(2)}, u32[]{:S(2)}) %collective-permute-start.21) | collective-permute-done | bytes 131104 | tf_op jit(solution)/shard_map/ppermute | solution.py:38
  43.6 1.0 collective-permute-start.4
  44.6 1.6 %collective-permute-start.2 = (bf16[64,3072]{1,0:T(8,128)(2,1)S(1)}, bf16[64,3072]{1,0:T(8,128)(2,1)}, u32[]{:S(2)}, u32[]{:S(2)}) collective-permute-start(bf16[64,3072]{1,0:T(8,128)(2,1)S(1)} %collective-permute-done.1.refs_4_), channel_id=1, source_target_pairs={{0,2},{1,3},{2,0},{3,1},{4,6},{5,7},{6,4},{7,5},{8,10},{9,11},{10,... | collective-permute-start | bytes 1179656 | tf_op jit(solution)/shard_map/ppermute | solution.py:38
  47.4 7.9 %collective-permute-done.5.refs_8_ = bf16[64,3072]{1,0:T(8,128)(2,1)S(1)} collective-permute-done((bf16[64,3072]{1,0:T(8,128)(2,1)S(1)}, bf16[64,3072]{1,0:T(8,128)(2,1)S(1)}, u32[]{:S(2)}, u32[]{:S(2)}) %collective-permute-start.5) | collective-permute-done | bytes 393248 | tf_op jit(solution)/shard_map/ppermute | solution.py:38
  56.1 4.6 %collective-permute-done.2.refs_5_ = bf16[64,3072]{1,0:T(8,128)(2,1)} collective-permute-done((bf16[64,3072]{1,0:T(8,128)(2,1)S(1)}, bf16[64,3072]{1,0:T(8,128)(2,1)}, u32[]{:S(2)}, u32[]{:S(2)}) %collective-permute-start.2) | collective-permute-done | bytes 393248 | tf_op jit(solution)/shard_map/ppermute | solution.py:38
  65.5 1.2 copy-done
  66.8 1.0 copy-done.3
  67.8 1.0 copy-done.5
  69.8 14.1 %attention.1.refs_1_ = bf16[512,1024]{1,0:T(8,128)(2,1)S(1)} custom-call(s32[16]{0:T(128)S(1)} %fusion.51.refs_0_, bf16[512,1024]{1,0:T(8,128)(2,1)S(1)} %bitcast.110, bf16[64,3072]{1,0:T(8,128)(2,1)S(1)} %copy-done.3, bf16[64,3072]{1,0:T(8,128)(2,1)S(1)} %collective-permute-done.refs_3_, bf16[64,3072]{1,0:T(8,128)(2,1)S(1)} %collective-permute-done.1.refs_4_, ...), custom_call_target="tpu_custom_call" | custom-call | flops 4294967296 | bytes 8388608 | tf_op jit(solution)/shard_map/attention/pallas_call | solution.py:152
  83.9 6.8 %router.1 = (f32[512,1024]{1,0:T(8,128)S(1)}, bf16[2,32,256]{2,1,0:T(8,128)(2,1)S(1)}, bf16[2,32,1024]{2,1,0:T(8,128)(2,1)S(1)}) custom-call(s32[16]{0:T(128)S(1)} %fusion.51.refs_0_, bf16[512,1024]{1,0:T(8,128)(2,1)S(1)} %attention.1.refs_1_, bf16[512,1024]{1,0:T(8,128)(2,1)S(1)} %bitcast.111, bf16[32,1024]{1,0:T(8,128)(2,1)S(1)} %bitcast.112, ...), custom_call_target="tpu_custom_call" | custom-call | flops 1140850688 | bytes 6291456 | tf_op jit(solution)/shard_map/router/pallas_call | solution.py:200
  90.9 13.9 %all_to_all.10 = bf16[2,32,1024]{2,0,1:T(2,128)(2,1)S(1)} all-to-all(bf16[2,32,1024]{2,0,1:T(2,128)(2,1)S(1)} %copy.16), channel_id=1, replica_groups=mesh['group'=2,'expert'=16] {'expert'}, dimensions={1} | all-to-all | bytes 262144 | tf_op jit(solution)/shard_map/all_to_all | solution.py:238
  104.8 6.1 %fusion.7 = bf16[2,16,1,2,1024]{4,1,3,0,2:T(8,128)(2,1)S(1)} fusion(bf16[1,2048,1024]{2,1,0:T(8,128)(2,1)} %param.13, bf16[1,1024,2048]{2,1,0:T(8,128)(2,1)} %param.12, bf16[2,16,2,1024]{3,0,2,1:T(2,128)(2,1)S(1)} %bitcast.114), kind=kOutput, calls=%fused_computation.6 | convolution fusion | flops 545456128 | bytes 8650752 | tf_op jit(solution)/shard_map/bneph,ehd->bnepd/dot_general | solution.py:242
  111.0 10.5 %all_to_all.11 = bf16[2,32,1024]{2,0,1:T(2,128)(2,1)S(1)} all-to-all(bf16[2,32,1024]{2,0,1:T(2,128)(2,1)S(1)} %bitcast.113), channel_id=1, replica_groups=mesh['group'=2,'expert'=16] {'expert'}, dimensions={1} | all-to-all | bytes 262144 | tf_op jit(solution)/shard_map/all_to_all | solution.py:244
  122.0 1.3 %add_convert_fusion = bf16[2,256,1024]{2,1,0:T(8,128)(2,1)} fusion(f32[2,256,1024]{2,1,0:T(8,128)S(1)} %bitcast.109, f32[2,256,1024]{2,1,0:T(8,128)S(1)} %fusion.45), kind=kLoop, calls=%fused_computation.4 | loop fusion | flops 1048576 | bytes 5242880 | tf_op jit(solution)/shard_map/convert_element_type | solution.py:246
  (62 shorter events, 9.9 us)
Async XLA Ops:
  0.0 36.1 %collective-permute-start.3 = (bf16[64,3072]{1,0:T(8,128)(2,1)}, bf16[64,3072]{1,0:T(8,128)(2,1)S(1)}, u32[]{:S(2)}, u32[]{:S(2)}) collective-permute-start(bf16[64,3072]{1,0:T(8,128)(2,1)} %refs_2_.1), channel_id=1, source_target_pairs={{0,8},{1,9},{2,10},{3,11},{4,12},{5,13},{6,14},{7,15},{8,0},{9,1},... | collective-permute-start | bytes 1179656 | tf_op jit(solution)/shard_map/ppermute | solution.py:38
  4.0 23.4 %collective-permute-start.18 = (bf16[64,1024]{1,0:T(8,128)(2,1)}, bf16[64,1024]{1,0:T(8,128)(2,1)S(1)}, u32[]{:S(2)}, u32[]{:S(2)}) collective-permute-start(bf16[64,1024]{1,0:T(8,128)(2,1)} %refs_4_.1), channel_id=1, source_target_pairs={{0,8},{1,9},{2,10},{3,11},{4,12},{5,13},{6,14},{7,15},{8,0},{9,1},... | collective-permute-start | bytes 393224 | tf_op jit(solution)/shard_map/ppermute | solution.py:38
  4.1 24.9 %collective-permute-start.16 = (bf16[64,1024]{1,0:T(8,128)(2,1)}, bf16[64,1024]{1,0:T(8,128)(2,1)S(1)}, u32[]{:S(2)}, u32[]{:S(2)}) collective-permute-start(bf16[64,1024]{1,0:T(8,128)(2,1)} %refs_4_.1), channel_id=1, source_target_pairs={{0,4},{1,5},{2,6},{3,7},{4,0},{5,1},{6,2},{7,3},{8,12},{9,13},{10,... | collective-permute-start | bytes 393224 | tf_op jit(solution)/shard_map/ppermute | solution.py:38
  6.0 23.0 %collective-permute-start.15 = (bf16[64,1024]{1,0:T(8,128)(2,1)}, bf16[64,1024]{1,0:T(8,128)(2,1)S(1)}, u32[]{:S(2)}, u32[]{:S(2)}) collective-permute-start(bf16[64,1024]{1,0:T(8,128)(2,1)} %refs_4_.1), channel_id=1, source_target_pairs={{0,2},{1,3},{2,0},{3,1},{4,6},{5,7},{6,4},{7,5},{8,10},{9,11},{10,... | collective-permute-start | bytes 393224 | tf_op jit(solution)/shard_map/ppermute | solution.py:38
  7.5 22.0 %collective-permute-start.22 = (bf16[64,1024]{1,0:T(8,128)(2,1)}, bf16[64,1024]{1,0:T(8,128)(2,1)S(1)}, u32[]{:S(2)}, u32[]{:S(2)}) collective-permute-start(bf16[64,1024]{1,0:T(8,128)(2,1)} %refs_4_.1), channel_id=1, source_target_pairs={{0,1},{1,0},{2,3},{3,2},{4,5},{5,4},{6,7},{7,6},{8,9},{9,8},{10,11... | collective-permute-start | bytes 393224 | tf_op jit(solution)/shard_map/ppermute | solution.py:38
  27.4 6.1 %collective-permute-start.20 = (bf16[64,1024]{1,0:T(8,128)(2,1)S(1)}, bf16[64,1024]{1,0:T(8,128)(2,1)S(1)}, u32[]{:S(2)}, u32[]{:S(2)}) collective-permute-start(bf16[64,1024]{1,0:T(8,128)(2,1)S(1)} %collective-permute-done.18.refs_8_), channel_id=1, source_target_pairs={{0,2},{1,3},{2,0},{3,1},{4,6},{5,7},{6,4},{7,5},{8,10},{9,11},{10,... | collective-permute-start | bytes 393224 | tf_op jit(solution)/shard_map/ppermute | solution.py:38
  29.0 5.6 %collective-permute-start.19 = (bf16[64,1024]{1,0:T(8,128)(2,1)S(1)}, bf16[64,1024]{1,0:T(8,128)(2,1)S(1)}, u32[]{:S(2)}, u32[]{:S(2)}) collective-permute-start(bf16[64,1024]{1,0:T(8,128)(2,1)S(1)} %collective-permute-done.18.refs_8_), channel_id=1, source_target_pairs={{0,16},{1,17},{2,18},{3,19},{4,20},{5,21},{6,22},{7,23},{8,24},{9,... | collective-permute-start | bytes 393224 | tf_op jit(solution)/shard_map/ppermute | solution.py:38
  29.0 7.1 %collective-permute-start.17 = (bf16[64,1024]{1,0:T(8,128)(2,1)S(1)}, bf16[64,1024]{1,0:T(8,128)(2,1)S(1)}, u32[]{:S(2)}, u32[]{:S(2)}) collective-permute-start(bf16[64,1024]{1,0:T(8,128)(2,1)S(1)} %collective-permute-done.16.refs_6_), channel_id=1, source_target_pairs={{0,2},{1,3},{2,0},{3,1},{4,6},{5,7},{6,4},{7,5},{8,10},{9,11},{10,... | collective-permute-start | bytes 393224 | tf_op jit(solution)/shard_map/ppermute | solution.py:38
  29.5 7.2 %collective-permute-start.26 = (bf16[64,1024]{1,0:T(8,128)(2,1)S(1)}, bf16[64,1024]{1,0:T(8,128)(2,1)S(1)}, u32[]{:S(2)}, u32[]{:S(2)}) collective-permute-start(bf16[64,1024]{1,0:T(8,128)(2,1)S(1)} %collective-permute-done.18.refs_8_), channel_id=1, source_target_pairs={{0,1},{1,0},{2,3},{3,2},{4,5},{5,4},{6,7},{7,6},{8,9},{9,8},{10,11... | collective-permute-start | bytes 393224 | tf_op jit(solution)/shard_map/ppermute | solution.py:38
  33.5 11.1 %collective-permute-start.1 = (bf16[64,3072]{1,0:T(8,128)(2,1)}, bf16[64,3072]{1,0:T(8,128)(2,1)S(1)}, u32[]{:S(2)}, u32[]{:S(2)}) collective-permute-start(bf16[64,3072]{1,0:T(8,128)(2,1)} %refs_2_.1), channel_id=1, source_target_pairs={{0,4},{1,5},{2,6},{3,7},{4,0},{5,1},{6,2},{7,3},{8,12},{9,13},{10,... | collective-permute-start | bytes 1179656 | tf_op jit(solution)/shard_map/ppermute | solution.py:38
  34.6 12.3 %collective-permute-start = (bf16[64,3072]{1,0:T(8,128)(2,1)}, bf16[64,3072]{1,0:T(8,128)(2,1)S(1)}, u32[]{:S(2)}, u32[]{:S(2)}) collective-permute-start(bf16[64,3072]{1,0:T(8,128)(2,1)} %refs_2_.1), channel_id=1, source_target_pairs={{0,2},{1,3},{2,0},{3,1},{4,6},{5,7},{6,4},{7,5},{8,10},{9,11},{10,... | collective-permute-start | bytes 1179656 | tf_op jit(solution)/shard_map/ppermute | solution.py:38
  36.1 10.7 %collective-permute-start.7 = (bf16[64,3072]{1,0:T(8,128)(2,1)}, bf16[64,3072]{1,0:T(8,128)(2,1)S(1)}, u32[]{:S(2)}, u32[]{:S(2)}) collective-permute-start(bf16[64,3072]{1,0:T(8,128)(2,1)} %refs_2_.1), channel_id=1, source_target_pairs={{0,1},{1,0},{2,3},{3,2},{4,5},{5,4},{6,7},{7,6},{8,9},{9,8},{10,11... | collective-permute-start | bytes 1179656 | tf_op jit(solution)/shard_map/ppermute | solution.py:38
  36.1 19.2 %collective-permute-start.5 = (bf16[64,3072]{1,0:T(8,128)(2,1)S(1)}, bf16[64,3072]{1,0:T(8,128)(2,1)S(1)}, u32[]{:S(2)}, u32[]{:S(2)}) collective-permute-start(bf16[64,3072]{1,0:T(8,128)(2,1)S(1)} %collective-permute-done.3.refs_6_), channel_id=1, source_target_pairs={{0,2},{1,3},{2,0},{3,1},{4,6},{5,7},{6,4},{7,5},{8,10},{9,11},{10,... | collective-permute-start | bytes 1179656 | tf_op jit(solution)/shard_map/ppermute | solution.py:38
  43.6 12.5 %collective-permute-start.4 = (bf16[64,3072]{1,0:T(8,128)(2,1)S(1)}, bf16[64,3072]{1,0:T(8,128)(2,1)}, u32[]{:S(2)}, u32[]{:S(2)}) collective-permute-start(bf16[64,3072]{1,0:T(8,128)(2,1)S(1)} %collective-permute-done.3.refs_6_), channel_id=1, source_target_pairs={{0,16},{1,17},{2,18},{3,19},{4,20},{5,21},{6,22},{7,23},{8,24},{9,... | collective-permute-start | bytes 1179656 | tf_op jit(solution)/shard_map/ppermute | solution.py:38
  44.6 16.1 %collective-permute-start.2 = (bf16[64,3072]{1,0:T(8,128)(2,1)S(1)}, bf16[64,3072]{1,0:T(8,128)(2,1)}, u32[]{:S(2)}, u32[]{:S(2)}) collective-permute-start(bf16[64,3072]{1,0:T(8,128)(2,1)S(1)} %collective-permute-done.1.refs_4_), channel_id=1, source_target_pairs={{0,2},{1,3},{2,0},{3,1},{4,6},{5,7},{6,4},{7,5},{8,10},{9,11},{10,... | collective-permute-start | bytes 1179656 | tf_op jit(solution)/shard_map/ppermute | solution.py:38
  46.9 13.9 %collective-permute-start.11 = (bf16[64,3072]{1,0:T(8,128)(2,1)S(1)}, bf16[64,3072]{1,0:T(8,128)(2,1)S(1)}, u32[]{:S(2)}, u32[]{:S(2)}) collective-permute-start(bf16[64,3072]{1,0:T(8,128)(2,1)S(1)} %collective-permute-done.3.refs_6_), channel_id=1, source_target_pairs={{0,1},{1,0},{2,3},{3,2},{4,5},{5,4},{6,7},{7,6},{8,9},{9,8},{10,11... | collective-permute-start | bytes 1179656 | tf_op jit(solution)/shard_map/ppermute | solution.py:38
  46.9 15.2 %collective-permute-start.9 = (bf16[64,3072]{1,0:T(8,128)(2,1)S(1)}, bf16[64,3072]{1,0:T(8,128)(2,1)S(1)}, u32[]{:S(2)}, u32[]{:S(2)}) collective-permute-start(bf16[64,3072]{1,0:T(8,128)(2,1)S(1)} %collective-permute-done.1.refs_4_), channel_id=1, source_target_pairs={{0,1},{1,0},{2,3},{3,2},{4,5},{5,4},{6,7},{7,6},{8,9},{9,8},{10,11... | collective-permute-start | bytes 1179656 | tf_op jit(solution)/shard_map/ppermute | solution.py:38
  55.3 7.9 %collective-permute-start.6 = (bf16[64,3072]{1,0:T(8,128)(2,1)S(1)}, bf16[64,3072]{1,0:T(8,128)(2,1)}, u32[]{:S(2)}, u32[]{:S(2)}) collective-permute-start(bf16[64,3072]{1,0:T(8,128)(2,1)S(1)} %collective-permute-done.5.refs_8_), channel_id=1, source_target_pairs={{0,16},{1,17},{2,18},{3,19},{4,20},{5,21},{6,22},{7,23},{8,24},{9,... | collective-permute-start | bytes 1179656 | tf_op jit(solution)/shard_map/ppermute | solution.py:38
  56.1 7.9 %collective-permute-start.8 = (bf16[64,3072]{1,0:T(8,128)(2,1)S(1)}, bf16[64,3072]{1,0:T(8,128)(2,1)}, u32[]{:S(2)}, u32[]{:S(2)}) collective-permute-start(bf16[64,3072]{1,0:T(8,128)(2,1)S(1)} %collective-permute-done.refs_3_), channel_id=1, source_target_pairs={{0,1},{1,0},{2,3},{3,2},{4,5},{5,4},{6,7},{7,6},{8,9},{9,8},{10,11... | collective-permute-start | bytes 1179656 | tf_op jit(solution)/shard_map/ppermute | solution.py:38
  64.0 19.9 %collective-permute-start.23 = (bf16[64,1024]{1,0:T(8,128)(2,1)S(1)}, bf16[64,1024]{1,0:T(8,128)(2,1)S(1)}, u32[]{:S(2)}, u32[]{:S(2)}) collective-permute-start(bf16[64,1024]{1,0:T(8,128)(2,1)S(1)} %collective-permute-done.15.refs_5_), channel_id=1, source_target_pairs={{0,1},{1,0},{2,3},{3,2},{4,5},{5,4},{6,7},{7,6},{8,9},{9,8},{10,11... | collective-permute-start | bytes 393224 | tf_op jit(solution)/shard_map/ppermute | solution.py:38
  64.3 19.5 %collective-permute-start.28 = (bf16[64,1024]{1,0:T(8,128)(2,1)S(1)}, bf16[64,1024]{1,0:T(8,128)(2,1)S(1)}, u32[]{:S(2)}, u32[]{:S(2)}) collective-permute-start(bf16[64,1024]{1,0:T(8,128)(2,1)S(1)} %collective-permute-done.20.refs_10_), channel_id=1, source_target_pairs={{0,1},{1,0},{2,3},{3,2},{4,5},{5,4},{6,7},{7,6},{8,9},{9,8},{10,11... | collective-permute-start | bytes 393224 | tf_op jit(solution)/shard_map/ppermute | solution.py:38
  64.5 19.4 %collective-permute-start.27 = (bf16[64,1024]{1,0:T(8,128)(2,1)S(1)}, bf16[64,1024]{1,0:T(8,128)(2,1)S(1)}, u32[]{:S(2)}, u32[]{:S(2)}) collective-permute-start(bf16[64,1024]{1,0:T(8,128)(2,1)S(1)} %collective-permute-done.19.refs_9_), channel_id=1, source_target_pairs={{0,1},{1,0},{2,3},{3,2},{4,5},{5,4},{6,7},{7,6},{8,9},{9,8},{10,11... | collective-permute-start | bytes 393224 | tf_op jit(solution)/shard_map/ppermute | solution.py:38
  64.9 19.0 %collective-permute-start.25 = (bf16[64,1024]{1,0:T(8,128)(2,1)S(1)}, bf16[64,1024]{1,0:T(8,128)(2,1)S(1)}, u32[]{:S(2)}, u32[]{:S(2)}) collective-permute-start(bf16[64,1024]{1,0:T(8,128)(2,1)S(1)} %collective-permute-done.17.refs_7_), channel_id=1, source_target_pairs={{0,1},{1,0},{2,3},{3,2},{4,5},{5,4},{6,7},{7,6},{8,9},{9,8},{10,11... | collective-permute-start | bytes 393224 | tf_op jit(solution)/shard_map/ppermute | solution.py:38
  65.4 18.5 %collective-permute-start.29 = (bf16[64,1024]{1,0:T(8,128)(2,1)S(1)}, bf16[64,1024]{1,0:T(8,128)(2,1)S(1)}, u32[]{:S(2)}, u32[]{:S(2)}) collective-permute-start(bf16[64,1024]{1,0:T(8,128)(2,1)S(1)} %collective-permute-done.21.refs_11_), channel_id=1, source_target_pairs={{0,1},{1,0},{2,3},{3,2},{4,5},{5,4},{6,7},{7,6},{8,9},{9,8},{10,11... | collective-permute-start | bytes 393224 | tf_op jit(solution)/shard_map/ppermute | solution.py:38
  (14 other events, 51.8 us)

commit v2 on v0

v2 whole, which is shorter than its diff:
```python
import functools

import jax
import jax.numpy as jnp
from jax import lax
from jax.experimental import pallas as pl
from jax.experimental.pallas import tpu as pltpu
from jax.sharding import PartitionSpec as P

HEADS = 16
AXES = ("group", "expert")
F32 = jnp.float32
BF16 = jnp.bfloat16


def layer_norm(values):
    center = values - jnp.mean(values, axis=-1, keepdims=True)
    spread = jnp.mean(center * center, axis=-1, keepdims=True)
    return center * lax.rsqrt(spread + 1e-06)


def is_grid(groups, experts):
    return groups == 2 and experts == 16


def after(value, *earlier):
    return lax.optimization_barrier((value,) + earlier)[0]


def norm_kernel(tokens_ref, out_ref):
    out_ref[...] = layer_norm(tokens_ref[...].astype(F32)).astype(BF16)


def norm(tokens):
    rows, width = tokens.shape
    return pl.pallas_call(
        norm_kernel,
        out_shape=jax.ShapeDtypeStruct((rows, width), BF16),
        in_specs=[pl.BlockSpec(memory_space=pltpu.VMEM)],
        out_specs=pl.BlockSpec(memory_space=pltpu.VMEM),
        compiler_params=pltpu.CompilerParams(vmem_limit_bytes=16 << 20),
        cost_estimate=pl.CostEstimate(
            flops=8 * rows * width, bytes_accessed=4 * rows * width, transcendentals=rows
        ),
        name="norm",
    )(tokens)


def split_kernel(core_ref, qkv_ref, out_ref, keep_ref, give_ref):
    span = out_ref.shape[1] // 4
    for side, target in enumerate((keep_ref, give_ref)):
        core = jnp.bitwise_xor(core_ref[0], side)
        for chunk in range(2):
            for which in range(3):
                start = (which * 4 + core * 2 + chunk) * span
                at = (chunk * 3 + which) * span
                target[:, at : at + span] = qkv_ref[:, pl.ds(pl.multiple_of(start, span), span)]
        start = pl.multiple_of(core * 2 * span, 2 * span)
        target[:, 6 * span : 8 * span] = out_ref[:, pl.ds(start, 2 * span)]


def split(core, w_qkv, w_attn_out):
    rows, width = w_attn_out.shape
    vmem = pl.BlockSpec(memory_space=pltpu.VMEM)
    return pl.pallas_call(
        split_kernel,
        out_shape=[jax.ShapeDtypeStruct((rows, 2 * width), BF16)] * 2,
        in_specs=[pl.BlockSpec(memory_space=pltpu.SMEM), vmem, vmem],
        out_specs=[vmem] * 2,
        compiler_params=pltpu.CompilerParams(vmem_limit_bytes=8 << 20),
        cost_estimate=pl.CostEstimate(
            flops=0, bytes_accessed=16 * rows * width, transcendentals=0
        ),
        name="split",
    )(core.reshape(1), w_qkv, w_attn_out)


def load_blocks(place_ref, blocks, whole, sem, columns=slice(None)):
    core = place_ref[len(blocks)]
    half = blocks[0].shape[0] // 2
    copies = []
    for at, block in enumerate(blocks):
        for part in range(2):
            start = place_ref[at] * (2 * half) + jnp.bitwise_xor(core, part) * half
            copy = pltpu.make_async_copy(
                block.at[pl.ds(part * half, half)],
                whole.at[pl.ds(pl.multiple_of(start, half), half), columns],
                sem.at[2 * at + part],
            )
            copy.start()
            copies.append(copy)
    return copies


def attend(query, keys, values, head, out_ref, rows, columns):
    lane = lax.broadcasted_iota(jnp.int32, query.shape, 1)
    first = lane < head
    result = []
    for mask in (first, ~first):
        scores = lax.dot_general(
            jnp.where(mask, query, jnp.zeros_like(query)),
            keys,
            (((1,), (1,)), ((), ())),
            preferred_element_type=F32,
        )
        top = jnp.max(scores, axis=-1, keepdims=True)
        weights = jnp.exp(scores - top).astype(BF16)
        mixed = jnp.dot(
            weights, jnp.where(mask, values, jnp.ones_like(values)), preferred_element_type=F32
        )
        result.append(mixed / pltpu.roll(mixed, head, 1))
    out_ref[rows, columns] = jnp.where(first, result[0], result[1]).astype(BF16)


def attention_kernel(count, length, head, *refs):
    place_ref, mine_ref, other_ref = refs[:3]
    blocks = refs[3 : 3 + count]
    outs = refs[3 + count : 5 + count]
    weight, sem = refs[5 + count :]
    for copy in load_blocks(place_ref, blocks, weight, sem):
        copy.wait()
    span = weight.shape[1] // 3
    pair = 2 * head
    for normed, out_ref in zip((mine_ref, other_ref), outs):

        def project(at):
            return jnp.dot(
                normed[...], weight[:, at * span : (at + 1) * span], preferred_element_type=F32
            )

        query = (project(0) * head**-0.5).astype(BF16)
        keys = project(1).astype(BF16)
        values = project(2).astype(BF16)
        for start in range(0, normed.shape[0], length):
            rows = slice(start, start + length)
            for left in range(0, span, pair):
                columns = slice(left, left + pair)
                attend(
                    query[rows, columns],
                    keys[rows, columns],
                    values[rows, columns],
                    head,
                    out_ref,
                    rows,
                    columns,
                )


def attention(place, mine, other, blocks, length, head):
    rows, width = mine.shape
    count = len(blocks)
    span = blocks[0].shape[1] // 3
    vmem = pl.BlockSpec(memory_space=pltpu.VMEM)
    return pl.pallas_call(
        functools.partial(attention_kernel, count, length, head),
        out_shape=[jax.ShapeDtypeStruct((rows, span), BF16)] * 2,
        in_specs=[pl.BlockSpec(memory_space=pltpu.SMEM), vmem, vmem]
        + [pl.BlockSpec(memory_space=pltpu.HBM)] * count,
        out_specs=[vmem] * 2,
        scratch_shapes=[
            pltpu.VMEM((width, 3 * span), BF16),
            pltpu.SemaphoreType.DMA((2 * count,)),
        ],
        compiler_params=pltpu.CompilerParams(vmem_limit_bytes=24 << 20),
        cost_estimate=pl.CostEstimate(
            flops=4 * rows * span * (3 * width + 2 * length),
            bytes_accessed=6 * width * span + 4 * rows * width,
            transcendentals=2 * rows * (span // head) * length,
        ),
        name="attention",
    )(place, mine, other, *blocks)


def router_kernel(count, images, length, *refs):
    place_ref, tokens_ref, keys_ref = refs[:3]
    parts = refs[3:7]
    blocks = refs[7 : 7 + 2 * count]
    resid_ref, combine_ref, inputs_ref = refs[7 + 2 * count : 10 + 2 * count]
    weight, sem = refs[10 + 2 * count :]
    core = place_ref[count]
    span = blocks[0].shape[1]
    copies = []
    for side in range(2):
        left = pl.multiple_of(jnp.bitwise_xor(core, side) * span, span)
        copies += load_halves(
            place_ref, blocks[side * count : (side + 1) * count], weight, sem, left, span, core, side
        )
    for copy in copies:
        copy.wait()
    inner = parts[0].shape[1]
    for image in range(images):
        at = slice(image * length, (image + 1) * length)
        resid = tokens_ref[at].astype(F32)
        for which, part in enumerate(parts):
            side, chunk = which // 2, which % 2
            start = (2 * jnp.bitwise_xor(core, side) + chunk) * inner
            resid += jnp.dot(
                part[at],
                weight[pl.ds(pl.multiple_of(start, inner), inner)],
                preferred_element_type=F32,
            )
        resid_ref[at] = resid
        normed = layer_norm(resid).astype(BF16)
        logits = lax.dot_general(
            keys_ref[...], normed, (((1,), (1,)), ((), ())), preferred_element_type=F32
        )
        dispatch = jax.nn.softmax(logits, axis=1).astype(BF16)
        combine_ref[image] = jax.nn.softmax(logits, axis=0).astype(BF16)
        inputs_ref[image] = jnp.dot(dispatch, normed, preferred_element_type=F32).astype(BF16)


def load_halves(place_ref, blocks, whole, sem, left, span, core, side):
    half = blocks[0].shape[0] // 2
    copies = []
    for at, block in enumerate(blocks):
        for part in range(2):
            start = place_ref[at] * (2 * half) + jnp.bitwise_xor(core, part ^ side) * half
            copy = pltpu.make_async_copy(
                block.at[pl.ds(part * half, half)],
                whole.at[pl.ds(pl.multiple_of(start, half), half), pl.ds(left, span)],
                sem.at[(side * len(blocks) + at) * 2 + part],
            )
            copy.start()
            copies.append(copy)
    return copies


def router(place, tokens, slot_keys, parts, blocks, images, length):
    rows, width = tokens.shape
    slots = slot_keys.shape[1]
    count = place.shape[0] - 1
    vmem = pl.BlockSpec(memory_space=pltpu.VMEM)
    hbm = pl.BlockSpec(memory_space=pltpu.HBM)
    return pl.pallas_call(
        functools.partial(router_kernel, count, images, length),
        out_shape=[
            jax.ShapeDtypeStruct((rows, width), F32),
            jax.ShapeDtypeStruct((images, slots, length), BF16),
            jax.ShapeDtypeStruct((images, slots, width), BF16),
        ],
        in_specs=[pl.BlockSpec(memory_space=pltpu.SMEM)] + [vmem] * 6 + [hbm] * 2 * count,
        out_specs=[vmem] * 3,
        scratch_shapes=[
            pltpu.VMEM((width, width), BF16),
            pltpu.SemaphoreType.DMA((4 * count,)),
        ],
        compiler_params=pltpu.CompilerParams(vmem_limit_bytes=24 << 20),
        cost_estimate=pl.CostEstimate(
            flops=2 * rows * width * (width + 2 * slots),
            bytes_accessed=2 * width * width + 8 * rows * width,
            transcendentals=2 * rows * slots,
        ),
        name="router",
    )(place, tokens, slot_keys.T, *parts, *blocks)


def front_on_grid(groups, experts, tokens, w_qkv, w_attn_out, slot_keys):
    images, length, width = tokens.shape
    head = width // HEADS
    flat = tokens.reshape(images * length, width)
    expert = lax.axis_index("expert")
    group = lax.axis_index("group")
    core = expert % 2
    rows = w_qkv.shape[0]

    def send(value, move):
        pairs = []
        for at in range(groups):
            mask, flip = move(at)
            for index in range(experts):
                target = (at ^ flip) * experts + (index ^ mask)
                pairs.append((at * experts + index, target))
        return lax.ppermute(value, AXES, pairs)

    def in_chip(value):
        return send(value, lambda at: (1, 0))

    def over_y(value):
        return send(value, lambda at: (2, 0))

    def near_z(value):
        return send(value, lambda at: (4, 0))

    def far_z(value):
        return send(value, lambda at: (12, 0) if at else (8, 0))

    def over_x(value):
        return send(value, lambda at: (0, 1))

    span = width // 4
    keep, give = split(core, w_qkv, w_attn_out)
    block = jnp.concatenate([keep, in_chip(give)], axis=0)
    a = block[:, : 3 * span]
    b = block[:, 3 * span : 6 * span]
    c = block[:, 6 * span :]

    c_far = far_z(c)
    c_near = near_z(c)
    c_y = over_y(c)
    a_far = far_z(a)
    a_y = over_y(a)
    a_near = near_z(after(a, c_y))
    c_y_far = over_y(after(c_far, c_y))
    c_x = over_x(after(c_far, c_y))
    c_y_near = over_y(after(c_near, a_y))
    b_y = over_y(after(b, c_y_far, c_x))
    b_far = far_z(after(b, c_y_far, c_x))
    c_x_far = over_x(c_y_far)
    a_y_far = over_y(after(a_far, c_y_near))
    a_x = over_x(after(a_far, c_y_near))
    a_y_near = over_y(after(a_near, b_y))
    b_near = near_z(after(b, a_near, a_x))
    normed = norm(after(flat, a_x))
    normed_other = in_chip(normed)
    a_x_far = over_x(a_y_far)
    b_y_far = over_y(after(b_far, a_y_near))
    b_x = over_x(after(b_far, a_y_near))
    b_y_near = over_y(after(b_near, a_x_far))
    b_x_far = over_x(b_y_far)

    a_blocks = [a, a_y, a_near, a_y_near, a_far, a_x, a_y_far, a_x_far]
    b_blocks = [b, b_y, b_near, b_y_near, b_far, b_x, b_y_far, b_x_far]
    c_blocks = [c, c_y, c_near, c_y_near, c_far, c_x, c_y_far, c_x_far]
    masks = jnp.array([[0, 1, 2, 3, 4, 6, 5, 7, 0], [0, 1, 2, 3, 6, 4, 7, 5, 0]], jnp.int32)
    chips = jnp.bitwise_xor(jnp.where(group == 0, masks[0], masks[1]), expert // 2)
    last = lax.broadcasted_iota(jnp.int32, chips.shape, 0) == len(a_blocks)
    place = jnp.where(last, core, chips).astype(jnp.int32)

    mine_a, other_a = attention(
        place, after(normed, b_y_far, b_x), normed_other, a_blocks, length, head
    )
    mine_b, other_b = attention(place, normed, after(normed_other, mine_a), b_blocks, length, head)
    c_blocks += [in_chip(after(block, a_far)) for block in c_blocks[:5]] + [
        in_chip(after(block, a_x)) for block in c_blocks[5:]
    ]
    parts = [mine_a, mine_b, in_chip(other_a), in_chip(other_b)]
    return router(place, flat, slot_keys, parts, c_blocks, images, length)


def front(tokens, w_qkv, w_attn_out, slot_keys):
    images, length, width = tokens.shape
    head = width // HEADS
    rows = images * length
    normed = layer_norm(tokens.astype(F32)).astype(BF16).reshape(rows, width)
    full_qkv = lax.all_gather(w_qkv, "expert", axis=0, tiled=True)
    qkv = jnp.dot(normed, full_qkv, preferred_element_type=F32).astype(BF16)
    query, keys, values = [
        part[:, :, 0] for part in jnp.split(qkv.reshape(images, length, 3, HEADS, head), 3, axis=2)
    ]
    scores = jnp.einsum("bqhd,bkhd->bhqk", query, keys, preferred_element_type=F32) * head**-0.5
    weights = jax.nn.softmax(scores, axis=-1).astype(BF16)
    attended = jnp.einsum("bhqk,bkhd->bqhd", weights, values, preferred_element_type=F32)
    full_out = lax.all_gather(w_attn_out, "expert", axis=0, tiled=True)
    projected = jnp.dot(
        attended.astype(BF16).reshape(rows, width), full_out, preferred_element_type=F32
    )
    resid = tokens.astype(F32).reshape(rows, width) + projected
    normed_two = layer_norm(resid).astype(BF16).reshape(images, length, width)
    logits = jnp.einsum("bsd,dn->bns", normed_two, slot_keys, preferred_element_type=F32)
    dispatch = jax.nn.softmax(logits, axis=2).astype(BF16)
    combine = jax.nn.softmax(logits, axis=1).astype(BF16)
    slot_inputs = jnp.einsum("bns,bsd->bnd", dispatch, normed_two, preferred_element_type=F32)
    return resid, combine, slot_inputs.astype(BF16)


def on_device(mesh_shape, tokens, w_qkv, w_attn_out, slot_keys, w_expert_in, w_expert_out):
    images, length, width = tokens.shape
    if is_grid(*mesh_shape):
        resid, combine, slot_inputs = front_on_grid(
            *mesh_shape, tokens, w_qkv, w_attn_out, slot_keys
        )
    else:
        resid, combine, slot_inputs = front(tokens, w_qkv, w_attn_out, slot_keys)
    slots = slot_keys.shape[1]
    sources = mesh_shape[1]
    expert_here = w_expert_in.shape[0]
    pairs = slots // (sources * expert_here)
    block = lax.all_to_all(slot_inputs, "expert", split_axis=1, concat_axis=1, tiled=True)
    arranged = block.reshape(images, sources, expert_here, pairs, width)
    hidden = jnp.einsum("bnepd,edh->bneph", arranged, w_expert_in, preferred_element_type=F32)
    hidden = jax.nn.gelu(hidden, approximate=False).astype(BF16)
    answer = jnp.einsum("bneph,ehd->bnepd", hidden, w_expert_out, preferred_element_type=F32)
    answered = answer.astype(BF16).reshape(images, slots, width)
    slot_outputs = lax.all_to_all(answered, "expert", split_axis=1, concat_axis=1, tiled=True)
    mixed = jnp.einsum("bns,bnd->bsd", combine, slot_outputs, preferred_element_type=F32)
    return (resid.reshape(images, length, width) + mixed).astype(BF16)


def solution(mesh):
    placed = (
        P(AXES, None, None),
        P("expert", None),
        P("expert", None),
        P(),
        P("expert", None, None),
        P("expert", None, None),
    )
    return jax.shard_map(
        functools.partial(on_device, (mesh.shape["group"], mesh.shape["expert"])),
        mesh=mesh,
        in_specs=placed,
        out_specs=P(AXES, None, None),
        check_vma=False,
    )
```

time: 160 us -> 121 us (0.76)
  waiting for transfers between devices: 73.3 us -> 23.9 us
  starting transfers between devices: 3.55 us -> 34.4 us
  Pallas kernels: 0 us -> 22.9 us
  local copies, waits for them, and re-layouts: 25.1 us -> 7.42 us
  matrix products: 24 us -> 6.56 us
  between operations: 13.5 us -> 0.2 us
  blocking collectives: 11.3 us -> 23.5 us
  other arithmetic: 9.08 us -> 1.27 us
    all_gather x2 -> x0, waiting for transfers between devices: 64 us -> none  [the longest x1 64 us: on_device(): full_qkv = lax.all_gather(w_qkv, 'expert', axis=0, tiled=True)]
    ppermute x0 -> x33, starting transfers between devices: none -> 34.4 us  [send(): return lax.ppermute(value, AXES, pairs)]
    ppermute x0 -> x33, waiting for transfers between devices: none -> 23.9 us  [send(): return lax.ppermute(value, AXES, pairs)]
    pallas_call x0 -> x5, Pallas kernels: none -> 22.9 us  [the longest x2 17.2 us: attention(): pl.pallas_call(functools.partial(attention_kernel, count, length, head),...]
    dot_general x7 -> x1, matrix products: 17.9 us -> 0.47 us  [on_device(): jnp.einsum('bns,bnd->bsd', combine, slot_outputs, preferred_element_type=...]
    all_to_all x0 -> x1, blocking collectives: none -> 10.5 us  [on_device(): lax.all_to_all(answered, 'expert', split_axis=1, concat_axis=1, tiled=True)]
    reshape x1 -> x0, local copies, waits for them, and re-layouts: 8.6 us -> none  [on_device(): qkv.astype(jnp.bfloat16)]
    all_to_all x1 -> x0, waiting for transfers between devices: 7.85 us -> none  [on_device(): lax.all_to_all(answered, 'expert', split_axis=1, concat_axis=1, tiled=True)]
  transfers between devices with their start and end apart: 3 -> 33, of which waited for: 2 -> 15; matrix products, arithmetic and copies ran while one was open for 28% -> 0% of each run, Pallas kernels for 0% -> 15%
where the time goes in v2:
time: 121 us; the launch traced here: 120 us
  starting transfers between devices  34.4 us (28%)
  waiting for transfers between devices  23.9 us (20%)
  blocking collectives  23.5 us (19%)
  Pallas kernels  22.9 us (19%)
  local copies, waits for them, and re-layouts  7.42 us (6%)
  matrix products  6.56 us (5%)
  other arithmetic  1.27 us (1%)
    ppermute x33, starting transfers between devices, send(): return lax.ppermute(value, AXES, pairs)  34.4 us
    ppermute x33, waiting for transfers between devices, send(): return lax.ppermute(value, AXES, pairs)  23.9 us
    pallas_call x2, Pallas kernels, attention(): pl.pallas_call(functools.partial(attention_kernel, count, length, head),...  17.2 us
    all_to_all x1, blocking collectives, on_device(): lax.all_to_all(slot_inputs, 'expert', split_axis=1, concat_axis=1, tiled=...  13 us
    all_to_all x1, blocking collectives, on_device(): lax.all_to_all(answered, 'expert', split_axis=1, concat_axis=1, tiled=True)  10.5 us
    unnamed x27, local copies, waits for them, and re-layouts  7.09 us
    dot_general x1, matrix products, on_device(): jnp.einsum('bneph,ehd->bnepd', hidden, w_expert_out, preferred_element_ty...  6.09 us
    pallas_call x1, Pallas kernels, router(): pl.pallas_call(functools.partial(router_kernel, count, images, length), o...  4.97 us
  transfers between devices with their start and end apart: 33, of which 15 were waited for; matrix products, arithmetic and copies ran while one was open for 0% of the time, Pallas kernels for 15%

profile of v2, /device:TPU:0, one launch (start us, length us, event | category | flops | bytes accessed | tf_op | source)
XLA Modules:
  0.0 120.1 jit_solution(14473514609930164726)
XLA Ops:
  3.7 3.0 %collective-permute-start.3 = (bf16[128,768]{1,0:T(8,128)(2,1)S(1)}, bf16[128,768]{1,0:T(8,128)(2,1)S(1)}, u32[]{:S(2)}, u32[]{:S(2)}) collective-permute-start(bf16[128,768]{1,0:T(8,128)(2,1)S(1)} %get-tuple-element.41.refs_3_), channel_id=1, source_target_pairs={{0,2},{1,3},{2,0},{3,1},{4,6},{5,7},{6,4},{7,5},{8,10},{9,11},{10,... | collective-permute-start | bytes 589832 | tf_op jit(solution)/shard_map/ppermute | solution.py:273
  6.7 1.6 %collective-permute-start.2 = (bf16[128,512]{1,0:T(8,128)(2,1)S(1)}, bf16[128,512]{1,0:T(8,128)(2,1)S(1)}, u32[]{:S(2)}, u32[]{:S(2)}) collective-permute-start(bf16[128,512]{1,0:T(8,128)(2,1)S(1)} %slice.21.refs_7_), channel_id=1, source_target_pairs={{0,4},{1,5},{2,6},{3,7},{4,0},{5,1},{6,2},{7,3},{8,12},{9,13},{10,... | collective-permute-start | bytes 393224 | tf_op jit(solution)/shard_map/ppermute | solution.py:273
  8.3 2.6 %collective-permute-start.1 = (bf16[128,768]{1,0:T(8,128)(2,1)S(1)}, bf16[128,768]{1,0:T(8,128)(2,1)S(1)}, u32[]{:S(2)}, u32[]{:S(2)}) collective-permute-start(bf16[128,768]{1,0:T(8,128)(2,1)S(1)} %get-tuple-element.41.refs_3_), channel_id=1, source_target_pairs={{0,8},{1,9},{2,10},{3,11},{4,12},{5,13},{6,14},{7,15},{8,0},{9,1},... | collective-permute-start | bytes 589832 | tf_op jit(solution)/shard_map/ppermute | solution.py:273
  10.9 3.1 %collective-permute-done.2.refs_9_ = bf16[128,512]{1,0:T(8,128)(2,1)S(1)} collective-permute-done((bf16[128,512]{1,0:T(8,128)(2,1)S(1)}, bf16[128,512]{1,0:T(8,128)(2,1)S(1)}, u32[]{:S(2)}, u32[]{:S(2)}) %collective-permute-start.2) | collective-permute-done | bytes 131104 | tf_op jit(solution)/shard_map/ppermute | solution.py:273
  14.2 5.6 %collective-permute-done.1.refs_7_ = bf16[128,768]{1,0:T(8,128)(2,1)S(1)} collective-permute-done((bf16[128,768]{1,0:T(8,128)(2,1)S(1)}, bf16[128,768]{1,0:T(8,128)(2,1)S(1)}, u32[]{:S(2)}, u32[]{:S(2)}) %collective-permute-start.1) | collective-permute-done | bytes 196640 | tf_op jit(solution)/shard_map/ppermute | solution.py:273
  19.9 3.1 %collective-permute-start.6 = (bf16[128,512]{1,0:T(8,128)(2,1)S(1)}, bf16[128,512]{1,0:T(8,128)(2,1)S(1)}, u32[]{:S(2)}, u32[]{:S(2)}) collective-permute-start(bf16[128,512]{1,0:T(8,128)(2,1)S(1)} %slice.21.refs_7_), channel_id=1, source_target_pairs={{0,8},{1,9},{2,10},{3,11},{4,12},{5,13},{6,14},{7,15},{8,0},{9,1},... | collective-permute-start | bytes 393224 | tf_op jit(solution)/shard_map/ppermute | solution.py:273
  23.5 2.0 %collective-permute-done.5.refs_8_ = bf16[128,768]{1,0:T(8,128)(2,1)S(1)} collective-permute-done((bf16[128,768]{1,0:T(8,128)(2,1)S(1)}, bf16[128,768]{1,0:T(8,128)(2,1)S(1)}, u32[]{:S(2)}, u32[]{:S(2)}) %collective-permute-start.5) | collective-permute-done | bytes 196640 | tf_op jit(solution)/shard_map/ppermute | solution.py:273
  28.5 3.3 %collective-permute-start.9 = (bf16[128,512]{1,0:T(8,128)(2,1)S(1)}, bf16[128,512]{1,0:T(8,128)(2,1)S(1)}, u32[]{:S(2)}, u32[]{:S(2)}) collective-permute-start(bf16[128,512]{1,0:T(8,128)(2,1)S(1)} %collective-permute-done.6.refs_11_), channel_id=1, source_target_pairs={{0,16},{1,17},{2,18},{3,19},{4,20},{5,21},{6,22},{7,23},{8,24},{9,... | collective-permute-start | bytes 393224 | tf_op jit(solution)/shard_map/ppermute | solution.py:273
  33.4 1.3 %collective-permute-done.9.refs_12_ = bf16[128,512]{1,0:T(8,128)(2,1)S(1)} collective-permute-done((bf16[128,512]{1,0:T(8,128)(2,1)S(1)}, bf16[128,512]{1,0:T(8,128)(2,1)S(1)}, u32[]{:S(2)}, u32[]{:S(2)}) %collective-permute-start.9) | collective-permute-done | bytes 131104 | tf_op jit(solution)/shard_map/ppermute | solution.py:273
  34.7 1.5 %collective-permute-start.12 = (bf16[128,768]{1,0:T(8,128)(2,1)S(1)}, bf16[128,768]{1,0:T(8,128)(2,1)S(1)}, u32[]{:S(2)}, u32[]{:S(2)}) collective-permute-start(bf16[128,768]{1,0:T(8,128)(2,1)S(1)} %get-tuple-element.47.refs_3_), channel_id=1, source_target_pairs={{0,2},{1,3},{2,0},{3,1},{4,6},{5,7},{6,4},{7,5},{8,10},{9,11},{10,... | collective-permute-start | bytes 589832 | tf_op jit(solution)/shard_map/ppermute | solution.py:273
  37.1 2.4 %collective-permute-done.11.refs_5_ = bf16[128,768]{1,0:T(8,128)(2,1)S(1)} collective-permute-done((bf16[128,768]{1,0:T(8,128)(2,1)S(1)}, bf16[128,768]{1,0:T(8,128)(2,1)S(1)}, u32[]{:S(2)}, u32[]{:S(2)}) %collective-permute-start.11) | collective-permute-done | bytes 196640 | tf_op jit(solution)/shard_map/ppermute | solution.py:273
  39.6 2.9 %collective-permute-done.12.refs_4_ = bf16[128,768]{1,0:T(8,128)(2,1)S(1)} collective-permute-done((bf16[128,768]{1,0:T(8,128)(2,1)S(1)}, bf16[128,768]{1,0:T(8,128)(2,1)S(1)}, u32[]{:S(2)}, u32[]{:S(2)}) %collective-permute-start.12) | collective-permute-done | bytes 196640 | tf_op jit(solution)/shard_map/ppermute | solution.py:273
  42.5 1.5 %collective-permute-start.13 = (bf16[128,768]{1,0:T(8,128)(2,1)S(1)}, bf16[128,768]{1,0:T(8,128)(2,1)S(1)}, u32[]{:S(2)}, u32[]{:S(2)}) collective-permute-start(bf16[128,768]{1,0:T(8,128)(2,1)S(1)} %collective-permute-done.11.refs_5_), channel_id=1, source_target_pairs={{0,2},{1,3},{2,0},{3,1},{4,6},{5,7},{6,4},{7,5},{8,10},{9,11},{10,... | collective-permute-start | bytes 589832 | tf_op jit(solution)/shard_map/ppermute | solution.py:273
  44.7 2.6 %collective-permute-start.19 = (bf16[128,768]{1,0:T(8,128)(2,1)S(1)}, bf16[128,768]{1,0:T(8,128)(2,1)}, u32[]{:S(2)}, u32[]{:S(2)}) collective-permute-start(bf16[128,768]{1,0:T(8,128)(2,1)S(1)} %get-tuple-element.47.refs_3_), channel_id=1, source_target_pairs={{0,4},{1,5},{2,6},{3,7},{4,0},{5,1},{6,2},{7,3},{8,12},{9,13},{10,... | collective-permute-start | bytes 589832 | tf_op jit(solution)/shard_map/ppermute | solution.py:273
  47.3 2.1 %collective-permute-start.18 = (bf16[128,768]{1,0:T(8,128)(2,1)}, bf16[128,768]{1,0:T(8,128)(2,1)}, u32[]{:S(2)}, u32[]{:S(2)}) collective-permute-start(bf16[128,768]{1,0:T(8,128)(2,1)} %collective-permute-done.17.refs_9_), channel_id=1, source_target_pairs={{0,16},{1,17},{2,18},{3,19},{4,20},{5,21},{6,22},{7,23},{8,24},{9,... | collective-permute-start | bytes 589832 | tf_op jit(solution)/shard_map/ppermute | solution.py:273
  50.7 2.4 %collective-permute-start.15 = (bf16[128,768]{1,0:T(8,128)(2,1)S(1)}, bf16[128,768]{1,0:T(8,128)(2,1)S(1)}, u32[]{:S(2)}, u32[]{:S(2)}) collective-permute-start(bf16[128,768]{1,0:T(8,128)(2,1)S(1)} %collective-permute-done.10.refs_7_), channel_id=1, source_target_pairs={{0,16},{1,17},{2,18},{3,19},{4,20},{5,21},{6,22},{7,23},{8,24},{9,... | collective-permute-start | bytes 589832 | tf_op jit(solution)/shard_map/ppermute | solution.py:273
  55.3 1.7 %collective-permute-done.14.refs_9_ = bf16[128,768]{1,0:T(8,128)(2,1)} collective-permute-done((bf16[128,768]{1,0:T(8,128)(2,1)S(1)}, bf16[128,768]{1,0:T(8,128)(2,1)}, u32[]{:S(2)}, u32[]{:S(2)}) %collective-permute-start.14) | collective-permute-done | bytes 196640 | tf_op jit(solution)/shard_map/ppermute | solution.py:273
  57.0 2.1 %collective-permute-start.21 = (bf16[128,768]{1,0:T(8,128)(2,1)}, bf16[128,768]{1,0:T(8,128)(2,1)S(1)}, u32[]{:S(2)}, u32[]{:S(2)}) collective-permute-start(bf16[128,768]{1,0:T(8,128)(2,1)} %collective-permute-done.14.refs_9_), channel_id=1, source_target_pairs={{0,16},{1,17},{2,18},{3,19},{4,20},{5,21},{6,22},{7,23},{8,24},{9,... | collective-permute-start | bytes 589832 | tf_op jit(solution)/shard_map/ppermute | solution.py:273
  61.7 8.9 %attention.2 = (bf16[512,256]{1,0:T(8,128)(2,1)S(1)}, bf16[512,256]{1,0:T(8,128)(2,1)S(1)}) custom-call(s32[9]{0:T(128)S(1)} %compare_select_fusion.refs_0_, bf16[512,1024]{1,0:T(8,128)(2,1)S(1)} %norm.1.refs_1_, bf16[512,1024]{1,0:T(8,128)(2,1)} %collective-permute-done.16.refs_2_, bf16[128,768]{1,0:T(8,128)(2,1)S(1)} %get-tuple-element.41.refs_3_, ...), custom_call_target="tpu_custom_call" | custom-call | flops 1879048192 | bytes 3670016 | tf_op jit(solution)/shard_map/attention/pallas_call | solution.py:154
  72.3 8.4 %attention.3 = (bf16[512,256]{1,0:T(8,128)(2,1)S(1)}, bf16[512,256]{1,0:T(8,128)(2,1)S(1)}) custom-call(s32[9]{0:T(128)S(1)} %compare_select_fusion.refs_0_, bf16[512,1024]{1,0:T(8,128)(2,1)S(1)} %norm.1.refs_1_, bf16[512,1024]{1,0:T(8,128)(2,1)} %collective-permute-done.16.refs_2_, bf16[128,768]{1,0:T(8,128)(2,1)S(1)} %get-tuple-element.47.refs_3_, ...), custom_call_target="tpu_custom_call" | custom-call | flops 1879048192 | bytes 3670016 | tf_op jit(solution)/shard_map/attention/pallas_call | solution.py:154
  83.5 5.0 %router.1 = (f32[512,1024]{1,0:T(8,128)S(1)}, bf16[2,32,256]{2,1,0:T(8,128)(2,1)S(1)}, bf16[2,32,1024]{2,1,0:T(8,128)(2,1)S(1)}) custom-call(s32[9]{0:T(128)S(1)} %compare_select_fusion.refs_0_, bf16[512,1024]{1,0:T(8,128)(2,1)S(1)} %bitcast.113, bf16[32,1024]{1,0:T(8,128)(2,1)S(1)} %bitcast.115, bf16[512,256]{1,0:T(8,128)(2,1)S(1)} %get-tuple-element.45.refs_3_, ...), custom_call_target="tpu_custom_call" | custom-call | flops 1140850688 | bytes 6291456 | tf_op jit(solution)/shard_map/router/pallas_call | solution.py:234
  88.6 13.0 %all_to_all.10 = bf16[2,32,1024]{2,0,1:T(2,128)(2,1)S(1)} all-to-all(bf16[2,32,1024]{2,0,1:T(2,128)(2,1)S(1)} %copy.15), channel_id=1, replica_groups=mesh['group'=2,'expert'=16] {'expert'}, dimensions={1} | all-to-all | bytes 262144 | tf_op jit(solution)/shard_map/all_to_all | solution.py:378
  101.6 6.1 %fusion.7 = bf16[2,16,1,2,1024]{4,1,3,0,2:T(8,128)(2,1)S(1)} fusion(bf16[1,2048,1024]{2,1,0:T(8,128)(2,1)} %param.12, bf16[1,1024,2048]{2,1,0:T(8,128)(2,1)} %param.11, bf16[2,16,2,1024]{3,0,2,1:T(2,128)(2,1)S(1)} %bitcast.117), kind=kOutput, calls=%fused_computation.6 | convolution fusion | flops 545456128 | bytes 8650752 | tf_op jit(solution)/shard_map/bneph,ehd->bnepd/dot_general | solution.py:382
  107.8 10.5 %all_to_all.11 = bf16[2,32,1024]{2,0,1:T(2,128)(2,1)S(1)} all-to-all(bf16[2,32,1024]{2,0,1:T(2,128)(2,1)S(1)} %bitcast.116), channel_id=1, replica_groups=mesh['group'=2,'expert'=16] {'expert'}, dimensions={1} | all-to-all | bytes 262144 | tf_op jit(solution)/shard_map/all_to_all | solution.py:384
  (85 shorter events, 23.2 us)
Async XLA Ops:
  3.7 10.3 %collective-permute-start.3 = (bf16[128,768]{1,0:T(8,128)(2,1)S(1)}, bf16[128,768]{1,0:T(8,128)(2,1)S(1)}, u32[]{:S(2)}, u32[]{:S(2)}) collective-permute-start(bf16[128,768]{1,0:T(8,128)(2,1)S(1)} %get-tuple-element.41.refs_3_), channel_id=1, source_target_pairs={{0,2},{1,3},{2,0},{3,1},{4,6},{5,7},{6,4},{7,5},{8,10},{9,11},{10,... | collective-permute-start | bytes 589832 | tf_op jit(solution)/shard_map/ppermute | solution.py:273
  6.7 7.4 %collective-permute-start.2 = (bf16[128,512]{1,0:T(8,128)(2,1)S(1)}, bf16[128,512]{1,0:T(8,128)(2,1)S(1)}, u32[]{:S(2)}, u32[]{:S(2)}) collective-permute-start(bf16[128,512]{1,0:T(8,128)(2,1)S(1)} %slice.21.refs_7_), channel_id=1, source_target_pairs={{0,4},{1,5},{2,6},{3,7},{4,0},{5,1},{6,2},{7,3},{8,12},{9,13},{10,... | collective-permute-start | bytes 393224 | tf_op jit(solution)/shard_map/ppermute | solution.py:273
  8.3 11.5 %collective-permute-start.1 = (bf16[128,768]{1,0:T(8,128)(2,1)S(1)}, bf16[128,768]{1,0:T(8,128)(2,1)S(1)}, u32[]{:S(2)}, u32[]{:S(2)}) collective-permute-start(bf16[128,768]{1,0:T(8,128)(2,1)S(1)} %get-tuple-element.41.refs_3_), channel_id=1, source_target_pairs={{0,8},{1,9},{2,10},{3,11},{4,12},{5,13},{6,14},{7,15},{8,0},{9,1},... | collective-permute-start | bytes 589832 | tf_op jit(solution)/shard_map/ppermute | solution.py:273
  14.1 5.8 %collective-permute-start.4 = (bf16[128,512]{1,0:T(8,128)(2,1)S(1)}, bf16[128,512]{1,0:T(8,128)(2,1)S(1)}, u32[]{:S(2)}, u32[]{:S(2)}) collective-permute-start(bf16[128,512]{1,0:T(8,128)(2,1)S(1)} %collective-permute-done.2.refs_9_), channel_id=1, source_target_pairs={{0,2},{1,3},{2,0},{3,1},{4,6},{5,7},{6,4},{7,5},{8,10},{9,11},{10,... | collective-permute-start | bytes 393224 | tf_op jit(solution)/shard_map/ppermute | solution.py:273
  19.9 5.7 %collective-permute-start.5 = (bf16[128,768]{1,0:T(8,128)(2,1)S(1)}, bf16[128,768]{1,0:T(8,128)(2,1)S(1)}, u32[]{:S(2)}, u32[]{:S(2)}) collective-permute-start(bf16[128,768]{1,0:T(8,128)(2,1)S(1)} %collective-permute-done.1.refs_7_), channel_id=1, source_target_pairs={{0,16},{1,17},{2,18},{3,19},{4,20},{5,21},{6,22},{7,23},{8,24},{9,... | collective-permute-start | bytes 589832 | tf_op jit(solution)/shard_map/ppermute | solution.py:273
  19.9 7.6 %collective-permute-start.6 = (bf16[128,512]{1,0:T(8,128)(2,1)S(1)}, bf16[128,512]{1,0:T(8,128)(2,1)S(1)}, u32[]{:S(2)}, u32[]{:S(2)}) collective-permute-start(bf16[128,512]{1,0:T(8,128)(2,1)S(1)} %slice.21.refs_7_), channel_id=1, source_target_pairs={{0,8},{1,9},{2,10},{3,11},{4,12},{5,13},{6,14},{7,15},{8,0},{9,1},... | collective-permute-start | bytes 393224 | tf_op jit(solution)/shard_map/ppermute | solution.py:273
  27.4 32.3 %collective-permute-start.16 = (bf16[512,1024]{1,0:T(8,128)(2,1)S(1)}, bf16[512,1024]{1,0:T(8,128)(2,1)}, u32[]{:S(2)}, u32[]{:S(2)}) collective-permute-start(bf16[512,1024]{1,0:T(8,128)(2,1)S(1)} %norm.1.refs_1_), channel_id=1, source_target_pairs={{0,1},{1,0},{2,3},{3,2},{4,5},{5,4},{6,7},{7,6},{8,9},{9,8},{10,11... | collective-permute-start | bytes 3145736 | tf_op jit(solution)/shard_map/ppermute | solution.py:273
  28.5 6.2 %collective-permute-start.9 = (bf16[128,512]{1,0:T(8,128)(2,1)S(1)}, bf16[128,512]{1,0:T(8,128)(2,1)S(1)}, u32[]{:S(2)}, u32[]{:S(2)}) collective-permute-start(bf16[128,512]{1,0:T(8,128)(2,1)S(1)} %collective-permute-done.6.refs_11_), channel_id=1, source_target_pairs={{0,16},{1,17},{2,18},{3,19},{4,20},{5,21},{6,22},{7,23},{8,24},{9,... | collective-permute-start | bytes 393224 | tf_op jit(solution)/shard_map/ppermute | solution.py:273
  31.8 7.8 %collective-permute-start.11 = (bf16[128,768]{1,0:T(8,128)(2,1)S(1)}, bf16[128,768]{1,0:T(8,128)(2,1)S(1)}, u32[]{:S(2)}, u32[]{:S(2)}) collective-permute-start(bf16[128,768]{1,0:T(8,128)(2,1)S(1)} %get-tuple-element.41.refs_3_), channel_id=1, source_target_pairs={{0,4},{1,5},{2,6},{3,7},{4,0},{5,1},{6,2},{7,3},{8,12},{9,13},{10,... | collective-permute-start | bytes 589832 | tf_op jit(solution)/shard_map/ppermute | solution.py:273
  34.7 7.8 %collective-permute-start.12 = (bf16[128,768]{1,0:T(8,128)(2,1)S(1)}, bf16[128,768]{1,0:T(8,128)(2,1)S(1)}, u32[]{:S(2)}, u32[]{:S(2)}) collective-permute-start(bf16[128,768]{1,0:T(8,128)(2,1)S(1)} %get-tuple-element.47.refs_3_), channel_id=1, source_target_pairs={{0,2},{1,3},{2,0},{3,1},{4,6},{5,7},{6,4},{7,5},{8,10},{9,11},{10,... | collective-permute-start | bytes 589832 | tf_op jit(solution)/shard_map/ppermute | solution.py:273
  36.3 13.1 %collective-permute-start.10 = (bf16[128,768]{1,0:T(8,128)(2,1)S(1)}, bf16[128,768]{1,0:T(8,128)(2,1)S(1)}, u32[]{:S(2)}, u32[]{:S(2)}) collective-permute-start(bf16[128,768]{1,0:T(8,128)(2,1)S(1)} %get-tuple-element.47.refs_3_), channel_id=1, source_target_pairs={{0,8},{1,9},{2,10},{3,11},{4,12},{5,13},{6,14},{7,15},{8,0},{9,1},... | collective-permute-start | bytes 589832 | tf_op jit(solution)/shard_map/ppermute | solution.py:273
  36.6 10.7 %collective-permute-start.17 = (bf16[128,768]{1,0:T(8,128)(2,1)S(1)}, bf16[128,768]{1,0:T(8,128)(2,1)}, u32[]{:S(2)}, u32[]{:S(2)}) collective-permute-start(bf16[128,768]{1,0:T(8,128)(2,1)S(1)} %collective-permute-done.1.refs_7_), channel_id=1, source_target_pairs={{0,2},{1,3},{2,0},{3,1},{4,6},{5,7},{6,4},{7,5},{8,10},{9,11},{10,... | collective-permute-start | bytes 589832 | tf_op jit(solution)/shard_map/ppermute | solution.py:273
  42.5 6.8 %collective-permute-start.13 = (bf16[128,768]{1,0:T(8,128)(2,1)S(1)}, bf16[128,768]{1,0:T(8,128)(2,1)S(1)}, u32[]{:S(2)}, u32[]{:S(2)}) collective-permute-start(bf16[128,768]{1,0:T(8,128)(2,1)S(1)} %collective-permute-done.11.refs_5_), channel_id=1, source_target_pairs={{0,2},{1,3},{2,0},{3,1},{4,6},{5,7},{6,4},{7,5},{8,10},{9,11},{10,... | collective-permute-start | bytes 589832 | tf_op jit(solution)/shard_map/ppermute | solution.py:273
  44.7 9.7 %collective-permute-start.19 = (bf16[128,768]{1,0:T(8,128)(2,1)S(1)}, bf16[128,768]{1,0:T(8,128)(2,1)}, u32[]{:S(2)}, u32[]{:S(2)}) collective-permute-start(bf16[128,768]{1,0:T(8,128)(2,1)S(1)} %get-tuple-element.47.refs_3_), channel_id=1, source_target_pairs={{0,4},{1,5},{2,6},{3,7},{4,0},{5,1},{6,2},{7,3},{8,12},{9,13},{10,... | collective-permute-start | bytes 589832 | tf_op jit(solution)/shard_map/ppermute | solution.py:273
  47.3 7.1 %collective-permute-start.18 = (bf16[128,768]{1,0:T(8,128)(2,1)}, bf16[128,768]{1,0:T(8,128)(2,1)}, u32[]{:S(2)}, u32[]{:S(2)}) collective-permute-start(bf16[128,768]{1,0:T(8,128)(2,1)} %collective-permute-done.17.refs_9_), channel_id=1, source_target_pairs={{0,16},{1,17},{2,18},{3,19},{4,20},{5,21},{6,22},{7,23},{8,24},{9,... | collective-permute-start | bytes 589832 | tf_op jit(solution)/shard_map/ppermute | solution.py:273
  50.0 7.0 %collective-permute-start.14 = (bf16[128,768]{1,0:T(8,128)(2,1)S(1)}, bf16[128,768]{1,0:T(8,128)(2,1)}, u32[]{:S(2)}, u32[]{:S(2)}) collective-permute-start(bf16[128,768]{1,0:T(8,128)(2,1)S(1)} %collective-permute-done.10.refs_7_), channel_id=1, source_target_pairs={{0,2},{1,3},{2,0},{3,1},{4,6},{5,7},{6,4},{7,5},{8,10},{9,11},{10,... | collective-permute-start | bytes 589832 | tf_op jit(solution)/shard_map/ppermute | solution.py:273
  50.7 8.5 %collective-permute-start.15 = (bf16[128,768]{1,0:T(8,128)(2,1)S(1)}, bf16[128,768]{1,0:T(8,128)(2,1)S(1)}, u32[]{:S(2)}, u32[]{:S(2)}) collective-permute-start(bf16[128,768]{1,0:T(8,128)(2,1)S(1)} %collective-permute-done.10.refs_7_), channel_id=1, source_target_pairs={{0,16},{1,17},{2,18},{3,19},{4,20},{5,21},{6,22},{7,23},{8,24},{9,... | collective-permute-start | bytes 589832 | tf_op jit(solution)/shard_map/ppermute | solution.py:273
  54.4 16.1 %collective-permute-start.20 = (bf16[128,768]{1,0:T(8,128)(2,1)}, bf16[128,768]{1,0:T(8,128)(2,1)S(1)}, u32[]{:S(2)}, u32[]{:S(2)}) collective-permute-start(bf16[128,768]{1,0:T(8,128)(2,1)} %collective-permute-done.19.refs_5_), channel_id=1, source_target_pairs={{0,2},{1,3},{2,0},{3,1},{4,6},{5,7},{6,4},{7,5},{8,10},{9,11},{10,... | collective-permute-start | bytes 589832 | tf_op jit(solution)/shard_map/ppermute | solution.py:273
  57.0 14.1 %collective-permute-start.21 = (bf16[128,768]{1,0:T(8,128)(2,1)}, bf16[128,768]{1,0:T(8,128)(2,1)S(1)}, u32[]{:S(2)}, u32[]{:S(2)}) collective-permute-start(bf16[128,768]{1,0:T(8,128)(2,1)} %collective-permute-done.14.refs_9_), channel_id=1, source_target_pairs={{0,16},{1,17},{2,18},{3,19},{4,20},{5,21},{6,22},{7,23},{8,24},{9,... | collective-permute-start | bytes 589832 | tf_op jit(solution)/shard_map/ppermute | solution.py:273
  59.1 21.5 %collective-permute-start.25 = (bf16[128,512]{1,0:T(8,128)(2,1)S(1)}, bf16[128,512]{1,0:T(8,128)(2,1)S(1)}, u32[]{:S(2)}, u32[]{:S(2)}) collective-permute-start(bf16[128,512]{1,0:T(8,128)(2,1)S(1)} %slice.21.refs_7_), channel_id=1, source_target_pairs={{0,1},{1,0},{2,3},{3,2},{4,5},{5,4},{6,7},{7,6},{8,9},{9,8},{10,11... | collective-permute-start | bytes 393224 | tf_op jit(solution)/shard_map/ppermute | solution.py:273
  59.2 21.7 %collective-permute-start.26 = (bf16[128,512]{1,0:T(8,128)(2,1)S(1)}, bf16[128,512]{1,0:T(8,128)(2,1)S(1)}, u32[]{:S(2)}, u32[]{:S(2)}) collective-permute-start(bf16[128,512]{1,0:T(8,128)(2,1)S(1)} %collective-permute-done.7.refs_8_), channel_id=1, source_target_pairs={{0,1},{1,0},{2,3},{3,2},{4,5},{5,4},{6,7},{7,6},{8,9},{9,8},{10,11... | collective-permute-start | bytes 393224 | tf_op jit(solution)/shard_map/ppermute | solution.py:273
  59.7 21.7 %collective-permute-start.27 = (bf16[128,512]{1,0:T(8,128)(2,1)S(1)}, bf16[128,512]{1,0:T(8,128)(2,1)S(1)}, u32[]{:S(2)}, u32[]{:S(2)}) collective-permute-start(bf16[128,512]{1,0:T(8,128)(2,1)S(1)} %collective-permute-done.2.refs_9_), channel_id=1, source_target_pairs={{0,1},{1,0},{2,3},{3,2},{4,5},{5,4},{6,7},{7,6},{8,9},{9,8},{10,11... | collective-permute-start | bytes 393224 | tf_op jit(solution)/shard_map/ppermute | solution.py:273
  70.6 11.2 %collective-permute-start.29 = (bf16[128,512]{1,0:T(8,128)(2,1)S(1)}, bf16[128,512]{1,0:T(8,128)(2,1)S(1)}, u32[]{:S(2)}, u32[]{:S(2)}) collective-permute-start(bf16[128,512]{1,0:T(8,128)(2,1)S(1)} %collective-permute-done.6.refs_11_), channel_id=1, source_target_pairs={{0,1},{1,0},{2,3},{3,2},{4,5},{5,4},{6,7},{7,6},{8,9},{9,8},{10,11... | collective-permute-start | bytes 393224 | tf_op jit(solution)/shard_map/ppermute | solution.py:273
  71.1 10.2 %collective-permute-start.24 = (bf16[128,512]{1,0:T(8,128)(2,1)S(1)}, bf16[128,512]{1,0:T(8,128)(2,1)S(1)}, u32[]{:S(2)}, u32[]{:S(2)}) collective-permute-start(bf16[128,512]{1,0:T(8,128)(2,1)S(1)} %collective-permute-done.8.refs_13_), channel_id=1, source_target_pairs={{0,16},{1,17},{2,18},{3,19},{4,20},{5,21},{6,22},{7,23},{8,24},{9,... | collective-permute-start | bytes 393224 | tf_op jit(solution)/shard_map/ppermute | solution.py:273
  (22 other events, 191.6 us)

commit v3 on v2

v3 whole, which is shorter than its diff:
```python
import functools

import jax
import jax.numpy as jnp
from jax import lax
from jax.experimental import pallas as pl
from jax.experimental.pallas import tpu as pltpu
from jax.sharding import PartitionSpec as P

HEADS = 16
EXPERT_STEPS = 4
CHIPS = 8
LONG = 1 << 34
EARLY = (0, 1, 2, 4, 6)
LATE = (3, 5, 7)
AXES = ("group", "expert")
F32 = jnp.float32
BF16 = jnp.bfloat16


def layer_norm(values):
    center = values - jnp.mean(values, axis=-1, keepdims=True)
    spread = jnp.mean(center * center, axis=-1, keepdims=True)
    return center * lax.rsqrt(spread + 1e-06)


def is_grid(groups, experts):
    return groups == 2 and experts == 16


def chip_of(block):
    far = lax.axis_index("group") * 2
    mask = (block, block, block, block, 4 + far, 6 - far, 5 + far, 7 - far)[block]
    return jnp.bitwise_xor(lax.axis_index("expert") // 2, mask)


def core_of():
    return lax.axis_index("expert") % 2


def norm_kernel(tokens_ref, *refs):
    mine_ref, other_ref, scratch = refs[-3:]
    scratch[...] = layer_norm(tokens_ref[...].astype(F32)).astype(BF16)
    core = core_of()
    block = mine_ref.shape[1] // CHIPS
    for at in range(CHIPS):
        start = pl.multiple_of(chip_of(at) * block, block)
        columns = scratch[:, pl.ds(start, block)]
        swapped = pltpu.roll(columns.astype(F32), block // 2, 1).astype(BF16)
        place = slice(at * block, (at + 1) * block)
        mine_ref[:, place] = jnp.where(core == 0, columns, swapped)
        other_ref[:, place] = jnp.where(core == 0, swapped, columns)


def norm(tokens, image, length, before, others=(), cost=0):
    rows, width = tokens.shape
    piece = pl.BlockSpec((length, width), lambda step: (image, 0))
    return pl.pallas_call(
        norm_kernel,
        out_shape=[jax.ShapeDtypeStruct((rows, width), BF16)] * 2,
        grid=(1,),
        in_specs=[piece] + [pl.BlockSpec(memory_space=pl.ANY)] * len((*others, *before)),
        out_specs=[piece] * 2,
        scratch_shapes=[pltpu.VMEM((length, width), BF16)],
        input_output_aliases={1: 0, 2: 1} if others else {},
        compiler_params=pltpu.CompilerParams(vmem_limit_bytes=16 << 20),
        cost_estimate=pl.CostEstimate(
            flops=cost or 8 * length * width,
            bytes_accessed=6 * length * width,
            transcendentals=length,
        ),
        name="norm",
    )(tokens, *others, *before)


def copy_kernel(count, *refs):
    for source, target in zip(refs[:count], refs[-count:]):
        target[...] = source[...]


def copies(values, before):
    vmem = pl.BlockSpec(memory_space=pltpu.VMEM)
    return pl.pallas_call(
        functools.partial(copy_kernel, len(values)),
        out_shape=[jax.ShapeDtypeStruct(value.shape, value.dtype) for value in values],
        in_specs=[vmem] * len(values) + [pl.BlockSpec(memory_space=pl.ANY)] * len(before),
        out_specs=[vmem] * len(values),
        compiler_params=pltpu.CompilerParams(vmem_limit_bytes=4 << 20),
        cost_estimate=pl.CostEstimate(flops=0, bytes_accessed=0, transcendentals=0),
        name="copies",
    )(*values, *before)


def split_kernel(weight_ref, *refs):
    span = weight_ref.shape[1] // 12
    for side, target in enumerate(refs[-2:]):
        core = jnp.bitwise_xor(core_of(), side)
        for chunk in range(2):
            for which in range(3):
                start = (which * 4 + core * 2 + chunk) * span
                at = (chunk * 3 + which) * span
                target[:, at : at + span] = weight_ref[:, pl.ds(pl.multiple_of(start, span), span)]


def split_out_kernel(weight_ref, *refs):
    span = weight_ref.shape[1] // 2
    for side, target in enumerate(refs[-2:]):
        start = jnp.bitwise_xor(core_of(), side) * span
        target[...] = weight_ref[:, pl.ds(pl.multiple_of(start, span), span)]


def split(kernel, weight, before=()):
    rows, columns = weight.shape
    vmem = pl.BlockSpec(memory_space=pltpu.VMEM)
    return pl.pallas_call(
        kernel,
        out_shape=[jax.ShapeDtypeStruct((rows, columns // 2), BF16)] * 2,
        in_specs=[vmem] + [pl.BlockSpec(memory_space=pl.ANY)] * len(before),
        out_specs=[vmem] * 2,
        compiler_params=pltpu.CompilerParams(vmem_limit_bytes=8 << 20),
        cost_estimate=pl.CostEstimate(
            flops=0, bytes_accessed=4 * rows * columns, transcendentals=0
        ),
        name="split",
    )(weight, *before)


def attend(query, keys, values, head, out_ref, rows, columns):
    lane = lax.broadcasted_iota(jnp.int32, query.shape, 1)
    first = lane < head
    result = []
    for mask in (first, ~first):
        scores = lax.dot_general(
            jnp.where(mask, query, jnp.zeros_like(query)),
            keys,
            (((1,), (1,)), ((), ())),
            preferred_element_type=F32,
        )
        top = jnp.max(scores, axis=-1, keepdims=True)
        weights = jnp.exp(scores - top).astype(BF16)
        mixed = jnp.dot(
            weights, jnp.where(mask, values, jnp.ones_like(values)), preferred_element_type=F32
        )
        result.append(mixed / pltpu.roll(mixed, head, 1))
    out_ref[rows, columns] = jnp.where(first, result[0], result[1]).astype(BF16)


def attention_kernel(length, head, normed, weight, *refs):
    out_ref = refs[-1]
    span = out_ref.shape[1]
    pair = 2 * head

    def project(at):
        return jnp.dot(
            normed[...], weight[:, at * span : (at + 1) * span], preferred_element_type=F32
        )

    query = (project(0) * head**-0.5).astype(BF16)
    keys = project(1).astype(BF16)
    values = project(2).astype(BF16)
    for start in range(0, normed.shape[0], length):
        rows = slice(start, start + length)
        for left in range(0, span, pair):
            columns = slice(left, left + pair)
            attend(
                query[rows, columns],
                keys[rows, columns],
                values[rows, columns],
                head,
                out_ref,
                rows,
                columns,
            )


def attention(normed, weight, length, head, before=()):
    rows, width = normed.shape
    span = weight.shape[1] // 3
    vmem = pl.BlockSpec(memory_space=pltpu.VMEM)
    return pl.pallas_call(
        functools.partial(attention_kernel, length, head),
        out_shape=jax.ShapeDtypeStruct((rows, span), BF16),
        in_specs=[vmem] * 2 + [pl.BlockSpec(memory_space=pl.ANY)] * len(before),
        out_specs=vmem,
        compiler_params=pltpu.CompilerParams(vmem_limit_bytes=20 << 20),
        cost_estimate=pl.CostEstimate(
            flops=2 * rows * span * (3 * width + 2 * length),
            bytes_accessed=6 * width * span + 4 * rows * width,
            transcendentals=rows * (span // head) * length,
        ),
        name="attention",
    )(normed, weight, *before)


def router_kernel(count, images, length, *refs):
    tokens_ref, keys_ref = refs[:2]
    parts = refs[2:6]
    sources = refs[6:10]
    resid_ref, combine_ref, inputs_ref = refs[10:13]
    weight, sem = refs[13:]
    core = core_of()
    span = sources[0].shape[1]
    half = weight.shape[0] // (2 * count)
    copies = []
    for which, source in enumerate(sources):
        side = which // 2
        left = pl.multiple_of(jnp.bitwise_xor(core, side) * span, span)
        for at, block in enumerate((EARLY, LATE)[which % 2]):
            for part in range(2):
                start = (2 * chip_of(block) + jnp.bitwise_xor(core, part ^ side)) * half
                copy = pltpu.make_async_copy(
                    source.at[pl.ds((2 * at + part) * half, half)],
                    weight.at[pl.ds(pl.multiple_of(start, half), half), pl.ds(left, span)],
                    sem.at[len(copies)],
                )
                copy.start()
                copies.append(copy)
    for copy in copies:
        copy.wait()
    inner = parts[0].shape[1]
    for image in range(images):
        at = slice(image * length, (image + 1) * length)
        resid = tokens_ref[at].astype(F32)
        for which, part in enumerate(parts):
            side, chunk = which // 2, which % 2
            start = (2 * jnp.bitwise_xor(core, side) + chunk) * inner
            resid += jnp.dot(
                part[at],
                weight[pl.ds(pl.multiple_of(start, inner), inner)],
                preferred_element_type=F32,
            )
        resid_ref[at] = resid
        normed = layer_norm(resid).astype(BF16)
        logits = lax.dot_general(
            keys_ref[...], normed, (((1,), (1,)), ((), ())), preferred_element_type=F32
        )
        dispatch = jax.nn.softmax(logits, axis=1).astype(BF16)
        combine_ref[image] = jax.nn.softmax(logits, axis=0).astype(BF16)
        inputs_ref[image] = jnp.dot(dispatch, normed, preferred_element_type=F32).astype(BF16)


def router(tokens, slot_keys, parts, blocks, images, length):
    rows, width = tokens.shape
    slots = slot_keys.shape[1]
    count = CHIPS
    vmem = pl.BlockSpec(memory_space=pltpu.VMEM)
    hbm = pl.BlockSpec(memory_space=pl.ANY)
    return pl.pallas_call(
        functools.partial(router_kernel, count, images, length),
        out_shape=[
            jax.ShapeDtypeStruct((rows, width), F32),
            jax.ShapeDtypeStruct((images, slots, length), BF16),
            jax.ShapeDtypeStruct((images, slots, width), BF16),
        ],
        in_specs=[vmem] * 6 + [hbm] * 4,
        out_specs=[vmem] * 3,
        scratch_shapes=[
            pltpu.VMEM((width, width), BF16),
            pltpu.SemaphoreType.DMA((4 * count,)),
        ],
        compiler_params=pltpu.CompilerParams(vmem_limit_bytes=24 << 20),
        cost_estimate=pl.CostEstimate(
            flops=2 * rows * width * (width + 2 * slots),
            bytes_accessed=2 * width * width + 8 * rows * width,
            transcendentals=2 * rows * slots,
        ),
        name="router",
    )(tokens, slot_keys.T, *parts, *blocks)


def expert_kernel(inputs_ref, first_ref, second_ref, out_ref, total):
    step = pl.program_id(1)
    hidden = jnp.dot(inputs_ref[0], first_ref[0], preferred_element_type=F32)
    hidden = (0.5 * hidden * (1.0 + lax.erf(hidden * 0.5**0.5))).astype(BF16)
    answer = jnp.dot(hidden, second_ref[0], preferred_element_type=F32)

    @pl.when(step == 0)
    def _():
        total[...] = answer

    @pl.when(step > 0)
    def _():
        total[...] += answer

    @pl.when(step == pl.num_programs(1) - 1)
    def _():
        out_ref[0] = total[...].astype(BF16)


def experts_here(inputs, first, second):
    count, rows, width = inputs.shape
    hidden = first.shape[2]
    piece = hidden // EXPERT_STEPS
    return pl.pallas_call(
        expert_kernel,
        out_shape=jax.ShapeDtypeStruct(inputs.shape, BF16),
        grid=(count, EXPERT_STEPS),
        in_specs=[
            pl.BlockSpec((1, rows, width), lambda e, h: (e, 0, 0)),
            pl.BlockSpec((1, width, piece), lambda e, h: (e, 0, h)),
            pl.BlockSpec((1, piece, width), lambda e, h: (e, h, 0)),
        ],
        out_specs=pl.BlockSpec((1, rows, width), lambda e, h: (e, 0, 0)),
        scratch_shapes=[pltpu.VMEM((rows, width), F32)],
        compiler_params=pltpu.CompilerParams(vmem_limit_bytes=24 << 20),
        cost_estimate=pl.CostEstimate(
            flops=4 * count * rows * width * hidden,
            bytes_accessed=4 * count * width * hidden,
            transcendentals=count * rows * hidden,
        ),
        name="experts",
    )(inputs, first, second)


def front_on_grid(groups, experts, tokens, w_qkv, w_attn_out, slot_keys):
    images, length, width = tokens.shape
    head = width // HEADS
    flat = tokens.reshape(images * length, width)
    def send(value, move):
        pairs = []
        for at in range(groups):
            mask, flip = move(at)
            for index in range(experts):
                target = (at ^ flip) * experts + (index ^ mask)
                pairs.append((at * experts + index, target))
        return lax.ppermute(value, AXES, pairs)

    def in_chip(value):
        return send(value, lambda at: (1, 0))

    def over_y(value):
        return send(value, lambda at: (2, 0))

    def near_z(value):
        return send(value, lambda at: (4, 0))

    def far_z(value):
        return send(value, lambda at: (12, 0) if at else (8, 0))

    def over_x(value):
        return send(value, lambda at: (0, 1))

    span = width // 4
    keep, give = split(split_kernel, w_qkv)
    block = jnp.concatenate([keep, in_chip(give)], axis=0)
    a = block[:, : 3 * span]
    b = block[:, 3 * span :]

    def whole(*blocks):
        return jnp.concatenate(blocks, axis=0)

    def step(*values, done=()):
        nonlocal token
        *result, token = copies([*values, token], done)
        return result

    a_far = far_z(a)
    a_near = near_z(a)
    a_y = over_y(a)
    normed, normed_sent = norm(flat, 0, length, (a,), cost=LONG)
    token = normed[:8, :128]
    (b_1,) = step(b)
    b_y = over_y(b_1)
    a_far_1, b_2 = step(a_far, b, done=(a_y, a_near))
    b_far = far_z(b_2)
    a_x = over_x(a_far_1)
    a_y_far = over_y(a_far_1)
    (a_near_1,) = step(a_near, done=(b_y,))
    a_y_near = over_y(a_near_1)
    for image in range(1, images):
        normed, normed_sent = norm(flat, image, length, (token,), (normed, normed_sent), LONG)
    (a_y_far_1,) = step(a_y_far)
    a_x_far = over_x(a_y_far_1)
    out_keep, out_give = split(split_out_kernel, w_attn_out, (token,))
    c = jnp.concatenate([out_keep, in_chip(out_give)], axis=0)
    b_3, c_1 = step(b, c, done=(a_x,))
    b_near = near_z(b_3)
    c_y = over_y(c_1)
    normed_other = in_chip(normed_sent)
    b_far_1, c_2 = step(b_far, c, done=(a_y_near, a_x_far))
    b_x = over_x(b_far_1)
    b_y_far = over_y(b_far_1)
    c_far = far_z(c_2)
    a_all = whole(a, a_y, a_near, a_y_near, a_far, a_x, a_y_far, a_x_far)
    other_a = attention(normed_other, a_all, length, head, (token,))
    mine_a = attention(normed, a_all, length, head, (other_a,))
    (b_near_1,) = step(b_near, done=(mine_a, c_y))
    b_y_near = over_y(b_near_1)
    (b_y_far_1,) = step(b_y_far)
    b_x_far = over_x(b_y_far_1)
    (c_3,) = step(c, done=(b_x,))
    c_near = near_z(c_3)
    (c_far_1,) = step(c_far)
    c_y_far = over_y(c_far_1)
    c_x = over_x(c_far_1)
    (c_near_1,) = step(c_near, done=(b_y_near,))
    c_y_near = over_y(c_near_1)
    (c_y_far_1,) = step(c_y_far)
    c_x_far = over_x(c_y_far_1)
    (other_a_1,) = step(other_a, done=(b_x_far,))
    parts_a = in_chip(other_a_1)
    b_all = whole(b, b_y, b_near, b_y_near, b_far, b_x, b_y_far, b_x_far)
    other_b = attention(normed_other, b_all, length, head, (token,))
    early = whole(c, c_y, c_near, c_far, c_y_far)
    late = whole(*step(c_y_near, c_x, c_x_far, done=(other_b,)))
    parts_b = in_chip(other_b)
    mine_b = attention(normed, b_all, length, head, (other_b,))
    parts = [mine_a, mine_b, parts_a, parts_b]
    outs = [early, late, in_chip(early), in_chip(late)]
    return router(flat, slot_keys, parts, outs, images, length)


def front(tokens, w_qkv, w_attn_out, slot_keys):
    images, length, width = tokens.shape
    head = width // HEADS
    rows = images * length
    normed = layer_norm(tokens.astype(F32)).astype(BF16).reshape(rows, width)
    full_qkv = lax.all_gather(w_qkv, "expert", axis=0, tiled=True)
    qkv = jnp.dot(normed, full_qkv, preferred_element_type=F32).astype(BF16)
    query, keys, values = [
        part[:, :, 0] for part in jnp.split(qkv.reshape(images, length, 3, HEADS, head), 3, axis=2)
    ]
    scores = jnp.einsum("bqhd,bkhd->bhqk", query, keys, preferred_element_type=F32) * head**-0.5
    weights = jax.nn.softmax(scores, axis=-1).astype(BF16)
    attended = jnp.einsum("bhqk,bkhd->bqhd", weights, values, preferred_element_type=F32)
    full_out = lax.all_gather(w_attn_out, "expert", axis=0, tiled=True)
    projected = jnp.dot(
        attended.astype(BF16).reshape(rows, width), full_out, preferred_element_type=F32
    )
    resid = tokens.astype(F32).reshape(rows, width) + projected
    normed_two = layer_norm(resid).astype(BF16).reshape(images, length, width)
    logits = jnp.einsum("bsd,dn->bns", normed_two, slot_keys, preferred_element_type=F32)
    dispatch = jax.nn.softmax(logits, axis=2).astype(BF16)
    combine = jax.nn.softmax(logits, axis=1).astype(BF16)
    slot_inputs = jnp.einsum("bns,bsd->bnd", dispatch, normed_two, preferred_element_type=F32)
    return resid, combine, slot_inputs.astype(BF16)


def on_device(mesh_shape, tokens, w_qkv, w_attn_out, slot_keys, w_expert_in, w_expert_out):
    images, length, width = tokens.shape
    if is_grid(*mesh_shape):
        resid, combine, slot_inputs = front_on_grid(
            *mesh_shape, tokens, w_qkv, w_attn_out, slot_keys
        )
    else:
        resid, combine, slot_inputs = front(tokens, w_qkv, w_attn_out, slot_keys)
    slots = slot_keys.shape[1]
    sources = mesh_shape[1]
    expert_here = w_expert_in.shape[0]
    pairs = slots // (sources * expert_here)
    block = lax.all_to_all(slot_inputs, "expert", split_axis=1, concat_axis=1, tiled=True)
    arranged = block.reshape(images, sources, expert_here, pairs, width)
    arranged = arranged.transpose(2, 0, 1, 3, 4).reshape(expert_here, -1, width)
    answer = experts_here(arranged, w_expert_in, w_expert_out)
    answer = answer.reshape(expert_here, images, sources, pairs, width)
    answered = answer.transpose(1, 2, 0, 3, 4).reshape(images, slots, width)
    slot_outputs = lax.all_to_all(answered, "expert", split_axis=1, concat_axis=1, tiled=True)
    mixed = jnp.einsum("bns,bnd->bsd", combine, slot_outputs, preferred_element_type=F32)
    return (resid.reshape(images, length, width) + mixed).astype(BF16)


def solution(mesh):
    placed = (
        P(AXES, None, None),
        P("expert", None),
        P("expert", None),
        P(),
        P("expert", None, None),
        P("expert", None, None),
    )
    return jax.shard_map(
        functools.partial(on_device, (mesh.shape["group"], mesh.shape["expert"])),
        mesh=mesh,
        in_specs=placed,
        out_specs=P(AXES, None, None),
        check_vma=False,
    )
```

time: 121 us -> 96 us (0.79)
  starting transfers between devices: 34.4 us -> 28.2 us
  matrix products: 6.56 us -> 0.47 us
  local copies, waits for them, and re-layouts: 7.42 us -> 1.79 us
  Pallas kernels: 22.9 us -> 19.9 us
  waiting for transfers between devices: 23.9 us -> 21.7 us
  blocking collectives: 23.5 us -> 21.9 us
    ppermute x33 -> x28, starting transfers between devices: 34.4 us -> 28.2 us  [send(): return lax.ppermute(value, AXES, pairs)]
    dot_general x1 -> x0, matrix products: 6.09 us -> none  [on_device(): jnp.einsum('bneph,ehd->bnepd', hidden, w_expert_out, preferred_element_ty...]
    unnamed x27 -> x33, local copies, waits for them, and re-layouts: 7.09 us -> 1.43 us
    pallas_call x4 -> x23, Pallas kernels: 17.9 us -> 15.6 us  [the longest x4 10.5 us: attention(): pl.pallas_call(functools.partial(attention_kernel, length, head), out_sha...]
    ppermute x33 -> x28, waiting for transfers between devices: 23.9 us -> 21.7 us  [send(): return lax.ppermute(value, AXES, pairs)]
    all_to_all x1, blocking collectives: 13 us -> 11.4 us  [on_device(): lax.all_to_all(slot_inputs, 'expert', split_axis=1, concat_axis=1, tiled=...]
  transfers between devices with their start and end apart: 33 -> 28, of which waited for: 15 -> 11; matrix products, arithmetic and copies ran while one was open for 0% -> 0% of each run, Pallas kernels for 15% -> 13%
where the time goes in v3:
time: 96 us; the launch traced here: 95.8 us
  starting transfers between devices  28.2 us (29%)
  blocking collectives  21.9 us (23%)
  waiting for transfers between devices  21.7 us (23%)
  Pallas kernels  19.9 us (21%)
  local copies, waits for them, and re-layouts  1.79 us (2%)
  other arithmetic  1.27 us (1%)
    ppermute x28, starting transfers between devices, send(): return lax.ppermute(value, AXES, pairs)  28.2 us
    ppermute x28, waiting for transfers between devices, send(): return lax.ppermute(value, AXES, pairs)  21.7 us
    all_to_all x1, blocking collectives, on_device(): lax.all_to_all(slot_inputs, 'expert', split_axis=1, concat_axis=1, tiled=...  11.4 us
    all_to_all x1, blocking collectives, on_device(): lax.all_to_all(answered, 'expert', split_axis=1, concat_axis=1, tiled=True)  10.5 us
    pallas_call x4, Pallas kernels, attention(): pl.pallas_call(functools.partial(attention_kernel, length, head), out_sha...  10.5 us
    pallas_call x1, Pallas kernels, router(): pl.pallas_call(functools.partial(router_kernel, count, images, length), o...  4.29 us
    pallas_call x1, Pallas kernels, experts_here(): pl.pallas_call(expert_kernel, out_shape=jax.ShapeDtypeStruct(inputs.shape...  2.75 us
  transfers between devices with their start and end apart: 28, of which 11 were waited for; matrix products, arithmetic and copies ran while one was open for 0% of the time, Pallas kernels for 13%

profile of v3, /device:TPU:0, one launch (start us, length us, event | category | flops | bytes accessed | tf_op | source)
XLA Modules:
  0.0 95.8 jit_solution(11340415787198157933)
XLA Ops:
  2.8 3.0 %collective-permute-start.3 = (bf16[128,768]{1,0:T(8,128)(2,1)S(1)}, bf16[128,768]{1,0:T(8,128)(2,1)S(1)}, u32[]{:S(2)}, u32[]{:S(2)}) collective-permute-start(bf16[128,768]{1,0:T(8,128)(2,1)S(1)} %get-tuple-element.94.refs_0_), channel_id=1, source_target_pairs={{0,2},{1,3},{2,0},{3,1},{4,6},{5,7},{6,4},{7,5},{8,10},{9,11},{10,... | collective-permute-start | bytes 589832 | tf_op jit(solution)/shard_map/ppermute | solution.py:326
  5.8 2.6 %collective-permute-start.2 = (bf16[128,768]{1,0:T(8,128)(2,1)S(1)}, bf16[128,768]{1,0:T(8,128)(2,1)S(1)}, u32[]{:S(2)}, u32[]{:S(2)}) collective-permute-start(bf16[128,768]{1,0:T(8,128)(2,1)S(1)} %get-tuple-element.94.refs_0_), channel_id=1, source_target_pairs={{0,8},{1,9},{2,10},{3,11},{4,12},{5,13},{6,14},{7,15},{8,0},{9,1},... | collective-permute-start | bytes 589832 | tf_op jit(solution)/shard_map/ppermute | solution.py:326
  8.4 1.6 %collective-permute-start.1 = (bf16[128,768]{1,0:T(8,128)(2,1)S(1)}, bf16[128,768]{1,0:T(8,128)(2,1)S(1)}, u32[]{:S(2)}, u32[]{:S(2)}) collective-permute-start(bf16[128,768]{1,0:T(8,128)(2,1)S(1)} %get-tuple-element.94.refs_0_), channel_id=1, source_target_pairs={{0,4},{1,5},{2,6},{3,7},{4,0},{5,1},{6,2},{7,3},{8,12},{9,13},{10,... | collective-permute-start | bytes 589832 | tf_op jit(solution)/shard_map/ppermute | solution.py:326
  11.3 6.3 %collective-permute-done.2.refs_0_ = bf16[128,768]{1,0:T(8,128)(2,1)S(1)} collective-permute-done((bf16[128,768]{1,0:T(8,128)(2,1)S(1)}, bf16[128,768]{1,0:T(8,128)(2,1)S(1)}, u32[]{:S(2)}, u32[]{:S(2)}) %collective-permute-start.2) | collective-permute-done | bytes 196640 | tf_op jit(solution)/shard_map/ppermute | solution.py:326
  18.4 2.3 %collective-permute-start.6 = (bf16[128,768]{1,0:T(8,128)(2,1)S(1)}, bf16[128,768]{1,0:T(8,128)(2,1)S(1)}, u32[]{:S(2)}, u32[]{:S(2)}) collective-permute-start(bf16[128,768]{1,0:T(8,128)(2,1)S(1)} %get-tuple-element.58), channel_id=1, source_target_pairs={{0,16},{1,17},{2,18},{3,19},{4,20},{5,21},{6,22},{7,23},{8,24},{9,... | collective-permute-start | bytes 589832 | tf_op jit(solution)/shard_map/ppermute | solution.py:326
  21.4 1.6 %collective-permute-start.5 = (bf16[128,768]{1,0:T(8,128)(2,1)S(1)}, bf16[128,768]{1,0:T(8,128)(2,1)S(1)}, u32[]{:S(2)}, u32[]{:S(2)}) collective-permute-start(bf16[128,768]{1,0:T(8,128)(2,1)S(1)} %get-tuple-element.57), channel_id=1, source_target_pairs={{0,2},{1,3},{2,0},{3,1},{4,6},{5,7},{6,4},{7,5},{8,10},{9,11},{10,... | collective-permute-start | bytes 589832 | tf_op jit(solution)/shard_map/ppermute | solution.py:326
  24.5 3.3 %collective-permute-done.5.refs_3_ = bf16[128,768]{1,0:T(8,128)(2,1)S(1)} collective-permute-done((bf16[128,768]{1,0:T(8,128)(2,1)S(1)}, bf16[128,768]{1,0:T(8,128)(2,1)S(1)}, u32[]{:S(2)}, u32[]{:S(2)}) %collective-permute-start.5) | collective-permute-done | bytes 196640 | tf_op jit(solution)/shard_map/ppermute | solution.py:326
  27.8 3.4 %collective-permute-start.8 = (bf16[128,768]{1,0:T(8,128)(2,1)S(1)}, bf16[128,768]{1,0:T(8,128)(2,1)S(1)}, u32[]{:S(2)}, u32[]{:S(2)}) collective-permute-start(bf16[128,768]{1,0:T(8,128)(2,1)S(1)} %get-tuple-element.59), channel_id=1, source_target_pairs={{0,16},{1,17},{2,18},{3,19},{4,20},{5,21},{6,22},{7,23},{8,24},{9,... | collective-permute-start | bytes 589832 | tf_op jit(solution)/shard_map/ppermute | solution.py:326
  32.7 2.8 %collective-permute-done.8.refs_4_ = bf16[128,768]{1,0:T(8,128)(2,1)S(1)} collective-permute-done((bf16[128,768]{1,0:T(8,128)(2,1)S(1)}, bf16[128,768]{1,0:T(8,128)(2,1)S(1)}, u32[]{:S(2)}, u32[]{:S(2)}) %collective-permute-start.8) | collective-permute-done | bytes 196640 | tf_op jit(solution)/shard_map/ppermute | solution.py:326
  35.6 1.9 %collective-permute-start.15 = (bf16[128,768]{1,0:T(8,128)(2,1)S(1)}, bf16[128,768]{1,0:T(8,128)(2,1)S(1)}, u32[]{:S(2)}, u32[]{:S(2)}) collective-permute-start(bf16[128,768]{1,0:T(8,128)(2,1)S(1)} %get-tuple-element.70), channel_id=1, source_target_pairs={{0,16},{1,17},{2,18},{3,19},{4,20},{5,21},{6,22},{7,23},{8,24},{9,... | collective-permute-start | bytes 589832 | tf_op jit(solution)/shard_map/ppermute | solution.py:326
  37.6 2.6 %attention.4.refs_0_ = bf16[512,256]{1,0:T(8,128)(2,1)S(1)} custom-call(bf16[512,1024]{1,0:T(8,128)(2,1)S(1)} %collective-permute-done.9.normed, bf16[1024,768]{1,0:T(8,128)(2,1)S(1)} %constant_dynamic-update-slice_fusion.2.weight, bf16[8,128]{1,0:T(8,128)(2,1)S(1)} %get-tuple-element.66.refs_0_.refs_1_), custom_call_target="tpu_custom_call" | custom-call | flops 939524096 | bytes 3670016 | tf_op jit(solution)/shard_map/attention/pallas_call | solution.py:180
  40.2 2.6 %attention.5.refs_2_ = bf16[512,256]{1,0:T(8,128)(2,1)S(1)} custom-call(bf16[512,1024]{1,0:T(8,128)(2,1)S(1)} %get-tuple-element.56.normed, bf16[1024,768]{1,0:T(8,128)(2,1)S(1)} %constant_dynamic-update-slice_fusion.2.weight, bf16[512,256]{1,0:T(8,128)(2,1)S(1)} %attention.4.refs_0_), custom_call_target="tpu_custom_call" | custom-call | flops 939524096 | bytes 3670016 | tf_op jit(solution)/shard_map/attention/pallas_call | solution.py:180
  42.9 1.7 %collective-permute-start.20 = (bf16[128,512]{1,0:T(8,128)(2,1)S(1)}, bf16[128,512]{1,0:T(8,128)(2,1)S(1)}, u32[]{:S(2)}, u32[]{:S(2)}) collective-permute-start(bf16[128,512]{1,0:T(8,128)(2,1)S(1)} %get-tuple-element.77), channel_id=1, source_target_pairs={{0,4},{1,5},{2,6},{3,7},{4,0},{5,1},{6,2},{7,3},{8,12},{9,13},{10,... | collective-permute-start | bytes 393224 | tf_op jit(solution)/shard_map/ppermute | solution.py:326
  46.0 1.8 %collective-permute-start.19 = (bf16[128,512]{1,0:T(8,128)(2,1)S(1)}, bf16[128,512]{1,0:T(8,128)(2,1)S(1)}, u32[]{:S(2)}, u32[]{:S(2)}) collective-permute-start(bf16[128,512]{1,0:T(8,128)(2,1)S(1)} %get-tuple-element.76), channel_id=1, source_target_pairs={{0,2},{1,3},{2,0},{3,1},{4,6},{5,7},{6,4},{7,5},{8,10},{9,11},{10,... | collective-permute-start | bytes 393224 | tf_op jit(solution)/shard_map/ppermute | solution.py:326
  49.1 2.2 %collective-permute-done.19.refs_0_ = bf16[128,512]{1,0:T(8,128)(2,1)S(1)} collective-permute-done((bf16[128,512]{1,0:T(8,128)(2,1)S(1)}, bf16[128,512]{1,0:T(8,128)(2,1)S(1)}, u32[]{:S(2)}, u32[]{:S(2)}) %collective-permute-start.19) | collective-permute-done | bytes 131104 | tf_op jit(solution)/shard_map/ppermute | solution.py:326
  51.4 3.0 %collective-permute-done.14.refs_2_ = bf16[128,768]{1,0:T(8,128)(2,1)S(1)} collective-permute-done((bf16[128,768]{1,0:T(8,128)(2,1)S(1)}, bf16[128,768]{1,0:T(8,128)(2,1)S(1)}, u32[]{:S(2)}, u32[]{:S(2)}) %collective-permute-start.14) | collective-permute-done | bytes 196640 | tf_op jit(solution)/shard_map/ppermute | solution.py:326
  54.4 1.2 %collective-permute-start.25 = (bf16[128,512]{1,0:T(8,128)(2,1)S(1)}, bf16[128,512]{1,0:T(8,128)(2,1)S(1)}, u32[]{:S(2)}, u32[]{:S(2)}) collective-permute-start(bf16[128,512]{1,0:T(8,128)(2,1)S(1)} %get-tuple-element.84), channel_id=1, source_target_pairs={{0,16},{1,17},{2,18},{3,19},{4,20},{5,21},{6,22},{7,23},{8,24},{9,... | collective-permute-start | bytes 393224 | tf_op jit(solution)/shard_map/ppermute | solution.py:326
  56.1 2.6 %attention.6.refs_0_.refs_4_ = bf16[512,256]{1,0:T(8,128)(2,1)S(1)} custom-call(bf16[512,1024]{1,0:T(8,128)(2,1)S(1)} %collective-permute-done.9.normed, bf16[1024,768]{1,0:T(8,128)(2,1)S(1)} %constant_dynamic-update-slice_fusion.12.weight, bf16[8,128]{1,0:T(8,128)(2,1)S(1)} %get-tuple-element.81.refs_0_.refs_3_), custom_call_target="tpu_custom_call" | custom-call | flops 939524096 | bytes 3670016 | tf_op jit(solution)/shard_map/attention/pallas_call | solution.py:180
  61.9 2.8 %attention.7.refs_3_ = bf16[512,256]{1,0:T(8,128)(2,1)S(1)} custom-call(bf16[512,1024]{1,0:T(8,128)(2,1)S(1)} %get-tuple-element.56.normed, bf16[1024,768]{1,0:T(8,128)(2,1)S(1)} %constant_dynamic-update-slice_fusion.12.weight, bf16[512,256]{1,0:T(8,128)(2,1)S(1)} %attention.6.refs_0_.refs_4_), custom_call_target="tpu_custom_call" | custom-call | flops 939524096 | bytes 3670016 | tf_op jit(solution)/shard_map/attention/pallas_call | solution.py:180
  64.8 4.3 %router.1 = (f32[512,1024]{1,0:T(8,128)S(1)}, bf16[2,32,256]{2,1,0:T(8,128)(2,1)S(1)}, bf16[2,32,1024]{2,1,0:T(8,128)(2,1)S(1)}) custom-call(bf16[512,1024]{1,0:T(8,128)(2,1)S(1)} %bitcast.9, bf16[32,1024]{1,0:T(8,128)(2,1)S(1)} %bitcast.12, bf16[512,256]{1,0:T(8,128)(2,1)S(1)} %attention.5.refs_2_, bf16[512,256]{1,0:T(8,128)(2,1)S(1)} %attention.7.refs_3_, ...), custom_call_target="tpu_custom_call" | custom-call | flops 1140850688 | bytes 6291456 | tf_op jit(solution)/shard_map/router/pallas_call | solution.py:248
  69.2 11.4 %all_to_all.10 = bf16[2,32,1024]{2,0,1:T(2,128)(2,1)S(1)} all-to-all(bf16[2,32,1024]{2,0,1:T(2,128)(2,1)S(1)} %copy.9), channel_id=1, replica_groups=mesh['group'=2,'expert'=16] {'expert'}, dimensions={1} | all-to-all | bytes 262144 | tf_op jit(solution)/shard_map/all_to_all | solution.py:451
  80.7 2.8 %experts.1 = bf16[1,64,1024]{2,1,0:T(8,128)(2,1)S(1)} custom-call(bf16[1,64,1024]{2,1,0:T(8,128)(2,1)S(1)} %bitcast.10, bf16[1,1024,2048]{2,1,0:T(8,128)(2,1)S(1)} %copy-done, bf16[1,2048,1024]{2,1,0:T(8,128)(2,1)S(1)} %copy-done.1), custom_call_target="tpu_custom_call" | custom-call | flops 536870912 | bytes 8388608 | tf_op jit(solution)/shard_map/experts/pallas_call | solution.py:294
  83.6 10.5 %all_to_all.11 = bf16[2,32,1024]{2,0,1:T(2,128)(2,1)S(1)} all-to-all(bf16[2,32,1024]{2,0,1:T(2,128)(2,1)S(1)} %copy.11), channel_id=1, replica_groups=mesh['group'=2,'expert'=16] {'expert'}, dimensions={1} | all-to-all | bytes 262144 | tf_op jit(solution)/shard_map/all_to_all | solution.py:457
  94.6 1.3 %add_convert_fusion = bf16[2,256,1024]{2,1,0:T(8,128)(2,1)} fusion(f32[2,256,1024]{2,1,0:T(8,128)S(1)} %bitcast.6, f32[2,256,1024]{2,1,0:T(8,128)S(1)} %fusion), kind=kLoop, calls=%fused_computation | loop fusion | flops 1048576 | bytes 5242880 | tf_op jit(solution)/shard_map/convert_element_type | solution.py:459
  (102 shorter events, 15.9 us)
Async XLA Ops:
  2.8 8.5 %collective-permute-start.3 = (bf16[128,768]{1,0:T(8,128)(2,1)S(1)}, bf16[128,768]{1,0:T(8,128)(2,1)S(1)}, u32[]{:S(2)}, u32[]{:S(2)}) collective-permute-start(bf16[128,768]{1,0:T(8,128)(2,1)S(1)} %get-tuple-element.94.refs_0_), channel_id=1, source_target_pairs={{0,2},{1,3},{2,0},{3,1},{4,6},{5,7},{6,4},{7,5},{8,10},{9,11},{10,... | collective-permute-start | bytes 589832 | tf_op jit(solution)/shard_map/ppermute | solution.py:326
  5.8 11.9 %collective-permute-start.2 = (bf16[128,768]{1,0:T(8,128)(2,1)S(1)}, bf16[128,768]{1,0:T(8,128)(2,1)S(1)}, u32[]{:S(2)}, u32[]{:S(2)}) collective-permute-start(bf16[128,768]{1,0:T(8,128)(2,1)S(1)} %get-tuple-element.94.refs_0_), channel_id=1, source_target_pairs={{0,8},{1,9},{2,10},{3,11},{4,12},{5,13},{6,14},{7,15},{8,0},{9,1},... | collective-permute-start | bytes 589832 | tf_op jit(solution)/shard_map/ppermute | solution.py:326
  8.4 9.5 %collective-permute-start.1 = (bf16[128,768]{1,0:T(8,128)(2,1)S(1)}, bf16[128,768]{1,0:T(8,128)(2,1)S(1)}, u32[]{:S(2)}, u32[]{:S(2)}) collective-permute-start(bf16[128,768]{1,0:T(8,128)(2,1)S(1)} %get-tuple-element.94.refs_0_), channel_id=1, source_target_pairs={{0,4},{1,5},{2,6},{3,7},{4,0},{5,1},{6,2},{7,3},{8,12},{9,13},{10,... | collective-permute-start | bytes 589832 | tf_op jit(solution)/shard_map/ppermute | solution.py:326
  10.7 10.6 %collective-permute-start.4 = (bf16[128,768]{1,0:T(8,128)(2,1)S(1)}, bf16[128,768]{1,0:T(8,128)(2,1)S(1)}, u32[]{:S(2)}, u32[]{:S(2)}) collective-permute-start(bf16[128,768]{1,0:T(8,128)(2,1)S(1)} %get-tuple-element.54), channel_id=1, source_target_pairs={{0,2},{1,3},{2,0},{3,1},{4,6},{5,7},{6,4},{7,5},{8,10},{9,11},{10,... | collective-permute-start | bytes 589832 | tf_op jit(solution)/shard_map/ppermute | solution.py:326
  17.9 6.5 %collective-permute-start.7 = (bf16[128,768]{1,0:T(8,128)(2,1)S(1)}, bf16[128,768]{1,0:T(8,128)(2,1)S(1)}, u32[]{:S(2)}, u32[]{:S(2)}) collective-permute-start(bf16[128,768]{1,0:T(8,128)(2,1)S(1)} %get-tuple-element.58), channel_id=1, source_target_pairs={{0,2},{1,3},{2,0},{3,1},{4,6},{5,7},{6,4},{7,5},{8,10},{9,11},{10,... | collective-permute-start | bytes 589832 | tf_op jit(solution)/shard_map/ppermute | solution.py:326
  18.4 12.9 %collective-permute-start.6 = (bf16[128,768]{1,0:T(8,128)(2,1)S(1)}, bf16[128,768]{1,0:T(8,128)(2,1)S(1)}, u32[]{:S(2)}, u32[]{:S(2)}) collective-permute-start(bf16[128,768]{1,0:T(8,128)(2,1)S(1)} %get-tuple-element.58), channel_id=1, source_target_pairs={{0,16},{1,17},{2,18},{3,19},{4,20},{5,21},{6,22},{7,23},{8,24},{9,... | collective-permute-start | bytes 589832 | tf_op jit(solution)/shard_map/ppermute | solution.py:326
  20.7 12.0 %collective-permute-start.10 = (bf16[128,768]{1,0:T(8,128)(2,1)S(1)}, bf16[128,768]{1,0:T(8,128)(2,1)S(1)}, u32[]{:S(2)}, u32[]{:S(2)}) collective-permute-start(bf16[128,768]{1,0:T(8,128)(2,1)S(1)} %get-tuple-element.61), channel_id=1, source_target_pairs={{0,8},{1,9},{2,10},{3,11},{4,12},{5,13},{6,14},{7,15},{8,0},{9,1},... | collective-permute-start | bytes 589832 | tf_op jit(solution)/shard_map/ppermute | solution.py:326
  21.4 6.5 %collective-permute-start.5 = (bf16[128,768]{1,0:T(8,128)(2,1)S(1)}, bf16[128,768]{1,0:T(8,128)(2,1)S(1)}, u32[]{:S(2)}, u32[]{:S(2)}) collective-permute-start(bf16[128,768]{1,0:T(8,128)(2,1)S(1)} %get-tuple-element.57), channel_id=1, source_target_pairs={{0,2},{1,3},{2,0},{3,1},{4,6},{5,7},{6,4},{7,5},{8,10},{9,11},{10,... | collective-permute-start | bytes 589832 | tf_op jit(solution)/shard_map/ppermute | solution.py:326
  23.7 13.8 %collective-permute-start.9 = (bf16[512,1024]{1,0:T(8,128)(2,1)S(1)}, bf16[512,1024]{1,0:T(8,128)(2,1)S(1)}, u32[]{:S(2)}, u32[]{:S(2)}) collective-permute-start(bf16[512,1024]{1,0:T(8,128)(2,1)S(1)} %get-tuple-element.60), channel_id=1, source_target_pairs={{0,1},{1,0},{2,3},{3,2},{4,5},{5,4},{6,7},{7,6},{8,9},{9,8},{10,11... | collective-permute-start | bytes 3145736 | tf_op jit(solution)/shard_map/ppermute | solution.py:326
  24.4 7.0 %collective-permute-start.11 = (bf16[64,512]{1,0:T(8,128)(2,1)S(1)}, bf16[64,512]{1,0:T(8,128)(2,1)S(1)}, u32[]{:S(2)}, u32[]{:S(2)}) collective-permute-start(bf16[64,512]{1,0:T(8,128)(2,1)S(1)} %get-tuple-element.64), channel_id=1, source_target_pairs={{0,1},{1,0},{2,3},{3,2},{4,5},{5,4},{6,7},{7,6},{8,9},{9,8},{10,11... | collective-permute-start | bytes 196616 | tf_op jit(solution)/shard_map/ppermute | solution.py:326
  27.8 7.6 %collective-permute-start.8 = (bf16[128,768]{1,0:T(8,128)(2,1)S(1)}, bf16[128,768]{1,0:T(8,128)(2,1)S(1)}, u32[]{:S(2)}, u32[]{:S(2)}) collective-permute-start(bf16[128,768]{1,0:T(8,128)(2,1)S(1)} %get-tuple-element.59), channel_id=1, source_target_pairs={{0,16},{1,17},{2,18},{3,19},{4,20},{5,21},{6,22},{7,23},{8,24},{9,... | collective-permute-start | bytes 589832 | tf_op jit(solution)/shard_map/ppermute | solution.py:326
  31.4 11.3 %collective-permute-start.13 = (bf16[128,512]{1,0:T(8,128)(2,1)S(1)}, bf16[128,512]{1,0:T(8,128)(2,1)S(1)}, u32[]{:S(2)}, u32[]{:S(2)}) collective-permute-start(bf16[128,512]{1,0:T(8,128)(2,1)S(1)} %get-tuple-element.68), channel_id=1, source_target_pairs={{0,2},{1,3},{2,0},{3,1},{4,6},{5,7},{6,4},{7,5},{8,10},{9,11},{10,... | collective-permute-start | bytes 393224 | tf_op jit(solution)/shard_map/ppermute | solution.py:326
  32.0 10.8 %collective-permute-start.12 = (bf16[128,768]{1,0:T(8,128)(2,1)S(1)}, bf16[128,768]{1,0:T(8,128)(2,1)S(1)}, u32[]{:S(2)}, u32[]{:S(2)}) collective-permute-start(bf16[128,768]{1,0:T(8,128)(2,1)S(1)} %get-tuple-element.67), channel_id=1, source_target_pairs={{0,4},{1,5},{2,6},{3,7},{4,0},{5,1},{6,2},{7,3},{8,12},{9,13},{10,... | collective-permute-start | bytes 589832 | tf_op jit(solution)/shard_map/ppermute | solution.py:326
  35.5 7.3 %collective-permute-start.16 = (bf16[128,768]{1,0:T(8,128)(2,1)S(1)}, bf16[128,768]{1,0:T(8,128)(2,1)S(1)}, u32[]{:S(2)}, u32[]{:S(2)}) collective-permute-start(bf16[128,768]{1,0:T(8,128)(2,1)S(1)} %get-tuple-element.70), channel_id=1, source_target_pairs={{0,2},{1,3},{2,0},{3,1},{4,6},{5,7},{6,4},{7,5},{8,10},{9,11},{10,... | collective-permute-start | bytes 589832 | tf_op jit(solution)/shard_map/ppermute | solution.py:326
  35.6 7.2 %collective-permute-start.15 = (bf16[128,768]{1,0:T(8,128)(2,1)S(1)}, bf16[128,768]{1,0:T(8,128)(2,1)S(1)}, u32[]{:S(2)}, u32[]{:S(2)}) collective-permute-start(bf16[128,768]{1,0:T(8,128)(2,1)S(1)} %get-tuple-element.70), channel_id=1, source_target_pairs={{0,16},{1,17},{2,18},{3,19},{4,20},{5,21},{6,22},{7,23},{8,24},{9,... | collective-permute-start | bytes 589832 | tf_op jit(solution)/shard_map/ppermute | solution.py:326
  37.5 7.4 %collective-permute-start.18 = (bf16[128,512]{1,0:T(8,128)(2,1)S(1)}, bf16[128,512]{1,0:T(8,128)(2,1)S(1)}, u32[]{:S(2)}, u32[]{:S(2)}) collective-permute-start(bf16[128,512]{1,0:T(8,128)(2,1)S(1)} %get-tuple-element.73), channel_id=1, source_target_pairs={{0,8},{1,9},{2,10},{3,11},{4,12},{5,13},{6,14},{7,15},{8,0},{9,1},... | collective-permute-start | bytes 393224 | tf_op jit(solution)/shard_map/ppermute | solution.py:326
  42.9 6.2 %collective-permute-start.20 = (bf16[128,512]{1,0:T(8,128)(2,1)S(1)}, bf16[128,512]{1,0:T(8,128)(2,1)S(1)}, u32[]{:S(2)}, u32[]{:S(2)}) collective-permute-start(bf16[128,512]{1,0:T(8,128)(2,1)S(1)} %get-tuple-element.77), channel_id=1, source_target_pairs={{0,4},{1,5},{2,6},{3,7},{4,0},{5,1},{6,2},{7,3},{8,12},{9,13},{10,... | collective-permute-start | bytes 393224 | tf_op jit(solution)/shard_map/ppermute | solution.py:326
  45.0 13.6 %collective-permute-start.24 = (bf16[128,512]{1,0:T(8,128)(2,1)S(1)}, bf16[128,512]{1,0:T(8,128)(2,1)S(1)}, u32[]{:S(2)}, u32[]{:S(2)}) collective-permute-start(bf16[128,512]{1,0:T(8,128)(2,1)S(1)} %get-tuple-element.76), channel_id=1, source_target_pairs={{0,16},{1,17},{2,18},{3,19},{4,20},{5,21},{6,22},{7,23},{8,24},{9,... | collective-permute-start | bytes 393224 | tf_op jit(solution)/shard_map/ppermute | solution.py:326
  46.0 5.3 %collective-permute-start.19 = (bf16[128,512]{1,0:T(8,128)(2,1)S(1)}, bf16[128,512]{1,0:T(8,128)(2,1)S(1)}, u32[]{:S(2)}, u32[]{:S(2)}) collective-permute-start(bf16[128,512]{1,0:T(8,128)(2,1)S(1)} %get-tuple-element.76), channel_id=1, source_target_pairs={{0,2},{1,3},{2,0},{3,1},{4,6},{5,7},{6,4},{7,5},{8,10},{9,11},{10,... | collective-permute-start | bytes 393224 | tf_op jit(solution)/shard_map/ppermute | solution.py:326
  47.9 8.1 %collective-permute-start.17 = (bf16[128,768]{1,0:T(8,128)(2,1)S(1)}, bf16[128,768]{1,0:T(8,128)(2,1)S(1)}, u32[]{:S(2)}, u32[]{:S(2)}) collective-permute-start(bf16[128,768]{1,0:T(8,128)(2,1)S(1)} %get-tuple-element.72), channel_id=1, source_target_pairs={{0,16},{1,17},{2,18},{3,19},{4,20},{5,21},{6,22},{7,23},{8,24},{9,... | collective-permute-start | bytes 589832 | tf_op jit(solution)/shard_map/ppermute | solution.py:326
  48.7 5.7 %collective-permute-start.14 = (bf16[128,768]{1,0:T(8,128)(2,1)S(1)}, bf16[128,768]{1,0:T(8,128)(2,1)S(1)}, u32[]{:S(2)}, u32[]{:S(2)}) collective-permute-start(bf16[128,768]{1,0:T(8,128)(2,1)S(1)} %get-tuple-element.69), channel_id=1, source_target_pairs={{0,2},{1,3},{2,0},{3,1},{4,6},{5,7},{6,4},{7,5},{8,10},{9,11},{10,... | collective-permute-start | bytes 589832 | tf_op jit(solution)/shard_map/ppermute | solution.py:326
  51.4 13.4 %collective-permute-start.26 = (bf16[640,512]{1,0:T(8,128)(2,1)S(1)}, bf16[640,512]{1,0:T(8,128)(2,1)S(1)}, u32[]{:S(2)}, u32[]{:S(2)}) collective-permute-start(bf16[640,512]{1,0:T(8,128)(2,1)S(1)} %constant_dynamic-update-slice_fusion.20.refs_6_), channel_id=1, source_target_pairs={{0,1},{1,0},{2,3},{3,2},{4,5},{5,4},{6,7},{7,6},{8,9},{9,8},{10,11... | collective-permute-start | bytes 1966088 | tf_op jit(solution)/shard_map/ppermute | solution.py:326
  54.4 5.0 %collective-permute-start.25 = (bf16[128,512]{1,0:T(8,128)(2,1)S(1)}, bf16[128,512]{1,0:T(8,128)(2,1)S(1)}, u32[]{:S(2)}, u32[]{:S(2)}) collective-permute-start(bf16[128,512]{1,0:T(8,128)(2,1)S(1)} %get-tuple-element.84), channel_id=1, source_target_pairs={{0,16},{1,17},{2,18},{3,19},{4,20},{5,21},{6,22},{7,23},{8,24},{9,... | collective-permute-start | bytes 393224 | tf_op jit(solution)/shard_map/ppermute | solution.py:326
  55.6 5.0 %collective-permute-start.23 = (bf16[128,512]{1,0:T(8,128)(2,1)S(1)}, bf16[128,512]{1,0:T(8,128)(2,1)S(1)}, u32[]{:S(2)}, u32[]{:S(2)}) collective-permute-start(bf16[128,512]{1,0:T(8,128)(2,1)S(1)} %get-tuple-element.83), channel_id=1, source_target_pairs={{0,2},{1,3},{2,0},{3,1},{4,6},{5,7},{6,4},{7,5},{8,10},{9,11},{10,... | collective-permute-start | bytes 393224 | tf_op jit(solution)/shard_map/ppermute | solution.py:326
  (10 other events, 61.7 us)

commit v4 on v3

--- a/solution.py
+++ b/solution.py
@@ -8,7 +8,7 @@
 from jax.sharding import PartitionSpec as P
 
 HEADS = 16
-EXPERT_STEPS = 4
+EXPERT_STEPS = 2
 CHIPS = 8
 LONG = 1 << 34
 EARLY = (0, 1, 2, 4, 6)
@@ -91,38 +91,40 @@
     )(*values, *before)
 
 
-def split_kernel(weight_ref, *refs):
-    span = weight_ref.shape[1] // 12
-    for side, target in enumerate(refs[-2:]):
-        core = jnp.bitwise_xor(core_of(), side)
+def split_kernel(mine_ref, other_ref, *refs):
+    span = mine_ref.shape[1] // 12
+    rows = mine_ref.shape[0]
+    for side, source in enumerate((mine_ref, other_ref)):
         for chunk in range(2):
             for which in range(3):
-                start = (which * 4 + core * 2 + chunk) * span
-                at = (chunk * 3 + which) * span
-                target[:, at : at + span] = weight_ref[:, pl.ds(pl.multiple_of(start, span), span)]
-
-
-def split_out_kernel(weight_ref, *refs):
-    span = weight_ref.shape[1] // 2
-    for side, target in enumerate(refs[-2:]):
-        start = jnp.bitwise_xor(core_of(), side) * span
-        target[...] = weight_ref[:, pl.ds(pl.multiple_of(start, span), span)]
-
-
-def split(kernel, weight, before=()):
-    rows, columns = weight.shape
+                start = (which * 4 + core_of() * 2 + chunk) * span
+                refs[chunk - 2][
+                    side * rows : (side + 1) * rows, which * span : (which + 1) * span
+                ] = source[:, pl.ds(pl.multiple_of(start, span), span)]
+
+
+def split_out_kernel(mine_ref, other_ref, *refs):
+    span = mine_ref.shape[1] // 2
+    rows = mine_ref.shape[0]
+    for side, source in enumerate((mine_ref, other_ref)):
+        start = pl.multiple_of(core_of() * span, span)
+        refs[-1][side * rows : (side + 1) * rows] = source[:, pl.ds(start, span)]
+
+
+def split(kernel, mine, other, count, columns, before=()):
+    rows = mine.shape[0]
     vmem = pl.BlockSpec(memory_space=pltpu.VMEM)
     return pl.pallas_call(
         kernel,
-        out_shape=[jax.ShapeDtypeStruct((rows, columns // 2), BF16)] * 2,
-        in_specs=[vmem] + [pl.BlockSpec(memory_space=pl.ANY)] * len(before),
-        out_specs=[vmem] * 2,
+        out_shape=[jax.ShapeDtypeStruct((2 * rows, columns), BF16)] * count,
+        in_specs=[vmem] * 2 + [pl.BlockSpec(memory_space=pl.ANY)] * len(before),
+        out_specs=[vmem] * count,
         compiler_params=pltpu.CompilerParams(vmem_limit_bytes=8 << 20),
         cost_estimate=pl.CostEstimate(
-            flops=0, bytes_accessed=4 * rows * columns, transcendentals=0
+            flops=0, bytes_accessed=8 * rows * columns, transcendentals=0
         ),
         name="split",
-    )(weight, *before)
+    )(mine, other, *before)
 
 
 def attend(query, keys, values, head, out_ref, rows, columns):
@@ -341,10 +343,7 @@
         return send(value, lambda at: (0, 1))
 
     span = width // 4
-    keep, give = split(split_kernel, w_qkv)
-    block = jnp.concatenate([keep, in_chip(give)], axis=0)
-    a = block[:, : 3 * span]
-    b = block[:, 3 * span :]
+    a, b = split(split_kernel, w_qkv, in_chip(w_qkv), 2, 3 * span)
 
     def whole(*blocks):
         return jnp.concatenate(blocks, axis=0)
@@ -371,8 +370,8 @@
         normed, normed_sent = norm(flat, image, length, (token,), (normed, normed_sent), LONG)
     (a_y_far_1,) = step(a_y_far)
     a_x_far = over_x(a_y_far_1)
-    out_keep, out_give = split(split_out_kernel, w_attn_out, (token,))
-    c = jnp.concatenate([out_keep, in_chip(out_give)], axis=0)
+    (w_out,) = step(w_attn_out)
+    (c,) = split(split_out_kernel, w_out, in_chip(w_out), 1, 2 * span)
     b_3, c_1 = step(b, c, done=(a_x,))
     b_near = near_z(b_3)
     c_y = over_y(c_1)
@@ -383,8 +382,7 @@
     c_far = far_z(c_2)
     a_all = whole(a, a_y, a_near, a_y_near, a_far, a_x, a_y_far, a_x_far)
     other_a = attention(normed_other, a_all, length, head, (token,))
-    mine_a = attention(normed, a_all, length, head, (other_a,))
-    (b_near_1,) = step(b_near, done=(mine_a, c_y))
+    (b_near_1,) = step(b_near, done=(other_a, c_y))
     b_y_near = over_y(b_near_1)
     (b_y_far_1,) = step(b_y_far)
     b_x_far = over_x(b_y_far_1)
@@ -393,7 +391,8 @@
     (c_far_1,) = step(c_far)
     c_y_far = over_y(c_far_1)
     c_x = over_x(c_far_1)
-    (c_near_1,) = step(c_near, done=(b_y_near,))
+    mine_a = attention(normed, a_all, length, head, (token,))
+    (c_near_1,) = step(c_near, done=(b_y_near, mine_a))
     c_y_near = over_y(c_near_1)
     (c_y_far_1,) = step(c_y_far)
     c_x_far = over_x(c_y_far_1)
@@ -402,7 +401,7 @@
     b_all = whole(b, b_y, b_near, b_y_near, b_far, b_x, b_y_far, b_x_far)
     other_b = attention(normed_other, b_all, length, head, (token,))
     early = whole(c, c_y, c_near, c_far, c_y_far)
-    late = whole(*step(c_y_near, c_x, c_x_far, done=(other_b,)))
+    late = whole(c_y_near, c_x, c_x_far, jnp.concatenate([other_b[:16], other_b[16:32]], axis=1))
     parts_b = in_chip(other_b)
     mine_b = attention(normed, b_all, length, head, (other_b,))
     parts = [mine_a, mine_b, parts_a, parts_b]

time: 96 us -> 93.4 us (0.973)
  starting transfers between devices: 28.2 us -> 26.2 us
  Pallas kernels: 19.9 us -> 18.7 us
  local copies, waits for them, and re-layouts: 1.79 us -> 2.84 us
    ppermute x28, starting transfers between devices: 28.2 us -> 26.2 us  [send(): return lax.ppermute(value, AXES, pairs)]
    unnamed x33 -> x31, local copies, waits for them, and re-layouts: 1.43 us -> 2.49 us
  transfers between devices with their start and end apart: 28 -> 28, of which waited for: 11 -> 12; matrix products, arithmetic and copies ran while one was open for 0% -> 0% of each run, Pallas kernels for 13% -> 13%
where the time goes in v4:
time: 93.4 us; the launch traced here: 93.2 us
  starting transfers between devices  26.2 us (28%)
  blocking collectives  22 us (24%)
  waiting for transfers between devices  21.2 us (23%)
  Pallas kernels  18.7 us (20%)
  local copies, waits for them, and re-layouts  2.84 us (3%)
  other arithmetic  1.29 us (1%)
    ppermute x28, starting transfers between devices, send(): return lax.ppermute(value, AXES, pairs)  26.2 us
    ppermute x28, waiting for transfers between devices, send(): return lax.ppermute(value, AXES, pairs)  21.2 us
    all_to_all x1, blocking collectives, on_device(): lax.all_to_all(slot_inputs, 'expert', split_axis=1, concat_axis=1, tiled=...  11.5 us
    all_to_all x1, blocking collectives, on_device(): lax.all_to_all(answered, 'expert', split_axis=1, concat_axis=1, tiled=True)  10.5 us
    pallas_call x4, Pallas kernels, attention(): pl.pallas_call(functools.partial(attention_kernel, length, head), out_sha...  10.4 us
    pallas_call x1, Pallas kernels, router(): pl.pallas_call(functools.partial(router_kernel, count, images, length), o...  4.29 us
    unnamed x31, local copies, waits for them, and re-layouts  2.49 us
    pallas_call x1, Pallas kernels, experts_here(): pl.pallas_call(expert_kernel, out_shape=jax.ShapeDtypeStruct(inputs.shape...  2.12 us
  transfers between devices with their start and end apart: 28, of which 12 were waited for; matrix products, arithmetic and copies ran while one was open for 0% of the time, Pallas kernels for 13%

profile of v4, /device:TPU:0, one launch (start us, length us, event | category | flops | bytes accessed | tf_op | source)
XLA Modules:
  0.0 93.2 jit_solution(5172941680170372802)
XLA Ops:
  0.5 1.6 %collective-permute-done.other_ref = bf16[64,3072]{1,0:T(8,128)(2,1)S(1)} collective-permute-done((bf16[64,3072]{1,0:T(8,128)(2,1)}, bf16[64,3072]{1,0:T(8,128)(2,1)S(1)}, u32[]{:S(2)}, u32[]{:S(2)}) %collective-permute-start) | collective-permute-done | bytes 393248 | tf_op jit(solution)/shard_map/ppermute | solution.py:328
  3.1 3.0 %collective-permute-start.1 = (bf16[128,768]{1,0:T(8,128)(2,1)S(1)}, bf16[128,768]{1,0:T(8,128)(2,1)S(1)}, u32[]{:S(2)}, u32[]{:S(2)}) collective-permute-start(bf16[128,768]{1,0:T(8,128)(2,1)S(1)} %get-tuple-element.45.refs_0_), channel_id=1, source_target_pairs={{0,4},{1,5},{2,6},{3,7},{4,0},{5,1},{6,2},{7,3},{8,12},{9,13},{10,... | collective-permute-start | bytes 589832 | tf_op jit(solution)/shard_map/ppermute | solution.py:328
  6.1 2.6 %collective-permute-start.2 = (bf16[128,768]{1,0:T(8,128)(2,1)S(1)}, bf16[128,768]{1,0:T(8,128)(2,1)S(1)}, u32[]{:S(2)}, u32[]{:S(2)}) collective-permute-start(bf16[128,768]{1,0:T(8,128)(2,1)S(1)} %get-tuple-element.45.refs_0_), channel_id=1, source_target_pairs={{0,8},{1,9},{2,10},{3,11},{4,12},{5,13},{6,14},{7,15},{8,0},{9,1},... | collective-permute-start | bytes 589832 | tf_op jit(solution)/shard_map/ppermute | solution.py:328
  8.7 1.5 %collective-permute-start.3 = (bf16[128,768]{1,0:T(8,128)(2,1)S(1)}, bf16[128,768]{1,0:T(8,128)(2,1)S(1)}, u32[]{:S(2)}, u32[]{:S(2)}) collective-permute-start(bf16[128,768]{1,0:T(8,128)(2,1)S(1)} %get-tuple-element.45.refs_0_), channel_id=1, source_target_pairs={{0,2},{1,3},{2,0},{3,1},{4,6},{5,7},{6,4},{7,5},{8,10},{9,11},{10,... | collective-permute-start | bytes 589832 | tf_op jit(solution)/shard_map/ppermute | solution.py:328
  12.8 2.5 %collective-permute-done.1.refs_4_.refs_0_ = bf16[128,768]{1,0:T(8,128)(2,1)S(1)} collective-permute-done((bf16[128,768]{1,0:T(8,128)(2,1)S(1)}, bf16[128,768]{1,0:T(8,128)(2,1)S(1)}, u32[]{:S(2)}, u32[]{:S(2)}) %collective-permute-start.1) | collective-permute-done | bytes 196640 | tf_op jit(solution)/shard_map/ppermute | solution.py:328
  15.4 2.5 %collective-permute-done.2.refs_0_ = bf16[128,768]{1,0:T(8,128)(2,1)S(1)} collective-permute-done((bf16[128,768]{1,0:T(8,128)(2,1)S(1)}, bf16[128,768]{1,0:T(8,128)(2,1)S(1)}, u32[]{:S(2)}, u32[]{:S(2)}) %collective-permute-start.2) | collective-permute-done | bytes 196640 | tf_op jit(solution)/shard_map/ppermute | solution.py:328
  19.4 1.5 %collective-permute-start.7 = (bf16[128,768]{1,0:T(8,128)(2,1)S(1)}, bf16[128,768]{1,0:T(8,128)(2,1)S(1)}, u32[]{:S(2)}, u32[]{:S(2)}) collective-permute-start(bf16[128,768]{1,0:T(8,128)(2,1)S(1)} %get-tuple-element.55), channel_id=1, source_target_pairs={{0,2},{1,3},{2,0},{3,1},{4,6},{5,7},{6,4},{7,5},{8,10},{9,11},{10,... | collective-permute-start | bytes 589832 | tf_op jit(solution)/shard_map/ppermute | solution.py:328
  21.5 1.8 %collective-permute-start.9 = (bf16[128,768]{1,0:T(8,128)(2,1)S(1)}, bf16[128,768]{1,0:T(8,128)(2,1)S(1)}, u32[]{:S(2)}, u32[]{:S(2)}) collective-permute-start(bf16[128,768]{1,0:T(8,128)(2,1)S(1)} %get-tuple-element.57), channel_id=1, source_target_pairs={{0,8},{1,9},{2,10},{3,11},{4,12},{5,13},{6,14},{7,15},{8,0},{9,1},... | collective-permute-start | bytes 589832 | tf_op jit(solution)/shard_map/ppermute | solution.py:328
  24.2 3.0 %collective-permute-done.7.refs_0_ = bf16[128,768]{1,0:T(8,128)(2,1)S(1)} collective-permute-done((bf16[128,768]{1,0:T(8,128)(2,1)S(1)}, bf16[128,768]{1,0:T(8,128)(2,1)S(1)}, u32[]{:S(2)}, u32[]{:S(2)}) %collective-permute-start.7) | collective-permute-done | bytes 196640 | tf_op jit(solution)/shard_map/ppermute | solution.py:328
  27.7 1.6 %collective-permute-done.5.refs_3_ = bf16[128,768]{1,0:T(8,128)(2,1)S(1)} collective-permute-done((bf16[128,768]{1,0:T(8,128)(2,1)S(1)}, bf16[128,768]{1,0:T(8,128)(2,1)S(1)}, u32[]{:S(2)}, u32[]{:S(2)}) %collective-permute-start.5) | collective-permute-done | bytes 196640 | tf_op jit(solution)/shard_map/ppermute | solution.py:328
  30.8 1.6 %collective-permute-start.15 = (bf16[128,512]{1,0:T(8,128)(2,1)S(1)}, bf16[128,512]{1,0:T(8,128)(2,1)S(1)}, u32[]{:S(2)}, u32[]{:S(2)}) collective-permute-start(bf16[128,512]{1,0:T(8,128)(2,1)S(1)} %get-tuple-element.67), channel_id=1, source_target_pairs={{0,2},{1,3},{2,0},{3,1},{4,6},{5,7},{6,4},{7,5},{8,10},{9,11},{10,... | collective-permute-start | bytes 393224 | tf_op jit(solution)/shard_map/ppermute | solution.py:328
  33.0 1.6 %collective-permute-start.12 = (bf16[128,768]{1,0:T(8,128)(2,1)S(1)}, bf16[128,768]{1,0:T(8,128)(2,1)S(1)}, u32[]{:S(2)}, u32[]{:S(2)}) collective-permute-start(bf16[128,768]{1,0:T(8,128)(2,1)S(1)} %get-tuple-element.63), channel_id=1, source_target_pairs={{0,2},{1,3},{2,0},{3,1},{4,6},{5,7},{6,4},{7,5},{8,10},{9,11},{10,... | collective-permute-start | bytes 589832 | tf_op jit(solution)/shard_map/ppermute | solution.py:328
  35.0 2.2 %collective-permute-done.15.refs_3_ = bf16[128,512]{1,0:T(8,128)(2,1)S(1)} collective-permute-done((bf16[128,512]{1,0:T(8,128)(2,1)S(1)}, bf16[128,512]{1,0:T(8,128)(2,1)S(1)}, u32[]{:S(2)}, u32[]{:S(2)}) %collective-permute-start.15) | collective-permute-done | bytes 131104 | tf_op jit(solution)/shard_map/ppermute | solution.py:328
  38.7 2.6 %attention.4.refs_2_.refs_0_ = bf16[512,256]{1,0:T(8,128)(2,1)S(1)} custom-call(bf16[512,1024]{1,0:T(8,128)(2,1)S(1)} %collective-permute-done.14.normed, bf16[1024,768]{1,0:T(8,128)(2,1)S(1)} %constant_dynamic-update-slice_fusion.weight, bf16[8,128]{1,0:T(8,128)(2,1)S(1)} %get-tuple-element.65.refs_0_.refs_1_), custom_call_target="tpu_custom_call" | custom-call | flops 939524096 | bytes 3670016 | tf_op jit(solution)/shard_map/attention/pallas_call | solution.py:182
  41.5 3.3 %collective-permute-done.11.refs_0_ = bf16[128,512]{1,0:T(8,128)(2,1)S(1)} collective-permute-done((bf16[128,512]{1,0:T(8,128)(2,1)S(1)}, bf16[128,512]{1,0:T(8,128)(2,1)S(1)}, u32[]{:S(2)}, u32[]{:S(2)}) %collective-permute-start.11) | collective-permute-done | bytes 131104 | tf_op jit(solution)/shard_map/ppermute | solution.py:328
  46.9 2.0 %collective-permute-start.18 = (bf16[128,768]{1,0:T(8,128)(2,1)S(1)}, bf16[128,768]{1,0:T(8,128)(2,1)S(1)}, u32[]{:S(2)}, u32[]{:S(2)}) collective-permute-start(bf16[128,768]{1,0:T(8,128)(2,1)S(1)} %get-tuple-element.73), channel_id=1, source_target_pairs={{0,16},{1,17},{2,18},{3,19},{4,20},{5,21},{6,22},{7,23},{8,24},{9,... | collective-permute-start | bytes 589832 | tf_op jit(solution)/shard_map/ppermute | solution.py:328
  48.9 2.6 %attention.5.refs_3_.refs_2_ = bf16[512,256]{1,0:T(8,128)(2,1)S(1)} custom-call(bf16[512,1024]{1,0:T(8,128)(2,1)S(1)} %get-tuple-element.53.normed, bf16[1024,768]{1,0:T(8,128)(2,1)S(1)} %constant_dynamic-update-slice_fusion.weight, bf16[8,128]{1,0:T(8,128)(2,1)S(1)} %get-tuple-element.71.refs_0_.refs_1_), custom_call_target="tpu_custom_call" | custom-call | flops 939524096 | bytes 3670016 | tf_op jit(solution)/shard_map/attention/pallas_call | solution.py:182
  51.6 1.8 %collective-permute-done.17.refs_2_ = bf16[128,768]{1,0:T(8,128)(2,1)S(1)} collective-permute-done((bf16[128,768]{1,0:T(8,128)(2,1)S(1)}, bf16[128,768]{1,0:T(8,128)(2,1)S(1)}, u32[]{:S(2)}, u32[]{:S(2)}) %collective-permute-start.17) | collective-permute-done | bytes 196640 | tf_op jit(solution)/shard_map/ppermute | solution.py:328
  55.8 2.6 %attention.6.refs_0_ = bf16[512,256]{1,0:T(8,128)(2,1)S(1)} custom-call(bf16[512,1024]{1,0:T(8,128)(2,1)S(1)} %collective-permute-done.14.normed, bf16[1024,768]{1,0:T(8,128)(2,1)S(1)} %constant_dynamic-update-slice_fusion.8.weight, bf16[8,128]{1,0:T(8,128)(2,1)S(1)} %get-tuple-element.78.refs_0_), custom_call_target="tpu_custom_call" | custom-call | flops 939524096 | bytes 3670016 | tf_op jit(solution)/shard_map/attention/pallas_call | solution.py:182
  59.8 2.7 %attention.7.refs_3_ = bf16[512,256]{1,0:T(8,128)(2,1)S(1)} custom-call(bf16[512,1024]{1,0:T(8,128)(2,1)S(1)} %get-tuple-element.53.normed, bf16[1024,768]{1,0:T(8,128)(2,1)S(1)} %constant_dynamic-update-slice_fusion.8.weight, bf16[512,256]{1,0:T(8,128)(2,1)S(1)} %attention.6.refs_0_), custom_call_target="tpu_custom_call" | custom-call | flops 939524096 | bytes 3670016 | tf_op jit(solution)/shard_map/attention/pallas_call | solution.py:182
  62.7 4.3 %router.1 = (f32[512,1024]{1,0:T(8,128)S(1)}, bf16[2,32,256]{2,1,0:T(8,128)(2,1)S(1)}, bf16[2,32,1024]{2,1,0:T(8,128)(2,1)S(1)}) custom-call(bf16[512,1024]{1,0:T(8,128)(2,1)S(1)} %bitcast.9, bf16[32,1024]{1,0:T(8,128)(2,1)S(1)} %bitcast.12, bf16[512,256]{1,0:T(8,128)(2,1)S(1)} %attention.5.refs_3_.refs_2_, bf16[512,256]{1,0:T(8,128)(2,1)S(1)} %attention.7.refs_3_, ...), custom_call_target="tpu_custom_call" | custom-call | flops 1140850688 | bytes 6291456 | tf_op jit(solution)/shard_map/router/pallas_call | solution.py:250
  67.1 11.5 %all_to_all.10 = bf16[2,32,1024]{2,0,1:T(2,128)(2,1)S(1)} all-to-all(bf16[2,32,1024]{2,0,1:T(2,128)(2,1)S(1)} %copy.9), channel_id=1, replica_groups=mesh['group'=2,'expert'=16] {'expert'}, dimensions={1} | all-to-all | bytes 262144 | tf_op jit(solution)/shard_map/all_to_all | solution.py:450
  78.6 2.1 %experts.1 = bf16[1,64,1024]{2,1,0:T(8,128)(2,1)S(1)} custom-call(bf16[1,64,1024]{2,1,0:T(8,128)(2,1)S(1)} %bitcast.10, bf16[1,1024,2048]{2,1,0:T(8,128)(2,1)S(1)} %copy-done, bf16[1,2048,1024]{2,1,0:T(8,128)(2,1)S(1)} %copy-done.1), custom_call_target="tpu_custom_call" | custom-call | flops 536870912 | bytes 8388608 | tf_op jit(solution)/shard_map/experts/pallas_call | solution.py:296
  80.9 10.5 %all_to_all.11 = bf16[2,32,1024]{2,0,1:T(2,128)(2,1)S(1)} all-to-all(bf16[2,32,1024]{2,0,1:T(2,128)(2,1)S(1)} %copy.11), channel_id=1, replica_groups=mesh['group'=2,'expert'=16] {'expert'}, dimensions={1} | all-to-all | bytes 262144 | tf_op jit(solution)/shard_map/all_to_all | solution.py:456
  (100 shorter events, 19.7 us)
Async XLA Ops:
  3.1 12.3 %collective-permute-start.1 = (bf16[128,768]{1,0:T(8,128)(2,1)S(1)}, bf16[128,768]{1,0:T(8,128)(2,1)S(1)}, u32[]{:S(2)}, u32[]{:S(2)}) collective-permute-start(bf16[128,768]{1,0:T(8,128)(2,1)S(1)} %get-tuple-element.45.refs_0_), channel_id=1, source_target_pairs={{0,4},{1,5},{2,6},{3,7},{4,0},{5,1},{6,2},{7,3},{8,12},{9,13},{10,... | collective-permute-start | bytes 589832 | tf_op jit(solution)/shard_map/ppermute | solution.py:328
  6.1 11.8 %collective-permute-start.2 = (bf16[128,768]{1,0:T(8,128)(2,1)S(1)}, bf16[128,768]{1,0:T(8,128)(2,1)S(1)}, u32[]{:S(2)}, u32[]{:S(2)}) collective-permute-start(bf16[128,768]{1,0:T(8,128)(2,1)S(1)} %get-tuple-element.45.refs_0_), channel_id=1, source_target_pairs={{0,8},{1,9},{2,10},{3,11},{4,12},{5,13},{6,14},{7,15},{8,0},{9,1},... | collective-permute-start | bytes 589832 | tf_op jit(solution)/shard_map/ppermute | solution.py:328
  8.7 9.2 %collective-permute-start.3 = (bf16[128,768]{1,0:T(8,128)(2,1)S(1)}, bf16[128,768]{1,0:T(8,128)(2,1)S(1)}, u32[]{:S(2)}, u32[]{:S(2)}) collective-permute-start(bf16[128,768]{1,0:T(8,128)(2,1)S(1)} %get-tuple-element.45.refs_0_), channel_id=1, source_target_pairs={{0,2},{1,3},{2,0},{3,1},{4,6},{5,7},{6,4},{7,5},{8,10},{9,11},{10,... | collective-permute-start | bytes 589832 | tf_op jit(solution)/shard_map/ppermute | solution.py:328
  12.2 8.7 %collective-permute-start.4 = (bf16[128,768]{1,0:T(8,128)(2,1)S(1)}, bf16[128,768]{1,0:T(8,128)(2,1)S(1)}, u32[]{:S(2)}, u32[]{:S(2)}) collective-permute-start(bf16[128,768]{1,0:T(8,128)(2,1)S(1)} %get-tuple-element.51), channel_id=1, source_target_pairs={{0,2},{1,3},{2,0},{3,1},{4,6},{5,7},{6,4},{7,5},{8,10},{9,11},{10,... | collective-permute-start | bytes 589832 | tf_op jit(solution)/shard_map/ppermute | solution.py:328
  17.9 11.5 %collective-permute-start.6 = (bf16[128,768]{1,0:T(8,128)(2,1)S(1)}, bf16[128,768]{1,0:T(8,128)(2,1)S(1)}, u32[]{:S(2)}, u32[]{:S(2)}) collective-permute-start(bf16[128,768]{1,0:T(8,128)(2,1)S(1)} %get-tuple-element.55), channel_id=1, source_target_pairs={{0,16},{1,17},{2,18},{3,19},{4,20},{5,21},{6,22},{7,23},{8,24},{9,... | collective-permute-start | bytes 589832 | tf_op jit(solution)/shard_map/ppermute | solution.py:328
  19.4 7.8 %collective-permute-start.7 = (bf16[128,768]{1,0:T(8,128)(2,1)S(1)}, bf16[128,768]{1,0:T(8,128)(2,1)S(1)}, u32[]{:S(2)}, u32[]{:S(2)}) collective-permute-start(bf16[128,768]{1,0:T(8,128)(2,1)S(1)} %get-tuple-element.55), channel_id=1, source_target_pairs={{0,2},{1,3},{2,0},{3,1},{4,6},{5,7},{6,4},{7,5},{8,10},{9,11},{10,... | collective-permute-start | bytes 589832 | tf_op jit(solution)/shard_map/ppermute | solution.py:328
  20.9 8.4 %collective-permute-start.5 = (bf16[128,768]{1,0:T(8,128)(2,1)S(1)}, bf16[128,768]{1,0:T(8,128)(2,1)S(1)}, u32[]{:S(2)}, u32[]{:S(2)}) collective-permute-start(bf16[128,768]{1,0:T(8,128)(2,1)S(1)} %get-tuple-element.54), channel_id=1, source_target_pairs={{0,2},{1,3},{2,0},{3,1},{4,6},{5,7},{6,4},{7,5},{8,10},{9,11},{10,... | collective-permute-start | bytes 589832 | tf_op jit(solution)/shard_map/ppermute | solution.py:328
  21.5 10.9 %collective-permute-start.9 = (bf16[128,768]{1,0:T(8,128)(2,1)S(1)}, bf16[128,768]{1,0:T(8,128)(2,1)S(1)}, u32[]{:S(2)}, u32[]{:S(2)}) collective-permute-start(bf16[128,768]{1,0:T(8,128)(2,1)S(1)} %get-tuple-element.57), channel_id=1, source_target_pairs={{0,8},{1,9},{2,10},{3,11},{4,12},{5,13},{6,14},{7,15},{8,0},{9,1},... | collective-permute-start | bytes 589832 | tf_op jit(solution)/shard_map/ppermute | solution.py:328
  24.0 14.6 %collective-permute-start.14 = (bf16[512,1024]{1,0:T(8,128)(2,1)S(1)}, bf16[512,1024]{1,0:T(8,128)(2,1)S(1)}, u32[]{:S(2)}, u32[]{:S(2)}) collective-permute-start(bf16[512,1024]{1,0:T(8,128)(2,1)S(1)} %get-tuple-element.66), channel_id=1, source_target_pairs={{0,1},{1,0},{2,3},{3,2},{4,5},{5,4},{6,7},{7,6},{8,9},{9,8},{10,11... | collective-permute-start | bytes 3145736 | tf_op jit(solution)/shard_map/ppermute | solution.py:328
  27.2 5.7 %collective-permute-start.8 = (bf16[128,768]{1,0:T(8,128)(2,1)S(1)}, bf16[128,768]{1,0:T(8,128)(2,1)S(1)}, u32[]{:S(2)}, u32[]{:S(2)}) collective-permute-start(bf16[128,768]{1,0:T(8,128)(2,1)S(1)} %get-tuple-element.56), channel_id=1, source_target_pairs={{0,16},{1,17},{2,18},{3,19},{4,20},{5,21},{6,22},{7,23},{8,24},{9,... | collective-permute-start | bytes 589832 | tf_op jit(solution)/shard_map/ppermute | solution.py:328
  30.8 6.4 %collective-permute-start.15 = (bf16[128,512]{1,0:T(8,128)(2,1)S(1)}, bf16[128,512]{1,0:T(8,128)(2,1)S(1)}, u32[]{:S(2)}, u32[]{:S(2)}) collective-permute-start(bf16[128,512]{1,0:T(8,128)(2,1)S(1)} %get-tuple-element.67), channel_id=1, source_target_pairs={{0,2},{1,3},{2,0},{3,1},{4,6},{5,7},{6,4},{7,5},{8,10},{9,11},{10,... | collective-permute-start | bytes 393224 | tf_op jit(solution)/shard_map/ppermute | solution.py:328
  32.4 8.9 %collective-permute-start.13 = (bf16[128,768]{1,0:T(8,128)(2,1)S(1)}, bf16[128,768]{1,0:T(8,128)(2,1)S(1)}, u32[]{:S(2)}, u32[]{:S(2)}) collective-permute-start(bf16[128,768]{1,0:T(8,128)(2,1)S(1)} %get-tuple-element.64), channel_id=1, source_target_pairs={{0,4},{1,5},{2,6},{3,7},{4,0},{5,1},{6,2},{7,3},{8,12},{9,13},{10,... | collective-permute-start | bytes 589832 | tf_op jit(solution)/shard_map/ppermute | solution.py:328
  33.0 8.3 %collective-permute-start.12 = (bf16[128,768]{1,0:T(8,128)(2,1)S(1)}, bf16[128,768]{1,0:T(8,128)(2,1)S(1)}, u32[]{:S(2)}, u32[]{:S(2)}) collective-permute-start(bf16[128,768]{1,0:T(8,128)(2,1)S(1)} %get-tuple-element.63), channel_id=1, source_target_pairs={{0,2},{1,3},{2,0},{3,1},{4,6},{5,7},{6,4},{7,5},{8,10},{9,11},{10,... | collective-permute-start | bytes 589832 | tf_op jit(solution)/shard_map/ppermute | solution.py:328
  34.6 6.7 %collective-permute-start.16 = (bf16[128,768]{1,0:T(8,128)(2,1)S(1)}, bf16[128,768]{1,0:T(8,128)(2,1)S(1)}, u32[]{:S(2)}, u32[]{:S(2)}) collective-permute-start(bf16[128,768]{1,0:T(8,128)(2,1)S(1)} %get-tuple-element.63), channel_id=1, source_target_pairs={{0,16},{1,17},{2,18},{3,19},{4,20},{5,21},{6,22},{7,23},{8,24},{9,... | collective-permute-start | bytes 589832 | tf_op jit(solution)/shard_map/ppermute | solution.py:328
  37.2 7.6 %collective-permute-start.11 = (bf16[128,512]{1,0:T(8,128)(2,1)S(1)}, bf16[128,512]{1,0:T(8,128)(2,1)S(1)}, u32[]{:S(2)}, u32[]{:S(2)}) collective-permute-start(bf16[128,512]{1,0:T(8,128)(2,1)S(1)} %get-tuple-element.62), channel_id=1, source_target_pairs={{0,8},{1,9},{2,10},{3,11},{4,12},{5,13},{6,14},{7,15},{8,0},{9,1},... | collective-permute-start | bytes 393224 | tf_op jit(solution)/shard_map/ppermute | solution.py:328
  41.4 10.1 %collective-permute-start.20 = (bf16[128,512]{1,0:T(8,128)(2,1)S(1)}, bf16[128,512]{1,0:T(8,128)(2,1)S(1)}, u32[]{:S(2)}, u32[]{:S(2)}) collective-permute-start(bf16[128,512]{1,0:T(8,128)(2,1)S(1)} %get-tuple-element.75), channel_id=1, source_target_pairs={{0,4},{1,5},{2,6},{3,7},{4,0},{5,1},{6,2},{7,3},{8,12},{9,13},{10,... | collective-permute-start | bytes 393224 | tf_op jit(solution)/shard_map/ppermute | solution.py:328
  44.8 6.7 %collective-permute-start.19 = (bf16[128,512]{1,0:T(8,128)(2,1)S(1)}, bf16[128,512]{1,0:T(8,128)(2,1)S(1)}, u32[]{:S(2)}, u32[]{:S(2)}) collective-permute-start(bf16[128,512]{1,0:T(8,128)(2,1)S(1)} %get-tuple-element.74), channel_id=1, source_target_pairs={{0,2},{1,3},{2,0},{3,1},{4,6},{5,7},{6,4},{7,5},{8,10},{9,11},{10,... | collective-permute-start | bytes 393224 | tf_op jit(solution)/shard_map/ppermute | solution.py:328
  46.0 12.4 %collective-permute-start.24 = (bf16[128,512]{1,0:T(8,128)(2,1)S(1)}, bf16[128,512]{1,0:T(8,128)(2,1)S(1)}, u32[]{:S(2)}, u32[]{:S(2)}) collective-permute-start(bf16[128,512]{1,0:T(8,128)(2,1)S(1)} %get-tuple-element.74), channel_id=1, source_target_pairs={{0,16},{1,17},{2,18},{3,19},{4,20},{5,21},{6,22},{7,23},{8,24},{9,... | collective-permute-start | bytes 393224 | tf_op jit(solution)/shard_map/ppermute | solution.py:328
  46.4 7.0 %collective-permute-start.17 = (bf16[128,768]{1,0:T(8,128)(2,1)S(1)}, bf16[128,768]{1,0:T(8,128)(2,1)S(1)}, u32[]{:S(2)}, u32[]{:S(2)}) collective-permute-start(bf16[128,768]{1,0:T(8,128)(2,1)S(1)} %get-tuple-element.72), channel_id=1, source_target_pairs={{0,2},{1,3},{2,0},{3,1},{4,6},{5,7},{6,4},{7,5},{8,10},{9,11},{10,... | collective-permute-start | bytes 589832 | tf_op jit(solution)/shard_map/ppermute | solution.py:328
  46.9 8.8 %collective-permute-start.18 = (bf16[128,768]{1,0:T(8,128)(2,1)S(1)}, bf16[128,768]{1,0:T(8,128)(2,1)S(1)}, u32[]{:S(2)}, u32[]{:S(2)}) collective-permute-start(bf16[128,768]{1,0:T(8,128)(2,1)S(1)} %get-tuple-element.73), channel_id=1, source_target_pairs={{0,16},{1,17},{2,18},{3,19},{4,20},{5,21},{6,22},{7,23},{8,24},{9,... | collective-permute-start | bytes 589832 | tf_op jit(solution)/shard_map/ppermute | solution.py:328
  51.6 11.1 %collective-permute-start.26 = (bf16[640,512]{1,0:T(8,128)(2,1)S(1)}, bf16[640,512]{1,0:T(8,128)(2,1)S(1)}, u32[]{:S(2)}, u32[]{:S(2)}) collective-permute-start(bf16[640,512]{1,0:T(8,128)(2,1)S(1)} %constant_dynamic-update-slice_fusion.16.refs_6_), channel_id=1, source_target_pairs={{0,1},{1,0},{2,3},{3,2},{4,5},{5,4},{6,7},{7,6},{8,9},{9,8},{10,11... | collective-permute-start | bytes 1966088 | tf_op jit(solution)/shard_map/ppermute | solution.py:328
  53.4 5.0 %collective-permute-start.25 = (bf16[128,512]{1,0:T(8,128)(2,1)S(1)}, bf16[128,512]{1,0:T(8,128)(2,1)S(1)}, u32[]{:S(2)}, u32[]{:S(2)}) collective-permute-start(bf16[128,512]{1,0:T(8,128)(2,1)S(1)} %get-tuple-element.81), channel_id=1, source_target_pairs={{0,16},{1,17},{2,18},{3,19},{4,20},{5,21},{6,22},{7,23},{8,24},{9,... | collective-permute-start | bytes 393224 | tf_op jit(solution)/shard_map/ppermute | solution.py:328
  54.2 5.0 %collective-permute-start.23 = (bf16[128,512]{1,0:T(8,128)(2,1)S(1)}, bf16[128,512]{1,0:T(8,128)(2,1)S(1)}, u32[]{:S(2)}, u32[]{:S(2)}) collective-permute-start(bf16[128,512]{1,0:T(8,128)(2,1)S(1)} %get-tuple-element.80), channel_id=1, source_target_pairs={{0,2},{1,3},{2,0},{3,1},{4,6},{5,7},{6,4},{7,5},{8,10},{9,11},{10,... | collective-permute-start | bytes 393224 | tf_op jit(solution)/shard_map/ppermute | solution.py:328
  59.2 3.4 %collective-permute-start.27 = (bf16[400,512]{1,0:T(8,128)(2,1)S(1)}, bf16[400,512]{1,0:T(8,128)(2,1)S(1)}, u32[]{:S(2)}, u32[]{:S(2)}) collective-permute-start(bf16[400,512]{1,0:T(8,128)(2,1)S(1)} %maximum_maximum_fusion.refs_7_), channel_id=1, source_target_pairs={{0,1},{1,0},{2,3},{3,2},{4,5},{5,4},{6,7},{7,6},{8,9},{9,8},{10,11... | collective-permute-start | bytes 1228808 | tf_op jit(solution)/shard_map/ppermute | solution.py:328
  (11 other events, 65.4 us)

commit v5 on v4

--- a/solution.py
+++ b/solution.py
@@ -372,9 +372,8 @@
     a_x_far = over_x(a_y_far_1)
     (w_out,) = step(w_attn_out)
     (c,) = split(split_out_kernel, w_out, in_chip(w_out), 1, 2 * span)
-    b_3, c_1 = step(b, c, done=(a_x,))
+    (b_3,) = step(b, done=(a_x,))
     b_near = near_z(b_3)
-    c_y = over_y(c_1)
     normed_other = in_chip(normed_sent)
     b_far_1, c_2 = step(b_far, c, done=(a_y_near, a_x_far))
     b_x = over_x(b_far_1)
@@ -382,12 +381,13 @@
     c_far = far_z(c_2)
     a_all = whole(a, a_y, a_near, a_y_near, a_far, a_x, a_y_far, a_x_far)
     other_a = attention(normed_other, a_all, length, head, (token,))
-    (b_near_1,) = step(b_near, done=(other_a, c_y))
+    (b_near_1,) = step(b_near, done=(other_a,))
     b_y_near = over_y(b_near_1)
     (b_y_far_1,) = step(b_y_far)
     b_x_far = over_x(b_y_far_1)
     (c_3,) = step(c, done=(b_x,))
     c_near = near_z(c_3)
+    c_y = over_y(c_3)
     (c_far_1,) = step(c_far)
     c_y_far = over_y(c_far_1)
     c_x = over_x(c_far_1)

time: 93.4 us -> 92 us (0.985)
  starting transfers between devices: 26.2 us -> 25 us
  blocking collectives: 22 us -> 21 us
    ppermute x28, starting transfers between devices: 26.2 us -> 25 us  [send(): return lax.ppermute(value, AXES, pairs)]
    all_to_all x1, blocking collectives: 11.5 us -> 10.5 us  [on_device(): lax.all_to_all(slot_inputs, 'expert', split_axis=1, concat_axis=1, tiled=...]
  transfers between devices with their start and end apart: 28 -> 28, of which waited for: 12 -> 11; matrix products, arithmetic and copies ran while one was open for 0% -> 0% of each run, Pallas kernels for 13% -> 13%
where the time goes in v5:
time: 92 us; the launch traced here: 91.8 us
  starting transfers between devices  25 us (27%)
  waiting for transfers between devices  21.8 us (24%)
  blocking collectives  21 us (23%)
  Pallas kernels  18.8 us (20%)
  local copies, waits for them, and re-layouts  2.84 us (3%)
  other arithmetic  1.3 us (1%)
    ppermute x28, starting transfers between devices, send(): return lax.ppermute(value, AXES, pairs)  25 us
    ppermute x28, waiting for transfers between devices, send(): return lax.ppermute(value, AXES, pairs)  21.8 us
    all_to_all x1, blocking collectives, on_device(): lax.all_to_all(slot_inputs, 'expert', split_axis=1, concat_axis=1, tiled=...  10.5 us
    all_to_all x1, blocking collectives, on_device(): lax.all_to_all(answered, 'expert', split_axis=1, concat_axis=1, tiled=True)  10.5 us
    pallas_call x4, Pallas kernels, attention(): pl.pallas_call(functools.partial(attention_kernel, length, head), out_sha...  10.4 us
    pallas_call x1, Pallas kernels, router(): pl.pallas_call(functools.partial(router_kernel, count, images, length), o...  4.29 us
    unnamed x31, local copies, waits for them, and re-layouts  2.49 us
    pallas_call x1, Pallas kernels, experts_here(): pl.pallas_call(expert_kernel, out_shape=jax.ShapeDtypeStruct(inputs.shape...  2.11 us
  transfers between devices with their start and end apart: 28, of which 11 were waited for; matrix products, arithmetic and copies ran while one was open for 0% of the time, Pallas kernels for 13%

profile of v5, /device:TPU:0, one launch (start us, length us, event | category | flops | bytes accessed | tf_op | source)
XLA Modules:
  0.0 91.8 jit_solution(7492839211250961644)
XLA Ops:
  0.5 1.6 %collective-permute-done.other_ref = bf16[64,3072]{1,0:T(8,128)(2,1)S(1)} collective-permute-done((bf16[64,3072]{1,0:T(8,128)(2,1)}, bf16[64,3072]{1,0:T(8,128)(2,1)S(1)}, u32[]{:S(2)}, u32[]{:S(2)}) %collective-permute-start) | collective-permute-done | bytes 393248 | tf_op jit(solution)/shard_map/ppermute | solution.py:328
  3.1 3.0 %collective-permute-start.1 = (bf16[128,768]{1,0:T(8,128)(2,1)S(1)}, bf16[128,768]{1,0:T(8,128)(2,1)S(1)}, u32[]{:S(2)}, u32[]{:S(2)}) collective-permute-start(bf16[128,768]{1,0:T(8,128)(2,1)S(1)} %get-tuple-element.44.refs_0_), channel_id=1, source_target_pairs={{0,4},{1,5},{2,6},{3,7},{4,0},{5,1},{6,2},{7,3},{8,12},{9,13},{10,... | collective-permute-start | bytes 589832 | tf_op jit(solution)/shard_map/ppermute | solution.py:328
  6.1 2.6 %collective-permute-start.2 = (bf16[128,768]{1,0:T(8,128)(2,1)S(1)}, bf16[128,768]{1,0:T(8,128)(2,1)S(1)}, u32[]{:S(2)}, u32[]{:S(2)}) collective-permute-start(bf16[128,768]{1,0:T(8,128)(2,1)S(1)} %get-tuple-element.44.refs_0_), channel_id=1, source_target_pairs={{0,8},{1,9},{2,10},{3,11},{4,12},{5,13},{6,14},{7,15},{8,0},{9,1},... | collective-permute-start | bytes 589832 | tf_op jit(solution)/shard_map/ppermute | solution.py:328
  8.7 1.5 %collective-permute-start.3 = (bf16[128,768]{1,0:T(8,128)(2,1)S(1)}, bf16[128,768]{1,0:T(8,128)(2,1)S(1)}, u32[]{:S(2)}, u32[]{:S(2)}) collective-permute-start(bf16[128,768]{1,0:T(8,128)(2,1)S(1)} %get-tuple-element.44.refs_0_), channel_id=1, source_target_pairs={{0,2},{1,3},{2,0},{3,1},{4,6},{5,7},{6,4},{7,5},{8,10},{9,11},{10,... | collective-permute-start | bytes 589832 | tf_op jit(solution)/shard_map/ppermute | solution.py:328
  12.9 2.5 %collective-permute-done.1.refs_4_.refs_0_ = bf16[128,768]{1,0:T(8,128)(2,1)S(1)} collective-permute-done((bf16[128,768]{1,0:T(8,128)(2,1)S(1)}, bf16[128,768]{1,0:T(8,128)(2,1)S(1)}, u32[]{:S(2)}, u32[]{:S(2)}) %collective-permute-start.1) | collective-permute-done | bytes 196640 | tf_op jit(solution)/shard_map/ppermute | solution.py:328
  15.4 2.5 %collective-permute-done.2.refs_0_ = bf16[128,768]{1,0:T(8,128)(2,1)S(1)} collective-permute-done((bf16[128,768]{1,0:T(8,128)(2,1)S(1)}, bf16[128,768]{1,0:T(8,128)(2,1)S(1)}, u32[]{:S(2)}, u32[]{:S(2)}) %collective-permute-start.2) | collective-permute-done | bytes 196640 | tf_op jit(solution)/shard_map/ppermute | solution.py:328
  19.4 1.5 %collective-permute-start.7 = (bf16[128,768]{1,0:T(8,128)(2,1)S(1)}, bf16[128,768]{1,0:T(8,128)(2,1)S(1)}, u32[]{:S(2)}, u32[]{:S(2)}) collective-permute-start(bf16[128,768]{1,0:T(8,128)(2,1)S(1)} %get-tuple-element.54), channel_id=1, source_target_pairs={{0,2},{1,3},{2,0},{3,1},{4,6},{5,7},{6,4},{7,5},{8,10},{9,11},{10,... | collective-permute-start | bytes 589832 | tf_op jit(solution)/shard_map/ppermute | solution.py:328
  21.5 1.8 %collective-permute-start.9 = (bf16[128,768]{1,0:T(8,128)(2,1)S(1)}, bf16[128,768]{1,0:T(8,128)(2,1)S(1)}, u32[]{:S(2)}, u32[]{:S(2)}) collective-permute-start(bf16[128,768]{1,0:T(8,128)(2,1)S(1)} %get-tuple-element.56), channel_id=1, source_target_pairs={{0,8},{1,9},{2,10},{3,11},{4,12},{5,13},{6,14},{7,15},{8,0},{9,1},... | collective-permute-start | bytes 589832 | tf_op jit(solution)/shard_map/ppermute | solution.py:328
  24.3 3.0 %collective-permute-done.7.refs_0_ = bf16[128,768]{1,0:T(8,128)(2,1)S(1)} collective-permute-done((bf16[128,768]{1,0:T(8,128)(2,1)S(1)}, bf16[128,768]{1,0:T(8,128)(2,1)S(1)}, u32[]{:S(2)}, u32[]{:S(2)}) %collective-permute-start.7) | collective-permute-done | bytes 196640 | tf_op jit(solution)/shard_map/ppermute | solution.py:328
  27.8 1.5 %collective-permute-done.5.refs_3_ = bf16[128,768]{1,0:T(8,128)(2,1)S(1)} collective-permute-done((bf16[128,768]{1,0:T(8,128)(2,1)S(1)}, bf16[128,768]{1,0:T(8,128)(2,1)S(1)}, u32[]{:S(2)}, u32[]{:S(2)}) %collective-permute-start.5) | collective-permute-done | bytes 196640 | tf_op jit(solution)/shard_map/ppermute | solution.py:328
  29.5 1.5 %collective-permute-done.9.refs_0_ = bf16[128,768]{1,0:T(8,128)(2,1)S(1)} collective-permute-done((bf16[128,768]{1,0:T(8,128)(2,1)S(1)}, bf16[128,768]{1,0:T(8,128)(2,1)S(1)}, u32[]{:S(2)}, u32[]{:S(2)}) %collective-permute-start.9) | collective-permute-done | bytes 196640 | tf_op jit(solution)/shard_map/ppermute | solution.py:328
  31.1 1.9 %collective-permute-done.8.refs_4_ = bf16[128,768]{1,0:T(8,128)(2,1)S(1)} collective-permute-done((bf16[128,768]{1,0:T(8,128)(2,1)S(1)}, bf16[128,768]{1,0:T(8,128)(2,1)S(1)}, u32[]{:S(2)}, u32[]{:S(2)}) %collective-permute-start.8) | collective-permute-done | bytes 196640 | tf_op jit(solution)/shard_map/ppermute | solution.py:328
  33.0 1.7 %collective-permute-start.12 = (bf16[128,768]{1,0:T(8,128)(2,1)S(1)}, bf16[128,768]{1,0:T(8,128)(2,1)S(1)}, u32[]{:S(2)}, u32[]{:S(2)}) collective-permute-start(bf16[128,768]{1,0:T(8,128)(2,1)S(1)} %get-tuple-element.62), channel_id=1, source_target_pairs={{0,2},{1,3},{2,0},{3,1},{4,6},{5,7},{6,4},{7,5},{8,10},{9,11},{10,... | collective-permute-start | bytes 589832 | tf_op jit(solution)/shard_map/ppermute | solution.py:328
  36.4 2.6 %attention.4.refs_2_.refs_0_ = bf16[512,256]{1,0:T(8,128)(2,1)S(1)} custom-call(bf16[512,1024]{1,0:T(8,128)(2,1)S(1)} %collective-permute-done.14.normed, bf16[1024,768]{1,0:T(8,128)(2,1)S(1)} %constant_dynamic-update-slice_fusion.weight, bf16[8,128]{1,0:T(8,128)(2,1)S(1)} %get-tuple-element.64.refs_0_.refs_1_), custom_call_target="tpu_custom_call" | custom-call | flops 939524096 | bytes 3670016 | tf_op jit(solution)/shard_map/attention/pallas_call | solution.py:182
  43.1 2.2 %collective-permute-start.24 = (bf16[128,512]{1,0:T(8,128)(2,1)S(1)}, bf16[128,512]{1,0:T(8,128)(2,1)S(1)}, u32[]{:S(2)}, u32[]{:S(2)}) collective-permute-start(bf16[128,512]{1,0:T(8,128)(2,1)S(1)} %get-tuple-element.72), channel_id=1, source_target_pairs={{0,16},{1,17},{2,18},{3,19},{4,20},{5,21},{6,22},{7,23},{8,24},{9,... | collective-permute-start | bytes 393224 | tf_op jit(solution)/shard_map/ppermute | solution.py:328
  46.3 2.6 %attention.5.refs_3_.refs_2_ = bf16[512,256]{1,0:T(8,128)(2,1)S(1)} custom-call(bf16[512,1024]{1,0:T(8,128)(2,1)S(1)} %get-tuple-element.52.normed, bf16[1024,768]{1,0:T(8,128)(2,1)S(1)} %constant_dynamic-update-slice_fusion.weight, bf16[8,128]{1,0:T(8,128)(2,1)S(1)} %get-tuple-element.69.refs_0_.refs_1_), custom_call_target="tpu_custom_call" | custom-call | flops 939524096 | bytes 3670016 | tf_op jit(solution)/shard_map/attention/pallas_call | solution.py:182
  49.2 1.7 %collective-permute-done.16.refs_2_ = bf16[128,768]{1,0:T(8,128)(2,1)S(1)} collective-permute-done((bf16[128,768]{1,0:T(8,128)(2,1)S(1)}, bf16[128,768]{1,0:T(8,128)(2,1)S(1)}, u32[]{:S(2)}, u32[]{:S(2)}) %collective-permute-start.16) | collective-permute-done | bytes 196640 | tf_op jit(solution)/shard_map/ppermute | solution.py:328
  52.5 3.5 %collective-permute-done.17.refs_2_ = bf16[128,768]{1,0:T(8,128)(2,1)S(1)} collective-permute-done((bf16[128,768]{1,0:T(8,128)(2,1)S(1)}, bf16[128,768]{1,0:T(8,128)(2,1)S(1)}, u32[]{:S(2)}, u32[]{:S(2)}) %collective-permute-start.17) | collective-permute-done | bytes 196640 | tf_op jit(solution)/shard_map/ppermute | solution.py:328
  56.1 2.6 %attention.6.refs_0_ = bf16[512,256]{1,0:T(8,128)(2,1)S(1)} custom-call(bf16[512,1024]{1,0:T(8,128)(2,1)S(1)} %collective-permute-done.14.normed, bf16[1024,768]{1,0:T(8,128)(2,1)S(1)} %constant_dynamic-update-slice_fusion.8.weight, bf16[8,128]{1,0:T(8,128)(2,1)S(1)} %get-tuple-element.76.refs_0_), custom_call_target="tpu_custom_call" | custom-call | flops 939524096 | bytes 3670016 | tf_op jit(solution)/shard_map/attention/pallas_call | solution.py:182
  59.4 2.7 %attention.7.refs_3_ = bf16[512,256]{1,0:T(8,128)(2,1)S(1)} custom-call(bf16[512,1024]{1,0:T(8,128)(2,1)S(1)} %get-tuple-element.52.normed, bf16[1024,768]{1,0:T(8,128)(2,1)S(1)} %constant_dynamic-update-slice_fusion.8.weight, bf16[512,256]{1,0:T(8,128)(2,1)S(1)} %attention.6.refs_0_), custom_call_target="tpu_custom_call" | custom-call | flops 939524096 | bytes 3670016 | tf_op jit(solution)/shard_map/attention/pallas_call | solution.py:182
  62.2 4.3 %router.1 = (f32[512,1024]{1,0:T(8,128)S(1)}, bf16[2,32,256]{2,1,0:T(8,128)(2,1)S(1)}, bf16[2,32,1024]{2,1,0:T(8,128)(2,1)S(1)}) custom-call(bf16[512,1024]{1,0:T(8,128)(2,1)S(1)} %bitcast.9, bf16[32,1024]{1,0:T(8,128)(2,1)S(1)} %bitcast.12, bf16[512,256]{1,0:T(8,128)(2,1)S(1)} %attention.5.refs_3_.refs_2_, bf16[512,256]{1,0:T(8,128)(2,1)S(1)} %attention.7.refs_3_, ...), custom_call_target="tpu_custom_call" | custom-call | flops 1140850688 | bytes 6291456 | tf_op jit(solution)/shard_map/router/pallas_call | solution.py:250
  66.7 10.5 %all_to_all.10 = bf16[2,32,1024]{2,0,1:T(2,128)(2,1)S(1)} all-to-all(bf16[2,32,1024]{2,0,1:T(2,128)(2,1)S(1)} %copy.9), channel_id=1, replica_groups=mesh['group'=2,'expert'=16] {'expert'}, dimensions={1} | all-to-all | bytes 262144 | tf_op jit(solution)/shard_map/all_to_all | solution.py:450
  77.2 2.1 %experts.1 = bf16[1,64,1024]{2,1,0:T(8,128)(2,1)S(1)} custom-call(bf16[1,64,1024]{2,1,0:T(8,128)(2,1)S(1)} %bitcast.10, bf16[1,1024,2048]{2,1,0:T(8,128)(2,1)S(1)} %copy-done, bf16[1,2048,1024]{2,1,0:T(8,128)(2,1)S(1)} %copy-done.1), custom_call_target="tpu_custom_call" | custom-call | flops 536870912 | bytes 8388608 | tf_op jit(solution)/shard_map/experts/pallas_call | solution.py:296
  79.5 10.5 %all_to_all.11 = bf16[2,32,1024]{2,0,1:T(2,128)(2,1)S(1)} all-to-all(bf16[2,32,1024]{2,0,1:T(2,128)(2,1)S(1)} %copy.11), channel_id=1, replica_groups=mesh['group'=2,'expert'=16] {'expert'}, dimensions={1} | all-to-all | bytes 262144 | tf_op jit(solution)/shard_map/all_to_all | solution.py:456
  (100 shorter events, 19.3 us)
Async XLA Ops:
  3.1 12.3 %collective-permute-start.1 = (bf16[128,768]{1,0:T(8,128)(2,1)S(1)}, bf16[128,768]{1,0:T(8,128)(2,1)S(1)}, u32[]{:S(2)}, u32[]{:S(2)}) collective-permute-start(bf16[128,768]{1,0:T(8,128)(2,1)S(1)} %get-tuple-element.44.refs_0_), channel_id=1, source_target_pairs={{0,4},{1,5},{2,6},{3,7},{4,0},{5,1},{6,2},{7,3},{8,12},{9,13},{10,... | collective-permute-start | bytes 589832 | tf_op jit(solution)/shard_map/ppermute | solution.py:328
  6.1 11.8 %collective-permute-start.2 = (bf16[128,768]{1,0:T(8,128)(2,1)S(1)}, bf16[128,768]{1,0:T(8,128)(2,1)S(1)}, u32[]{:S(2)}, u32[]{:S(2)}) collective-permute-start(bf16[128,768]{1,0:T(8,128)(2,1)S(1)} %get-tuple-element.44.refs_0_), channel_id=1, source_target_pairs={{0,8},{1,9},{2,10},{3,11},{4,12},{5,13},{6,14},{7,15},{8,0},{9,1},... | collective-permute-start | bytes 589832 | tf_op jit(solution)/shard_map/ppermute | solution.py:328
  8.7 9.2 %collective-permute-start.3 = (bf16[128,768]{1,0:T(8,128)(2,1)S(1)}, bf16[128,768]{1,0:T(8,128)(2,1)S(1)}, u32[]{:S(2)}, u32[]{:S(2)}) collective-permute-start(bf16[128,768]{1,0:T(8,128)(2,1)S(1)} %get-tuple-element.44.refs_0_), channel_id=1, source_target_pairs={{0,2},{1,3},{2,0},{3,1},{4,6},{5,7},{6,4},{7,5},{8,10},{9,11},{10,... | collective-permute-start | bytes 589832 | tf_op jit(solution)/shard_map/ppermute | solution.py:328
  12.3 8.6 %collective-permute-start.4 = (bf16[128,768]{1,0:T(8,128)(2,1)S(1)}, bf16[128,768]{1,0:T(8,128)(2,1)S(1)}, u32[]{:S(2)}, u32[]{:S(2)}) collective-permute-start(bf16[128,768]{1,0:T(8,128)(2,1)S(1)} %get-tuple-element.50), channel_id=1, source_target_pairs={{0,2},{1,3},{2,0},{3,1},{4,6},{5,7},{6,4},{7,5},{8,10},{9,11},{10,... | collective-permute-start | bytes 589832 | tf_op jit(solution)/shard_map/ppermute | solution.py:328
  17.9 9.8 %collective-permute-start.6 = (bf16[128,768]{1,0:T(8,128)(2,1)S(1)}, bf16[128,768]{1,0:T(8,128)(2,1)S(1)}, u32[]{:S(2)}, u32[]{:S(2)}) collective-permute-start(bf16[128,768]{1,0:T(8,128)(2,1)S(1)} %get-tuple-element.54), channel_id=1, source_target_pairs={{0,16},{1,17},{2,18},{3,19},{4,20},{5,21},{6,22},{7,23},{8,24},{9,... | collective-permute-start | bytes 589832 | tf_op jit(solution)/shard_map/ppermute | solution.py:328
  19.4 7.8 %collective-permute-start.7 = (bf16[128,768]{1,0:T(8,128)(2,1)S(1)}, bf16[128,768]{1,0:T(8,128)(2,1)S(1)}, u32[]{:S(2)}, u32[]{:S(2)}) collective-permute-start(bf16[128,768]{1,0:T(8,128)(2,1)S(1)} %get-tuple-element.54), channel_id=1, source_target_pairs={{0,2},{1,3},{2,0},{3,1},{4,6},{5,7},{6,4},{7,5},{8,10},{9,11},{10,... | collective-permute-start | bytes 589832 | tf_op jit(solution)/shard_map/ppermute | solution.py:328
  20.9 8.4 %collective-permute-start.5 = (bf16[128,768]{1,0:T(8,128)(2,1)S(1)}, bf16[128,768]{1,0:T(8,128)(2,1)S(1)}, u32[]{:S(2)}, u32[]{:S(2)}) collective-permute-start(bf16[128,768]{1,0:T(8,128)(2,1)S(1)} %get-tuple-element.53), channel_id=1, source_target_pairs={{0,2},{1,3},{2,0},{3,1},{4,6},{5,7},{6,4},{7,5},{8,10},{9,11},{10,... | collective-permute-start | bytes 589832 | tf_op jit(solution)/shard_map/ppermute | solution.py:328
  21.5 9.6 %collective-permute-start.9 = (bf16[128,768]{1,0:T(8,128)(2,1)S(1)}, bf16[128,768]{1,0:T(8,128)(2,1)S(1)}, u32[]{:S(2)}, u32[]{:S(2)}) collective-permute-start(bf16[128,768]{1,0:T(8,128)(2,1)S(1)} %get-tuple-element.56), channel_id=1, source_target_pairs={{0,8},{1,9},{2,10},{3,11},{4,12},{5,13},{6,14},{7,15},{8,0},{9,1},... | collective-permute-start | bytes 589832 | tf_op jit(solution)/shard_map/ppermute | solution.py:328
  24.1 12.3 %collective-permute-start.14 = (bf16[512,1024]{1,0:T(8,128)(2,1)S(1)}, bf16[512,1024]{1,0:T(8,128)(2,1)S(1)}, u32[]{:S(2)}, u32[]{:S(2)}) collective-permute-start(bf16[512,1024]{1,0:T(8,128)(2,1)S(1)} %get-tuple-element.65), channel_id=1, source_target_pairs={{0,1},{1,0},{2,3},{3,2},{4,5},{5,4},{6,7},{7,6},{8,9},{9,8},{10,11... | collective-permute-start | bytes 3145736 | tf_op jit(solution)/shard_map/ppermute | solution.py:328
  27.2 5.7 %collective-permute-start.8 = (bf16[128,768]{1,0:T(8,128)(2,1)S(1)}, bf16[128,768]{1,0:T(8,128)(2,1)S(1)}, u32[]{:S(2)}, u32[]{:S(2)}) collective-permute-start(bf16[128,768]{1,0:T(8,128)(2,1)S(1)} %get-tuple-element.55), channel_id=1, source_target_pairs={{0,16},{1,17},{2,18},{3,19},{4,20},{5,21},{6,22},{7,23},{8,24},{9,... | collective-permute-start | bytes 589832 | tf_op jit(solution)/shard_map/ppermute | solution.py:328
  29.4 9.7 %collective-permute-start.13 = (bf16[128,768]{1,0:T(8,128)(2,1)S(1)}, bf16[128,768]{1,0:T(8,128)(2,1)S(1)}, u32[]{:S(2)}, u32[]{:S(2)}) collective-permute-start(bf16[128,768]{1,0:T(8,128)(2,1)S(1)} %get-tuple-element.63), channel_id=1, source_target_pairs={{0,4},{1,5},{2,6},{3,7},{4,0},{5,1},{6,2},{7,3},{8,12},{9,13},{10,... | collective-permute-start | bytes 589832 | tf_op jit(solution)/shard_map/ppermute | solution.py:328
  33.0 6.1 %collective-permute-start.12 = (bf16[128,768]{1,0:T(8,128)(2,1)S(1)}, bf16[128,768]{1,0:T(8,128)(2,1)S(1)}, u32[]{:S(2)}, u32[]{:S(2)}) collective-permute-start(bf16[128,768]{1,0:T(8,128)(2,1)S(1)} %get-tuple-element.62), channel_id=1, source_target_pairs={{0,2},{1,3},{2,0},{3,1},{4,6},{5,7},{6,4},{7,5},{8,10},{9,11},{10,... | collective-permute-start | bytes 589832 | tf_op jit(solution)/shard_map/ppermute | solution.py:328
  34.7 5.7 %collective-permute-start.15 = (bf16[128,768]{1,0:T(8,128)(2,1)S(1)}, bf16[128,768]{1,0:T(8,128)(2,1)S(1)}, u32[]{:S(2)}, u32[]{:S(2)}) collective-permute-start(bf16[128,768]{1,0:T(8,128)(2,1)S(1)} %get-tuple-element.62), channel_id=1, source_target_pairs={{0,16},{1,17},{2,18},{3,19},{4,20},{5,21},{6,22},{7,23},{8,24},{9,... | collective-permute-start | bytes 589832 | tf_op jit(solution)/shard_map/ppermute | solution.py:328
  35.0 7.3 %collective-permute-start.11 = (bf16[128,512]{1,0:T(8,128)(2,1)S(1)}, bf16[128,512]{1,0:T(8,128)(2,1)S(1)}, u32[]{:S(2)}, u32[]{:S(2)}) collective-permute-start(bf16[128,512]{1,0:T(8,128)(2,1)S(1)} %get-tuple-element.61), channel_id=1, source_target_pairs={{0,8},{1,9},{2,10},{3,11},{4,12},{5,13},{6,14},{7,15},{8,0},{9,1},... | collective-permute-start | bytes 393224 | tf_op jit(solution)/shard_map/ppermute | solution.py:328
  40.4 8.5 %collective-permute-start.22 = (bf16[128,512]{1,0:T(8,128)(2,1)S(1)}, bf16[128,512]{1,0:T(8,128)(2,1)S(1)}, u32[]{:S(2)}, u32[]{:S(2)}) collective-permute-start(bf16[128,512]{1,0:T(8,128)(2,1)S(1)} %get-tuple-element.73), channel_id=1, source_target_pairs={{0,2},{1,3},{2,0},{3,1},{4,6},{5,7},{6,4},{7,5},{8,10},{9,11},{10,... | collective-permute-start | bytes 393224 | tf_op jit(solution)/shard_map/ppermute | solution.py:328
  41.5 7.6 %collective-permute-start.19 = (bf16[128,512]{1,0:T(8,128)(2,1)S(1)}, bf16[128,512]{1,0:T(8,128)(2,1)S(1)}, u32[]{:S(2)}, u32[]{:S(2)}) collective-permute-start(bf16[128,512]{1,0:T(8,128)(2,1)S(1)} %get-tuple-element.73), channel_id=1, source_target_pairs={{0,4},{1,5},{2,6},{3,7},{4,0},{5,1},{6,2},{7,3},{8,12},{9,13},{10,... | collective-permute-start | bytes 393224 | tf_op jit(solution)/shard_map/ppermute | solution.py:328
  42.3 6.8 %collective-permute-start.18 = (bf16[128,512]{1,0:T(8,128)(2,1)S(1)}, bf16[128,512]{1,0:T(8,128)(2,1)S(1)}, u32[]{:S(2)}, u32[]{:S(2)}) collective-permute-start(bf16[128,512]{1,0:T(8,128)(2,1)S(1)} %get-tuple-element.72), channel_id=1, source_target_pairs={{0,2},{1,3},{2,0},{3,1},{4,6},{5,7},{6,4},{7,5},{8,10},{9,11},{10,... | collective-permute-start | bytes 393224 | tf_op jit(solution)/shard_map/ppermute | solution.py:328
  43.1 15.6 %collective-permute-start.24 = (bf16[128,512]{1,0:T(8,128)(2,1)S(1)}, bf16[128,512]{1,0:T(8,128)(2,1)S(1)}, u32[]{:S(2)}, u32[]{:S(2)}) collective-permute-start(bf16[128,512]{1,0:T(8,128)(2,1)S(1)} %get-tuple-element.72), channel_id=1, source_target_pairs={{0,16},{1,17},{2,18},{3,19},{4,20},{5,21},{6,22},{7,23},{8,24},{9,... | collective-permute-start | bytes 393224 | tf_op jit(solution)/shard_map/ppermute | solution.py:328
  45.2 5.7 %collective-permute-start.16 = (bf16[128,768]{1,0:T(8,128)(2,1)S(1)}, bf16[128,768]{1,0:T(8,128)(2,1)S(1)}, u32[]{:S(2)}, u32[]{:S(2)}) collective-permute-start(bf16[128,768]{1,0:T(8,128)(2,1)S(1)} %get-tuple-element.70), channel_id=1, source_target_pairs={{0,2},{1,3},{2,0},{3,1},{4,6},{5,7},{6,4},{7,5},{8,10},{9,11},{10,... | collective-permute-start | bytes 589832 | tf_op jit(solution)/shard_map/ppermute | solution.py:328
  48.9 7.1 %collective-permute-start.17 = (bf16[128,768]{1,0:T(8,128)(2,1)S(1)}, bf16[128,768]{1,0:T(8,128)(2,1)S(1)}, u32[]{:S(2)}, u32[]{:S(2)}) collective-permute-start(bf16[128,768]{1,0:T(8,128)(2,1)S(1)} %get-tuple-element.71), channel_id=1, source_target_pairs={{0,16},{1,17},{2,18},{3,19},{4,20},{5,21},{6,22},{7,23},{8,24},{9,... | collective-permute-start | bytes 589832 | tf_op jit(solution)/shard_map/ppermute | solution.py:328
  49.1 13.1 %collective-permute-start.26 = (bf16[640,512]{1,0:T(8,128)(2,1)S(1)}, bf16[640,512]{1,0:T(8,128)(2,1)S(1)}, u32[]{:S(2)}, u32[]{:S(2)}) collective-permute-start(bf16[640,512]{1,0:T(8,128)(2,1)S(1)} %constant_dynamic-update-slice_fusion.16.refs_6_), channel_id=1, source_target_pairs={{0,1},{1,0},{2,3},{3,2},{4,5},{5,4},{6,7},{7,6},{8,9},{9,8},{10,11... | collective-permute-start | bytes 1966088 | tf_op jit(solution)/shard_map/ppermute | solution.py:328
  50.9 7.7 %collective-permute-start.25 = (bf16[128,512]{1,0:T(8,128)(2,1)S(1)}, bf16[128,512]{1,0:T(8,128)(2,1)S(1)}, u32[]{:S(2)}, u32[]{:S(2)}) collective-permute-start(bf16[128,512]{1,0:T(8,128)(2,1)S(1)} %get-tuple-element.79), channel_id=1, source_target_pairs={{0,16},{1,17},{2,18},{3,19},{4,20},{5,21},{6,22},{7,23},{8,24},{9,... | collective-permute-start | bytes 393224 | tf_op jit(solution)/shard_map/ppermute | solution.py:328
  51.5 7.2 %collective-permute-start.23 = (bf16[128,512]{1,0:T(8,128)(2,1)S(1)}, bf16[128,512]{1,0:T(8,128)(2,1)S(1)}, u32[]{:S(2)}, u32[]{:S(2)}) collective-permute-start(bf16[128,512]{1,0:T(8,128)(2,1)S(1)} %get-tuple-element.78), channel_id=1, source_target_pairs={{0,2},{1,3},{2,0},{3,1},{4,6},{5,7},{6,4},{7,5},{8,10},{9,11},{10,... | collective-permute-start | bytes 393224 | tf_op jit(solution)/shard_map/ppermute | solution.py:328
  58.7 3.4 %collective-permute-start.27 = (bf16[400,512]{1,0:T(8,128)(2,1)S(1)}, bf16[400,512]{1,0:T(8,128)(2,1)S(1)}, u32[]{:S(2)}, u32[]{:S(2)}) collective-permute-start(bf16[400,512]{1,0:T(8,128)(2,1)S(1)} %maximum_maximum_fusion.refs_7_), channel_id=1, source_target_pairs={{0,1},{1,0},{2,3},{3,2},{4,5},{5,4},{6,7},{7,6},{8,9},{9,8},{10,11... | collective-permute-start | bytes 1228808 | tf_op jit(solution)/shard_map/ppermute | solution.py:328
  (11 other events, 63.8 us)

commit v6 on v5

--- a/solution.py
+++ b/solution.py
@@ -8,7 +8,7 @@
 from jax.sharding import PartitionSpec as P
 
 HEADS = 16
-EXPERT_STEPS = 2
+EXPERT_STEPS = 1
 CHIPS = 8
 LONG = 1 << 34
 EARLY = (0, 1, 2, 4, 6)

time: 92 us -> 91.5 us (level)
  transfers between devices with their start and end apart: 28 -> 28, of which waited for: 11 -> 11; matrix products, arithmetic and copies ran while one was open for 0% -> 0% of each run, Pallas kernels for 13% -> 14%
where the time goes in v6:
time: 91.5 us; the launch traced here: 91.3 us
  starting transfers between devices  25 us (27%)
  waiting for transfers between devices  21.8 us (24%)
  blocking collectives  21 us (23%)
  Pallas kernels  18.3 us (20%)
  local copies, waits for them, and re-layouts  2.84 us (3%)
  other arithmetic  1.3 us (1%)
    ppermute x28, starting transfers between devices, send(): return lax.ppermute(value, AXES, pairs)  25 us
    ppermute x28, waiting for transfers between devices, send(): return lax.ppermute(value, AXES, pairs)  21.8 us
    all_to_all x1, blocking collectives, on_device(): lax.all_to_all(answered, 'expert', split_axis=1, concat_axis=1, tiled=True)  10.5 us
    all_to_all x1, blocking collectives, on_device(): lax.all_to_all(slot_inputs, 'expert', split_axis=1, concat_axis=1, tiled=...  10.5 us
    pallas_call x4, Pallas kernels, attention(): pl.pallas_call(functools.partial(attention_kernel, length, head), out_sha...  10.4 us
    pallas_call x1, Pallas kernels, router(): pl.pallas_call(functools.partial(router_kernel, count, images, length), o...  4.29 us
    unnamed x31, local copies, waits for them, and re-layouts  2.49 us
  transfers between devices with their start and end apart: 28, of which 11 were waited for; matrix products, arithmetic and copies ran while one was open for 0% of the time, Pallas kernels for 14%

profile of v6, /device:TPU:0, one launch (start us, length us, event | category | flops | bytes accessed | tf_op | source)
XLA Modules:
  0.0 91.3 jit_solution(7193438153278768094)
XLA Ops:
  0.5 1.6 %collective-permute-done.other_ref = bf16[64,3072]{1,0:T(8,128)(2,1)S(1)} collective-permute-done((bf16[64,3072]{1,0:T(8,128)(2,1)}, bf16[64,3072]{1,0:T(8,128)(2,1)S(1)}, u32[]{:S(2)}, u32[]{:S(2)}) %collective-permute-start) | collective-permute-done | bytes 393248 | tf_op jit(solution)/shard_map/ppermute | solution.py:328
  3.1 3.0 %collective-permute-start.1 = (bf16[128,768]{1,0:T(8,128)(2,1)S(1)}, bf16[128,768]{1,0:T(8,128)(2,1)S(1)}, u32[]{:S(2)}, u32[]{:S(2)}) collective-permute-start(bf16[128,768]{1,0:T(8,128)(2,1)S(1)} %get-tuple-element.44.refs_0_), channel_id=1, source_target_pairs={{0,4},{1,5},{2,6},{3,7},{4,0},{5,1},{6,2},{7,3},{8,12},{9,13},{10,... | collective-permute-start | bytes 589832 | tf_op jit(solution)/shard_map/ppermute | solution.py:328
  6.1 2.6 %collective-permute-start.2 = (bf16[128,768]{1,0:T(8,128)(2,1)S(1)}, bf16[128,768]{1,0:T(8,128)(2,1)S(1)}, u32[]{:S(2)}, u32[]{:S(2)}) collective-permute-start(bf16[128,768]{1,0:T(8,128)(2,1)S(1)} %get-tuple-element.44.refs_0_), channel_id=1, source_target_pairs={{0,8},{1,9},{2,10},{3,11},{4,12},{5,13},{6,14},{7,15},{8,0},{9,1},... | collective-permute-start | bytes 589832 | tf_op jit(solution)/shard_map/ppermute | solution.py:328
  8.7 1.5 %collective-permute-start.3 = (bf16[128,768]{1,0:T(8,128)(2,1)S(1)}, bf16[128,768]{1,0:T(8,128)(2,1)S(1)}, u32[]{:S(2)}, u32[]{:S(2)}) collective-permute-start(bf16[128,768]{1,0:T(8,128)(2,1)S(1)} %get-tuple-element.44.refs_0_), channel_id=1, source_target_pairs={{0,2},{1,3},{2,0},{3,1},{4,6},{5,7},{6,4},{7,5},{8,10},{9,11},{10,... | collective-permute-start | bytes 589832 | tf_op jit(solution)/shard_map/ppermute | solution.py:328
  12.9 2.5 %collective-permute-done.1.refs_4_.refs_0_ = bf16[128,768]{1,0:T(8,128)(2,1)S(1)} collective-permute-done((bf16[128,768]{1,0:T(8,128)(2,1)S(1)}, bf16[128,768]{1,0:T(8,128)(2,1)S(1)}, u32[]{:S(2)}, u32[]{:S(2)}) %collective-permute-start.1) | collective-permute-done | bytes 196640 | tf_op jit(solution)/shard_map/ppermute | solution.py:328
  15.4 2.5 %collective-permute-done.2.refs_0_ = bf16[128,768]{1,0:T(8,128)(2,1)S(1)} collective-permute-done((bf16[128,768]{1,0:T(8,128)(2,1)S(1)}, bf16[128,768]{1,0:T(8,128)(2,1)S(1)}, u32[]{:S(2)}, u32[]{:S(2)}) %collective-permute-start.2) | collective-permute-done | bytes 196640 | tf_op jit(solution)/shard_map/ppermute | solution.py:328
  19.4 1.5 %collective-permute-start.7 = (bf16[128,768]{1,0:T(8,128)(2,1)S(1)}, bf16[128,768]{1,0:T(8,128)(2,1)S(1)}, u32[]{:S(2)}, u32[]{:S(2)}) collective-permute-start(bf16[128,768]{1,0:T(8,128)(2,1)S(1)} %get-tuple-element.54), channel_id=1, source_target_pairs={{0,2},{1,3},{2,0},{3,1},{4,6},{5,7},{6,4},{7,5},{8,10},{9,11},{10,... | collective-permute-start | bytes 589832 | tf_op jit(solution)/shard_map/ppermute | solution.py:328
  21.5 1.8 %collective-permute-start.9 = (bf16[128,768]{1,0:T(8,128)(2,1)S(1)}, bf16[128,768]{1,0:T(8,128)(2,1)S(1)}, u32[]{:S(2)}, u32[]{:S(2)}) collective-permute-start(bf16[128,768]{1,0:T(8,128)(2,1)S(1)} %get-tuple-element.56), channel_id=1, source_target_pairs={{0,8},{1,9},{2,10},{3,11},{4,12},{5,13},{6,14},{7,15},{8,0},{9,1},... | collective-permute-start | bytes 589832 | tf_op jit(solution)/shard_map/ppermute | solution.py:328
  24.3 3.0 %collective-permute-done.7.refs_0_ = bf16[128,768]{1,0:T(8,128)(2,1)S(1)} collective-permute-done((bf16[128,768]{1,0:T(8,128)(2,1)S(1)}, bf16[128,768]{1,0:T(8,128)(2,1)S(1)}, u32[]{:S(2)}, u32[]{:S(2)}) %collective-permute-start.7) | collective-permute-done | bytes 196640 | tf_op jit(solution)/shard_map/ppermute | solution.py:328
  27.8 1.5 %collective-permute-done.5.refs_3_ = bf16[128,768]{1,0:T(8,128)(2,1)S(1)} collective-permute-done((bf16[128,768]{1,0:T(8,128)(2,1)S(1)}, bf16[128,768]{1,0:T(8,128)(2,1)S(1)}, u32[]{:S(2)}, u32[]{:S(2)}) %collective-permute-start.5) | collective-permute-done | bytes 196640 | tf_op jit(solution)/shard_map/ppermute | solution.py:328
  29.5 1.5 %collective-permute-done.9.refs_0_ = bf16[128,768]{1,0:T(8,128)(2,1)S(1)} collective-permute-done((bf16[128,768]{1,0:T(8,128)(2,1)S(1)}, bf16[128,768]{1,0:T(8,128)(2,1)S(1)}, u32[]{:S(2)}, u32[]{:S(2)}) %collective-permute-start.9) | collective-permute-done | bytes 196640 | tf_op jit(solution)/shard_map/ppermute | solution.py:328
  31.1 1.9 %collective-permute-done.8.refs_4_ = bf16[128,768]{1,0:T(8,128)(2,1)S(1)} collective-permute-done((bf16[128,768]{1,0:T(8,128)(2,1)S(1)}, bf16[128,768]{1,0:T(8,128)(2,1)S(1)}, u32[]{:S(2)}, u32[]{:S(2)}) %collective-permute-start.8) | collective-permute-done | bytes 196640 | tf_op jit(solution)/shard_map/ppermute | solution.py:328
  33.0 1.7 %collective-permute-start.12 = (bf16[128,768]{1,0:T(8,128)(2,1)S(1)}, bf16[128,768]{1,0:T(8,128)(2,1)S(1)}, u32[]{:S(2)}, u32[]{:S(2)}) collective-permute-start(bf16[128,768]{1,0:T(8,128)(2,1)S(1)} %get-tuple-element.62), channel_id=1, source_target_pairs={{0,2},{1,3},{2,0},{3,1},{4,6},{5,7},{6,4},{7,5},{8,10},{9,11},{10,... | collective-permute-start | bytes 589832 | tf_op jit(solution)/shard_map/ppermute | solution.py:328
  36.4 2.6 %attention.4.refs_2_.refs_0_ = bf16[512,256]{1,0:T(8,128)(2,1)S(1)} custom-call(bf16[512,1024]{1,0:T(8,128)(2,1)S(1)} %collective-permute-done.14.normed, bf16[1024,768]{1,0:T(8,128)(2,1)S(1)} %constant_dynamic-update-slice_fusion.weight, bf16[8,128]{1,0:T(8,128)(2,1)S(1)} %get-tuple-element.64.refs_0_.refs_1_), custom_call_target="tpu_custom_call" | custom-call | flops 939524096 | bytes 3670016 | tf_op jit(solution)/shard_map/attention/pallas_call | solution.py:182
  43.1 2.2 %collective-permute-start.24 = (bf16[128,512]{1,0:T(8,128)(2,1)S(1)}, bf16[128,512]{1,0:T(8,128)(2,1)S(1)}, u32[]{:S(2)}, u32[]{:S(2)}) collective-permute-start(bf16[128,512]{1,0:T(8,128)(2,1)S(1)} %get-tuple-element.72), channel_id=1, source_target_pairs={{0,16},{1,17},{2,18},{3,19},{4,20},{5,21},{6,22},{7,23},{8,24},{9,... | collective-permute-start | bytes 393224 | tf_op jit(solution)/shard_map/ppermute | solution.py:328
  46.3 2.6 %attention.5.refs_3_.refs_2_ = bf16[512,256]{1,0:T(8,128)(2,1)S(1)} custom-call(bf16[512,1024]{1,0:T(8,128)(2,1)S(1)} %get-tuple-element.52.normed, bf16[1024,768]{1,0:T(8,128)(2,1)S(1)} %constant_dynamic-update-slice_fusion.weight, bf16[8,128]{1,0:T(8,128)(2,1)S(1)} %get-tuple-element.69.refs_0_.refs_1_), custom_call_target="tpu_custom_call" | custom-call | flops 939524096 | bytes 3670016 | tf_op jit(solution)/shard_map/attention/pallas_call | solution.py:182
  49.2 1.7 %collective-permute-done.16.refs_2_ = bf16[128,768]{1,0:T(8,128)(2,1)S(1)} collective-permute-done((bf16[128,768]{1,0:T(8,128)(2,1)S(1)}, bf16[128,768]{1,0:T(8,128)(2,1)S(1)}, u32[]{:S(2)}, u32[]{:S(2)}) %collective-permute-start.16) | collective-permute-done | bytes 196640 | tf_op jit(solution)/shard_map/ppermute | solution.py:328
  52.5 3.5 %collective-permute-done.17.refs_2_ = bf16[128,768]{1,0:T(8,128)(2,1)S(1)} collective-permute-done((bf16[128,768]{1,0:T(8,128)(2,1)S(1)}, bf16[128,768]{1,0:T(8,128)(2,1)S(1)}, u32[]{:S(2)}, u32[]{:S(2)}) %collective-permute-start.17) | collective-permute-done | bytes 196640 | tf_op jit(solution)/shard_map/ppermute | solution.py:328
  56.1 2.6 %attention.6.refs_0_ = bf16[512,256]{1,0:T(8,128)(2,1)S(1)} custom-call(bf16[512,1024]{1,0:T(8,128)(2,1)S(1)} %collective-permute-done.14.normed, bf16[1024,768]{1,0:T(8,128)(2,1)S(1)} %constant_dynamic-update-slice_fusion.8.weight, bf16[8,128]{1,0:T(8,128)(2,1)S(1)} %get-tuple-element.76.refs_0_), custom_call_target="tpu_custom_call" | custom-call | flops 939524096 | bytes 3670016 | tf_op jit(solution)/shard_map/attention/pallas_call | solution.py:182
  59.4 2.7 %attention.7.refs_3_ = bf16[512,256]{1,0:T(8,128)(2,1)S(1)} custom-call(bf16[512,1024]{1,0:T(8,128)(2,1)S(1)} %get-tuple-element.52.normed, bf16[1024,768]{1,0:T(8,128)(2,1)S(1)} %constant_dynamic-update-slice_fusion.8.weight, bf16[512,256]{1,0:T(8,128)(2,1)S(1)} %attention.6.refs_0_), custom_call_target="tpu_custom_call" | custom-call | flops 939524096 | bytes 3670016 | tf_op jit(solution)/shard_map/attention/pallas_call | solution.py:182
  62.2 4.3 %router.1 = (f32[512,1024]{1,0:T(8,128)S(1)}, bf16[2,32,256]{2,1,0:T(8,128)(2,1)S(1)}, bf16[2,32,1024]{2,1,0:T(8,128)(2,1)S(1)}) custom-call(bf16[512,1024]{1,0:T(8,128)(2,1)S(1)} %bitcast.9, bf16[32,1024]{1,0:T(8,128)(2,1)S(1)} %bitcast.12, bf16[512,256]{1,0:T(8,128)(2,1)S(1)} %attention.5.refs_3_.refs_2_, bf16[512,256]{1,0:T(8,128)(2,1)S(1)} %attention.7.refs_3_, ...), custom_call_target="tpu_custom_call" | custom-call | flops 1140850688 | bytes 6291456 | tf_op jit(solution)/shard_map/router/pallas_call | solution.py:250
  66.7 10.5 %all_to_all.10 = bf16[2,32,1024]{2,0,1:T(2,128)(2,1)S(1)} all-to-all(bf16[2,32,1024]{2,0,1:T(2,128)(2,1)S(1)} %copy.9), channel_id=1, replica_groups=mesh['group'=2,'expert'=16] {'expert'}, dimensions={1} | all-to-all | bytes 262144 | tf_op jit(solution)/shard_map/all_to_all | solution.py:450
  77.2 1.6 %experts.1 = bf16[1,64,1024]{2,1,0:T(8,128)(2,1)S(1)} custom-call(bf16[1,64,1024]{2,1,0:T(8,128)(2,1)S(1)} %bitcast.10, bf16[1,1024,2048]{2,1,0:T(8,128)(2,1)S(1)} %copy-done, bf16[1,2048,1024]{2,1,0:T(8,128)(2,1)S(1)} %copy-done.1), custom_call_target="tpu_custom_call" | custom-call | flops 536870912 | bytes 8388608 | tf_op jit(solution)/shard_map/experts/pallas_call | solution.py:296
  79.0 10.5 %all_to_all.11 = bf16[2,32,1024]{2,0,1:T(2,128)(2,1)S(1)} all-to-all(bf16[2,32,1024]{2,0,1:T(2,128)(2,1)S(1)} %copy.11), channel_id=1, replica_groups=mesh['group'=2,'expert'=16] {'expert'}, dimensions={1} | all-to-all | bytes 262144 | tf_op jit(solution)/shard_map/all_to_all | solution.py:456
  (100 shorter events, 19.3 us)
Async XLA Ops:
  3.1 12.3 %collective-permute-start.1 = (bf16[128,768]{1,0:T(8,128)(2,1)S(1)}, bf16[128,768]{1,0:T(8,128)(2,1)S(1)}, u32[]{:S(2)}, u32[]{:S(2)}) collective-permute-start(bf16[128,768]{1,0:T(8,128)(2,1)S(1)} %get-tuple-element.44.refs_0_), channel_id=1, source_target_pairs={{0,4},{1,5},{2,6},{3,7},{4,0},{5,1},{6,2},{7,3},{8,12},{9,13},{10,... | collective-permute-start | bytes 589832 | tf_op jit(solution)/shard_map/ppermute | solution.py:328
  6.1 11.8 %collective-permute-start.2 = (bf16[128,768]{1,0:T(8,128)(2,1)S(1)}, bf16[128,768]{1,0:T(8,128)(2,1)S(1)}, u32[]{:S(2)}, u32[]{:S(2)}) collective-permute-start(bf16[128,768]{1,0:T(8,128)(2,1)S(1)} %get-tuple-element.44.refs_0_), channel_id=1, source_target_pairs={{0,8},{1,9},{2,10},{3,11},{4,12},{5,13},{6,14},{7,15},{8,0},{9,1},... | collective-permute-start | bytes 589832 | tf_op jit(solution)/shard_map/ppermute | solution.py:328
  8.7 9.2 %collective-permute-start.3 = (bf16[128,768]{1,0:T(8,128)(2,1)S(1)}, bf16[128,768]{1,0:T(8,128)(2,1)S(1)}, u32[]{:S(2)}, u32[]{:S(2)}) collective-permute-start(bf16[128,768]{1,0:T(8,128)(2,1)S(1)} %get-tuple-element.44.refs_0_), channel_id=1, source_target_pairs={{0,2},{1,3},{2,0},{3,1},{4,6},{5,7},{6,4},{7,5},{8,10},{9,11},{10,... | collective-permute-start | bytes 589832 | tf_op jit(solution)/shard_map/ppermute | solution.py:328
  12.3 8.6 %collective-permute-start.4 = (bf16[128,768]{1,0:T(8,128)(2,1)S(1)}, bf16[128,768]{1,0:T(8,128)(2,1)S(1)}, u32[]{:S(2)}, u32[]{:S(2)}) collective-permute-start(bf16[128,768]{1,0:T(8,128)(2,1)S(1)} %get-tuple-element.50), channel_id=1, source_target_pairs={{0,2},{1,3},{2,0},{3,1},{4,6},{5,7},{6,4},{7,5},{8,10},{9,11},{10,... | collective-permute-start | bytes 589832 | tf_op jit(solution)/shard_map/ppermute | solution.py:328
  17.9 9.8 %collective-permute-start.6 = (bf16[128,768]{1,0:T(8,128)(2,1)S(1)}, bf16[128,768]{1,0:T(8,128)(2,1)S(1)}, u32[]{:S(2)}, u32[]{:S(2)}) collective-permute-start(bf16[128,768]{1,0:T(8,128)(2,1)S(1)} %get-tuple-element.54), channel_id=1, source_target_pairs={{0,16},{1,17},{2,18},{3,19},{4,20},{5,21},{6,22},{7,23},{8,24},{9,... | collective-permute-start | bytes 589832 | tf_op jit(solution)/shard_map/ppermute | solution.py:328
  19.4 7.8 %collective-permute-start.7 = (bf16[128,768]{1,0:T(8,128)(2,1)S(1)}, bf16[128,768]{1,0:T(8,128)(2,1)S(1)}, u32[]{:S(2)}, u32[]{:S(2)}) collective-permute-start(bf16[128,768]{1,0:T(8,128)(2,1)S(1)} %get-tuple-element.54), channel_id=1, source_target_pairs={{0,2},{1,3},{2,0},{3,1},{4,6},{5,7},{6,4},{7,5},{8,10},{9,11},{10,... | collective-permute-start | bytes 589832 | tf_op jit(solution)/shard_map/ppermute | solution.py:328
  20.9 8.4 %collective-permute-start.5 = (bf16[128,768]{1,0:T(8,128)(2,1)S(1)}, bf16[128,768]{1,0:T(8,128)(2,1)S(1)}, u32[]{:S(2)}, u32[]{:S(2)}) collective-permute-start(bf16[128,768]{1,0:T(8,128)(2,1)S(1)} %get-tuple-element.53), channel_id=1, source_target_pairs={{0,2},{1,3},{2,0},{3,1},{4,6},{5,7},{6,4},{7,5},{8,10},{9,11},{10,... | collective-permute-start | bytes 589832 | tf_op jit(solution)/shard_map/ppermute | solution.py:328
  21.5 9.6 %collective-permute-start.9 = (bf16[128,768]{1,0:T(8,128)(2,1)S(1)}, bf16[128,768]{1,0:T(8,128)(2,1)S(1)}, u32[]{:S(2)}, u32[]{:S(2)}) collective-permute-start(bf16[128,768]{1,0:T(8,128)(2,1)S(1)} %get-tuple-element.56), channel_id=1, source_target_pairs={{0,8},{1,9},{2,10},{3,11},{4,12},{5,13},{6,14},{7,15},{8,0},{9,1},... | collective-permute-start | bytes 589832 | tf_op jit(solution)/shard_map/ppermute | solution.py:328
  24.1 12.3 %collective-permute-start.14 = (bf16[512,1024]{1,0:T(8,128)(2,1)S(1)}, bf16[512,1024]{1,0:T(8,128)(2,1)S(1)}, u32[]{:S(2)}, u32[]{:S(2)}) collective-permute-start(bf16[512,1024]{1,0:T(8,128)(2,1)S(1)} %get-tuple-element.65), channel_id=1, source_target_pairs={{0,1},{1,0},{2,3},{3,2},{4,5},{5,4},{6,7},{7,6},{8,9},{9,8},{10,11... | collective-permute-start | bytes 3145736 | tf_op jit(solution)/shard_map/ppermute | solution.py:328
  27.2 5.7 %collective-permute-start.8 = (bf16[128,768]{1,0:T(8,128)(2,1)S(1)}, bf16[128,768]{1,0:T(8,128)(2,1)S(1)}, u32[]{:S(2)}, u32[]{:S(2)}) collective-permute-start(bf16[128,768]{1,0:T(8,128)(2,1)S(1)} %get-tuple-element.55), channel_id=1, source_target_pairs={{0,16},{1,17},{2,18},{3,19},{4,20},{5,21},{6,22},{7,23},{8,24},{9,... | collective-permute-start | bytes 589832 | tf_op jit(solution)/shard_map/ppermute | solution.py:328
  29.4 9.7 %collective-permute-start.13 = (bf16[128,768]{1,0:T(8,128)(2,1)S(1)}, bf16[128,768]{1,0:T(8,128)(2,1)S(1)}, u32[]{:S(2)}, u32[]{:S(2)}) collective-permute-start(bf16[128,768]{1,0:T(8,128)(2,1)S(1)} %get-tuple-element.63), channel_id=1, source_target_pairs={{0,4},{1,5},{2,6},{3,7},{4,0},{5,1},{6,2},{7,3},{8,12},{9,13},{10,... | collective-permute-start | bytes 589832 | tf_op jit(solution)/shard_map/ppermute | solution.py:328
  33.0 6.1 %collective-permute-start.12 = (bf16[128,768]{1,0:T(8,128)(2,1)S(1)}, bf16[128,768]{1,0:T(8,128)(2,1)S(1)}, u32[]{:S(2)}, u32[]{:S(2)}) collective-permute-start(bf16[128,768]{1,0:T(8,128)(2,1)S(1)} %get-tuple-element.62), channel_id=1, source_target_pairs={{0,2},{1,3},{2,0},{3,1},{4,6},{5,7},{6,4},{7,5},{8,10},{9,11},{10,... | collective-permute-start | bytes 589832 | tf_op jit(solution)/shard_map/ppermute | solution.py:328
  34.7 5.7 %collective-permute-start.15 = (bf16[128,768]{1,0:T(8,128)(2,1)S(1)}, bf16[128,768]{1,0:T(8,128)(2,1)S(1)}, u32[]{:S(2)}, u32[]{:S(2)}) collective-permute-start(bf16[128,768]{1,0:T(8,128)(2,1)S(1)} %get-tuple-element.62), channel_id=1, source_target_pairs={{0,16},{1,17},{2,18},{3,19},{4,20},{5,21},{6,22},{7,23},{8,24},{9,... | collective-permute-start | bytes 589832 | tf_op jit(solution)/shard_map/ppermute | solution.py:328
  35.0 7.3 %collective-permute-start.11 = (bf16[128,512]{1,0:T(8,128)(2,1)S(1)}, bf16[128,512]{1,0:T(8,128)(2,1)S(1)}, u32[]{:S(2)}, u32[]{:S(2)}) collective-permute-start(bf16[128,512]{1,0:T(8,128)(2,1)S(1)} %get-tuple-element.61), channel_id=1, source_target_pairs={{0,8},{1,9},{2,10},{3,11},{4,12},{5,13},{6,14},{7,15},{8,0},{9,1},... | collective-permute-start | bytes 393224 | tf_op jit(solution)/shard_map/ppermute | solution.py:328
  40.4 8.5 %collective-permute-start.22 = (bf16[128,512]{1,0:T(8,128)(2,1)S(1)}, bf16[128,512]{1,0:T(8,128)(2,1)S(1)}, u32[]{:S(2)}, u32[]{:S(2)}) collective-permute-start(bf16[128,512]{1,0:T(8,128)(2,1)S(1)} %get-tuple-element.73), channel_id=1, source_target_pairs={{0,2},{1,3},{2,0},{3,1},{4,6},{5,7},{6,4},{7,5},{8,10},{9,11},{10,... | collective-permute-start | bytes 393224 | tf_op jit(solution)/shard_map/ppermute | solution.py:328
  41.5 7.6 %collective-permute-start.19 = (bf16[128,512]{1,0:T(8,128)(2,1)S(1)}, bf16[128,512]{1,0:T(8,128)(2,1)S(1)}, u32[]{:S(2)}, u32[]{:S(2)}) collective-permute-start(bf16[128,512]{1,0:T(8,128)(2,1)S(1)} %get-tuple-element.73), channel_id=1, source_target_pairs={{0,4},{1,5},{2,6},{3,7},{4,0},{5,1},{6,2},{7,3},{8,12},{9,13},{10,... | collective-permute-start | bytes 393224 | tf_op jit(solution)/shard_map/ppermute | solution.py:328
  42.3 6.8 %collective-permute-start.18 = (bf16[128,512]{1,0:T(8,128)(2,1)S(1)}, bf16[128,512]{1,0:T(8,128)(2,1)S(1)}, u32[]{:S(2)}, u32[]{:S(2)}) collective-permute-start(bf16[128,512]{1,0:T(8,128)(2,1)S(1)} %get-tuple-element.72), channel_id=1, source_target_pairs={{0,2},{1,3},{2,0},{3,1},{4,6},{5,7},{6,4},{7,5},{8,10},{9,11},{10,... | collective-permute-start | bytes 393224 | tf_op jit(solution)/shard_map/ppermute | solution.py:328
  43.1 15.6 %collective-permute-start.24 = (bf16[128,512]{1,0:T(8,128)(2,1)S(1)}, bf16[128,512]{1,0:T(8,128)(2,1)S(1)}, u32[]{:S(2)}, u32[]{:S(2)}) collective-permute-start(bf16[128,512]{1,0:T(8,128)(2,1)S(1)} %get-tuple-element.72), channel_id=1, source_target_pairs={{0,16},{1,17},{2,18},{3,19},{4,20},{5,21},{6,22},{7,23},{8,24},{9,... | collective-permute-start | bytes 393224 | tf_op jit(solution)/shard_map/ppermute | solution.py:328
  45.2 5.7 %collective-permute-start.16 = (bf16[128,768]{1,0:T(8,128)(2,1)S(1)}, bf16[128,768]{1,0:T(8,128)(2,1)S(1)}, u32[]{:S(2)}, u32[]{:S(2)}) collective-permute-start(bf16[128,768]{1,0:T(8,128)(2,1)S(1)} %get-tuple-element.70), channel_id=1, source_target_pairs={{0,2},{1,3},{2,0},{3,1},{4,6},{5,7},{6,4},{7,5},{8,10},{9,11},{10,... | collective-permute-start | bytes 589832 | tf_op jit(solution)/shard_map/ppermute | solution.py:328
  48.9 7.1 %collective-permute-start.17 = (bf16[128,768]{1,0:T(8,128)(2,1)S(1)}, bf16[128,768]{1,0:T(8,128)(2,1)S(1)}, u32[]{:S(2)}, u32[]{:S(2)}) collective-permute-start(bf16[128,768]{1,0:T(8,128)(2,1)S(1)} %get-tuple-element.71), channel_id=1, source_target_pairs={{0,16},{1,17},{2,18},{3,19},{4,20},{5,21},{6,22},{7,23},{8,24},{9,... | collective-permute-start | bytes 589832 | tf_op jit(solution)/shard_map/ppermute | solution.py:328
  49.1 13.1 %collective-permute-start.26 = (bf16[640,512]{1,0:T(8,128)(2,1)S(1)}, bf16[640,512]{1,0:T(8,128)(2,1)S(1)}, u32[]{:S(2)}, u32[]{:S(2)}) collective-permute-start(bf16[640,512]{1,0:T(8,128)(2,1)S(1)} %constant_dynamic-update-slice_fusion.16.refs_6_), channel_id=1, source_target_pairs={{0,1},{1,0},{2,3},{3,2},{4,5},{5,4},{6,7},{7,6},{8,9},{9,8},{10,11... | collective-permute-start | bytes 1966088 | tf_op jit(solution)/shard_map/ppermute | solution.py:328
  50.9 7.7 %collective-permute-start.25 = (bf16[128,512]{1,0:T(8,128)(2,1)S(1)}, bf16[128,512]{1,0:T(8,128)(2,1)S(1)}, u32[]{:S(2)}, u32[]{:S(2)}) collective-permute-start(bf16[128,512]{1,0:T(8,128)(2,1)S(1)} %get-tuple-element.79), channel_id=1, source_target_pairs={{0,16},{1,17},{2,18},{3,19},{4,20},{5,21},{6,22},{7,23},{8,24},{9,... | collective-permute-start | bytes 393224 | tf_op jit(solution)/shard_map/ppermute | solution.py:328
  51.5 7.2 %collective-permute-start.23 = (bf16[128,512]{1,0:T(8,128)(2,1)S(1)}, bf16[128,512]{1,0:T(8,128)(2,1)S(1)}, u32[]{:S(2)}, u32[]{:S(2)}) collective-permute-start(bf16[128,512]{1,0:T(8,128)(2,1)S(1)} %get-tuple-element.78), channel_id=1, source_target_pairs={{0,2},{1,3},{2,0},{3,1},{4,6},{5,7},{6,4},{7,5},{8,10},{9,11},{10,... | collective-permute-start | bytes 393224 | tf_op jit(solution)/shard_map/ppermute | solution.py:328
  58.7 3.4 %collective-permute-start.27 = (bf16[400,512]{1,0:T(8,128)(2,1)S(1)}, bf16[400,512]{1,0:T(8,128)(2,1)S(1)}, u32[]{:S(2)}, u32[]{:S(2)}) collective-permute-start(bf16[400,512]{1,0:T(8,128)(2,1)S(1)} %maximum_maximum_fusion.refs_7_), channel_id=1, source_target_pairs={{0,1},{1,0},{2,3},{3,2},{4,5},{5,4},{6,7},{7,6},{8,9},{9,8},{10,11... | collective-permute-start | bytes 1228808 | tf_op jit(solution)/shard_map/ppermute | solution.py:328
  (11 other events, 63.8 us)

commit v7 on v6

--- a/solution.py
+++ b/solution.py
@@ -143,8 +143,9 @@
         mixed = jnp.dot(
             weights, jnp.where(mask, values, jnp.ones_like(values)), preferred_element_type=F32
         )
-        result.append(mixed / pltpu.roll(mixed, head, 1))
-    out_ref[rows, columns] = jnp.where(first, result[0], result[1]).astype(BF16)
+        result.append(mixed)
+    sums = pltpu.roll(jnp.where(first, result[1], result[0]), head, 1)
+    out_ref[rows, columns] = (jnp.where(first, result[0], result[1]) / sums).astype(BF16)
 
 
 def attention_kernel(length, head, normed, weight, *refs):

time: 91.5 us -> 91.5 us (level)
  transfers between devices with their start and end apart: 28 -> 28, of which waited for: 11 -> 11; matrix products, arithmetic and copies ran while one was open for 0% -> 0% of each run, Pallas kernels for 14% -> 13%
where the time goes in v7:
time: 91.5 us; the launch traced here: 91.2 us
  starting transfers between devices  25 us (27%)
  waiting for transfers between devices  21.8 us (24%)
  blocking collectives  21 us (23%)
  Pallas kernels  18.2 us (20%)
  local copies, waits for them, and re-layouts  2.84 us (3%)
  other arithmetic  1.3 us (1%)
    ppermute x28, starting transfers between devices, send(): return lax.ppermute(value, AXES, pairs)  25 us
    ppermute x28, waiting for transfers between devices, send(): return lax.ppermute(value, AXES, pairs)  21.8 us
    all_to_all x1, blocking collectives, on_device(): lax.all_to_all(slot_inputs, 'expert', split_axis=1, concat_axis=1, tiled=...  10.5 us
    all_to_all x1, blocking collectives, on_device(): lax.all_to_all(answered, 'expert', split_axis=1, concat_axis=1, tiled=True)  10.5 us
    pallas_call x4, Pallas kernels, attention(): pl.pallas_call(functools.partial(attention_kernel, length, head), out_sha...  10.4 us
    pallas_call x1, Pallas kernels, router(): pl.pallas_call(functools.partial(router_kernel, count, images, length), o...  4.29 us
    unnamed x31, local copies, waits for them, and re-layouts  2.49 us
  transfers between devices with their start and end apart: 28, of which 11 were waited for; matrix products, arithmetic and copies ran while one was open for 0% of the time, Pallas kernels for 13%

profile of v7, /device:TPU:0, one launch (start us, length us, event | category | flops | bytes accessed | tf_op | source)
XLA Modules:
  0.0 91.2 jit_solution(7609328685300573840)
XLA Ops:
  0.5 1.6 %collective-permute-done.other_ref = bf16[64,3072]{1,0:T(8,128)(2,1)S(1)} collective-permute-done((bf16[64,3072]{1,0:T(8,128)(2,1)}, bf16[64,3072]{1,0:T(8,128)(2,1)S(1)}, u32[]{:S(2)}, u32[]{:S(2)}) %collective-permute-start) | collective-permute-done | bytes 393248 | tf_op jit(solution)/shard_map/ppermute | solution.py:329
  3.1 3.0 %collective-permute-start.1 = (bf16[128,768]{1,0:T(8,128)(2,1)S(1)}, bf16[128,768]{1,0:T(8,128)(2,1)S(1)}, u32[]{:S(2)}, u32[]{:S(2)}) collective-permute-start(bf16[128,768]{1,0:T(8,128)(2,1)S(1)} %get-tuple-element.44.refs_0_), channel_id=1, source_target_pairs={{0,4},{1,5},{2,6},{3,7},{4,0},{5,1},{6,2},{7,3},{8,12},{9,13},{10,... | collective-permute-start | bytes 589832 | tf_op jit(solution)/shard_map/ppermute | solution.py:329
  6.1 2.6 %collective-permute-start.2 = (bf16[128,768]{1,0:T(8,128)(2,1)S(1)}, bf16[128,768]{1,0:T(8,128)(2,1)S(1)}, u32[]{:S(2)}, u32[]{:S(2)}) collective-permute-start(bf16[128,768]{1,0:T(8,128)(2,1)S(1)} %get-tuple-element.44.refs_0_), channel_id=1, source_target_pairs={{0,8},{1,9},{2,10},{3,11},{4,12},{5,13},{6,14},{7,15},{8,0},{9,1},... | collective-permute-start | bytes 589832 | tf_op jit(solution)/shard_map/ppermute | solution.py:329
  8.7 1.5 %collective-permute-start.3 = (bf16[128,768]{1,0:T(8,128)(2,1)S(1)}, bf16[128,768]{1,0:T(8,128)(2,1)S(1)}, u32[]{:S(2)}, u32[]{:S(2)}) collective-permute-start(bf16[128,768]{1,0:T(8,128)(2,1)S(1)} %get-tuple-element.44.refs_0_), channel_id=1, source_target_pairs={{0,2},{1,3},{2,0},{3,1},{4,6},{5,7},{6,4},{7,5},{8,10},{9,11},{10,... | collective-permute-start | bytes 589832 | tf_op jit(solution)/shard_map/ppermute | solution.py:329
  12.9 2.5 %collective-permute-done.1.refs_4_.refs_0_ = bf16[128,768]{1,0:T(8,128)(2,1)S(1)} collective-permute-done((bf16[128,768]{1,0:T(8,128)(2,1)S(1)}, bf16[128,768]{1,0:T(8,128)(2,1)S(1)}, u32[]{:S(2)}, u32[]{:S(2)}) %collective-permute-start.1) | collective-permute-done | bytes 196640 | tf_op jit(solution)/shard_map/ppermute | solution.py:329
  15.4 2.5 %collective-permute-done.2.refs_0_ = bf16[128,768]{1,0:T(8,128)(2,1)S(1)} collective-permute-done((bf16[128,768]{1,0:T(8,128)(2,1)S(1)}, bf16[128,768]{1,0:T(8,128)(2,1)S(1)}, u32[]{:S(2)}, u32[]{:S(2)}) %collective-permute-start.2) | collective-permute-done | bytes 196640 | tf_op jit(solution)/shard_map/ppermute | solution.py:329
  19.4 1.5 %collective-permute-start.7 = (bf16[128,768]{1,0:T(8,128)(2,1)S(1)}, bf16[128,768]{1,0:T(8,128)(2,1)S(1)}, u32[]{:S(2)}, u32[]{:S(2)}) collective-permute-start(bf16[128,768]{1,0:T(8,128)(2,1)S(1)} %get-tuple-element.54), channel_id=1, source_target_pairs={{0,2},{1,3},{2,0},{3,1},{4,6},{5,7},{6,4},{7,5},{8,10},{9,11},{10,... | collective-permute-start | bytes 589832 | tf_op jit(solution)/shard_map/ppermute | solution.py:329
  21.5 1.8 %collective-permute-start.9 = (bf16[128,768]{1,0:T(8,128)(2,1)S(1)}, bf16[128,768]{1,0:T(8,128)(2,1)S(1)}, u32[]{:S(2)}, u32[]{:S(2)}) collective-permute-start(bf16[128,768]{1,0:T(8,128)(2,1)S(1)} %get-tuple-element.56), channel_id=1, source_target_pairs={{0,8},{1,9},{2,10},{3,11},{4,12},{5,13},{6,14},{7,15},{8,0},{9,1},... | collective-permute-start | bytes 589832 | tf_op jit(solution)/shard_map/ppermute | solution.py:329
  24.3 3.0 %collective-permute-done.7.refs_0_ = bf16[128,768]{1,0:T(8,128)(2,1)S(1)} collective-permute-done((bf16[128,768]{1,0:T(8,128)(2,1)S(1)}, bf16[128,768]{1,0:T(8,128)(2,1)S(1)}, u32[]{:S(2)}, u32[]{:S(2)}) %collective-permute-start.7) | collective-permute-done | bytes 196640 | tf_op jit(solution)/shard_map/ppermute | solution.py:329
  27.8 1.5 %collective-permute-done.5.refs_3_ = bf16[128,768]{1,0:T(8,128)(2,1)S(1)} collective-permute-done((bf16[128,768]{1,0:T(8,128)(2,1)S(1)}, bf16[128,768]{1,0:T(8,128)(2,1)S(1)}, u32[]{:S(2)}, u32[]{:S(2)}) %collective-permute-start.5) | collective-permute-done | bytes 196640 | tf_op jit(solution)/shard_map/ppermute | solution.py:329
  29.5 1.5 %collective-permute-done.9.refs_0_ = bf16[128,768]{1,0:T(8,128)(2,1)S(1)} collective-permute-done((bf16[128,768]{1,0:T(8,128)(2,1)S(1)}, bf16[128,768]{1,0:T(8,128)(2,1)S(1)}, u32[]{:S(2)}, u32[]{:S(2)}) %collective-permute-start.9) | collective-permute-done | bytes 196640 | tf_op jit(solution)/shard_map/ppermute | solution.py:329
  31.1 1.9 %collective-permute-done.8.refs_4_ = bf16[128,768]{1,0:T(8,128)(2,1)S(1)} collective-permute-done((bf16[128,768]{1,0:T(8,128)(2,1)S(1)}, bf16[128,768]{1,0:T(8,128)(2,1)S(1)}, u32[]{:S(2)}, u32[]{:S(2)}) %collective-permute-start.8) | collective-permute-done | bytes 196640 | tf_op jit(solution)/shard_map/ppermute | solution.py:329
  33.0 1.7 %collective-permute-start.12 = (bf16[128,768]{1,0:T(8,128)(2,1)S(1)}, bf16[128,768]{1,0:T(8,128)(2,1)S(1)}, u32[]{:S(2)}, u32[]{:S(2)}) collective-permute-start(bf16[128,768]{1,0:T(8,128)(2,1)S(1)} %get-tuple-element.62), channel_id=1, source_target_pairs={{0,2},{1,3},{2,0},{3,1},{4,6},{5,7},{6,4},{7,5},{8,10},{9,11},{10,... | collective-permute-start | bytes 589832 | tf_op jit(solution)/shard_map/ppermute | solution.py:329
  36.4 2.5 %attention.4.refs_2_.refs_0_ = bf16[512,256]{1,0:T(8,128)(2,1)S(1)} custom-call(bf16[512,1024]{1,0:T(8,128)(2,1)S(1)} %collective-permute-done.14.normed, bf16[1024,768]{1,0:T(8,128)(2,1)S(1)} %constant_dynamic-update-slice_fusion.weight, bf16[8,128]{1,0:T(8,128)(2,1)S(1)} %get-tuple-element.64.refs_0_.refs_1_), custom_call_target="tpu_custom_call" | custom-call | flops 939524096 | bytes 3670016 | tf_op jit(solution)/shard_map/attention/pallas_call | solution.py:183
  43.1 2.2 %collective-permute-start.24 = (bf16[128,512]{1,0:T(8,128)(2,1)S(1)}, bf16[128,512]{1,0:T(8,128)(2,1)S(1)}, u32[]{:S(2)}, u32[]{:S(2)}) collective-permute-start(bf16[128,512]{1,0:T(8,128)(2,1)S(1)} %get-tuple-element.72), channel_id=1, source_target_pairs={{0,16},{1,17},{2,18},{3,19},{4,20},{5,21},{6,22},{7,23},{8,24},{9,... | collective-permute-start | bytes 393224 | tf_op jit(solution)/shard_map/ppermute | solution.py:329
  46.3 2.6 %attention.5.refs_3_.refs_2_ = bf16[512,256]{1,0:T(8,128)(2,1)S(1)} custom-call(bf16[512,1024]{1,0:T(8,128)(2,1)S(1)} %get-tuple-element.52.normed, bf16[1024,768]{1,0:T(8,128)(2,1)S(1)} %constant_dynamic-update-slice_fusion.weight, bf16[8,128]{1,0:T(8,128)(2,1)S(1)} %get-tuple-element.69.refs_0_.refs_1_), custom_call_target="tpu_custom_call" | custom-call | flops 939524096 | bytes 3670016 | tf_op jit(solution)/shard_map/attention/pallas_call | solution.py:183
  49.2 1.7 %collective-permute-done.16.refs_2_ = bf16[128,768]{1,0:T(8,128)(2,1)S(1)} collective-permute-done((bf16[128,768]{1,0:T(8,128)(2,1)S(1)}, bf16[128,768]{1,0:T(8,128)(2,1)S(1)}, u32[]{:S(2)}, u32[]{:S(2)}) %collective-permute-start.16) | collective-permute-done | bytes 196640 | tf_op jit(solution)/shard_map/ppermute | solution.py:329
  52.5 3.5 %collective-permute-done.17.refs_2_ = bf16[128,768]{1,0:T(8,128)(2,1)S(1)} collective-permute-done((bf16[128,768]{1,0:T(8,128)(2,1)S(1)}, bf16[128,768]{1,0:T(8,128)(2,1)S(1)}, u32[]{:S(2)}, u32[]{:S(2)}) %collective-permute-start.17) | collective-permute-done | bytes 196640 | tf_op jit(solution)/shard_map/ppermute | solution.py:329
  56.1 2.5 %attention.6.refs_0_ = bf16[512,256]{1,0:T(8,128)(2,1)S(1)} custom-call(bf16[512,1024]{1,0:T(8,128)(2,1)S(1)} %collective-permute-done.14.normed, bf16[1024,768]{1,0:T(8,128)(2,1)S(1)} %constant_dynamic-update-slice_fusion.8.weight, bf16[8,128]{1,0:T(8,128)(2,1)S(1)} %get-tuple-element.76.refs_0_), custom_call_target="tpu_custom_call" | custom-call | flops 939524096 | bytes 3670016 | tf_op jit(solution)/shard_map/attention/pallas_call | solution.py:183
  59.4 2.7 %attention.7.refs_3_ = bf16[512,256]{1,0:T(8,128)(2,1)S(1)} custom-call(bf16[512,1024]{1,0:T(8,128)(2,1)S(1)} %get-tuple-element.52.normed, bf16[1024,768]{1,0:T(8,128)(2,1)S(1)} %constant_dynamic-update-slice_fusion.8.weight, bf16[512,256]{1,0:T(8,128)(2,1)S(1)} %attention.6.refs_0_), custom_call_target="tpu_custom_call" | custom-call | flops 939524096 | bytes 3670016 | tf_op jit(solution)/shard_map/attention/pallas_call | solution.py:183
  62.2 4.3 %router.1 = (f32[512,1024]{1,0:T(8,128)S(1)}, bf16[2,32,256]{2,1,0:T(8,128)(2,1)S(1)}, bf16[2,32,1024]{2,1,0:T(8,128)(2,1)S(1)}) custom-call(bf16[512,1024]{1,0:T(8,128)(2,1)S(1)} %bitcast.9, bf16[32,1024]{1,0:T(8,128)(2,1)S(1)} %bitcast.12, bf16[512,256]{1,0:T(8,128)(2,1)S(1)} %attention.5.refs_3_.refs_2_, bf16[512,256]{1,0:T(8,128)(2,1)S(1)} %attention.7.refs_3_, ...), custom_call_target="tpu_custom_call" | custom-call | flops 1140850688 | bytes 6291456 | tf_op jit(solution)/shard_map/router/pallas_call | solution.py:251
  66.6 10.5 %all_to_all.10 = bf16[2,32,1024]{2,0,1:T(2,128)(2,1)S(1)} all-to-all(bf16[2,32,1024]{2,0,1:T(2,128)(2,1)S(1)} %copy.9), channel_id=1, replica_groups=mesh['group'=2,'expert'=16] {'expert'}, dimensions={1} | all-to-all | bytes 262144 | tf_op jit(solution)/shard_map/all_to_all | solution.py:451
  77.2 1.6 %experts.1 = bf16[1,64,1024]{2,1,0:T(8,128)(2,1)S(1)} custom-call(bf16[1,64,1024]{2,1,0:T(8,128)(2,1)S(1)} %bitcast.10, bf16[1,1024,2048]{2,1,0:T(8,128)(2,1)S(1)} %copy-done, bf16[1,2048,1024]{2,1,0:T(8,128)(2,1)S(1)} %copy-done.1), custom_call_target="tpu_custom_call" | custom-call | flops 536870912 | bytes 8388608 | tf_op jit(solution)/shard_map/experts/pallas_call | solution.py:297
  78.9 10.5 %all_to_all.11 = bf16[2,32,1024]{2,0,1:T(2,128)(2,1)S(1)} all-to-all(bf16[2,32,1024]{2,0,1:T(2,128)(2,1)S(1)} %copy.11), channel_id=1, replica_groups=mesh['group'=2,'expert'=16] {'expert'}, dimensions={1} | all-to-all | bytes 262144 | tf_op jit(solution)/shard_map/all_to_all | solution.py:457
  (100 shorter events, 19.3 us)
Async XLA Ops:
  3.1 12.3 %collective-permute-start.1 = (bf16[128,768]{1,0:T(8,128)(2,1)S(1)}, bf16[128,768]{1,0:T(8,128)(2,1)S(1)}, u32[]{:S(2)}, u32[]{:S(2)}) collective-permute-start(bf16[128,768]{1,0:T(8,128)(2,1)S(1)} %get-tuple-element.44.refs_0_), channel_id=1, source_target_pairs={{0,4},{1,5},{2,6},{3,7},{4,0},{5,1},{6,2},{7,3},{8,12},{9,13},{10,... | collective-permute-start | bytes 589832 | tf_op jit(solution)/shard_map/ppermute | solution.py:329
  6.1 11.8 %collective-permute-start.2 = (bf16[128,768]{1,0:T(8,128)(2,1)S(1)}, bf16[128,768]{1,0:T(8,128)(2,1)S(1)}, u32[]{:S(2)}, u32[]{:S(2)}) collective-permute-start(bf16[128,768]{1,0:T(8,128)(2,1)S(1)} %get-tuple-element.44.refs_0_), channel_id=1, source_target_pairs={{0,8},{1,9},{2,10},{3,11},{4,12},{5,13},{6,14},{7,15},{8,0},{9,1},... | collective-permute-start | bytes 589832 | tf_op jit(solution)/shard_map/ppermute | solution.py:329
  8.7 9.2 %collective-permute-start.3 = (bf16[128,768]{1,0:T(8,128)(2,1)S(1)}, bf16[128,768]{1,0:T(8,128)(2,1)S(1)}, u32[]{:S(2)}, u32[]{:S(2)}) collective-permute-start(bf16[128,768]{1,0:T(8,128)(2,1)S(1)} %get-tuple-element.44.refs_0_), channel_id=1, source_target_pairs={{0,2},{1,3},{2,0},{3,1},{4,6},{5,7},{6,4},{7,5},{8,10},{9,11},{10,... | collective-permute-start | bytes 589832 | tf_op jit(solution)/shard_map/ppermute | solution.py:329
  12.3 8.6 %collective-permute-start.4 = (bf16[128,768]{1,0:T(8,128)(2,1)S(1)}, bf16[128,768]{1,0:T(8,128)(2,1)S(1)}, u32[]{:S(2)}, u32[]{:S(2)}) collective-permute-start(bf16[128,768]{1,0:T(8,128)(2,1)S(1)} %get-tuple-element.50), channel_id=1, source_target_pairs={{0,2},{1,3},{2,0},{3,1},{4,6},{5,7},{6,4},{7,5},{8,10},{9,11},{10,... | collective-permute-start | bytes 589832 | tf_op jit(solution)/shard_map/ppermute | solution.py:329
  17.9 9.8 %collective-permute-start.6 = (bf16[128,768]{1,0:T(8,128)(2,1)S(1)}, bf16[128,768]{1,0:T(8,128)(2,1)S(1)}, u32[]{:S(2)}, u32[]{:S(2)}) collective-permute-start(bf16[128,768]{1,0:T(8,128)(2,1)S(1)} %get-tuple-element.54), channel_id=1, source_target_pairs={{0,16},{1,17},{2,18},{3,19},{4,20},{5,21},{6,22},{7,23},{8,24},{9,... | collective-permute-start | bytes 589832 | tf_op jit(solution)/shard_map/ppermute | solution.py:329
  19.4 7.8 %collective-permute-start.7 = (bf16[128,768]{1,0:T(8,128)(2,1)S(1)}, bf16[128,768]{1,0:T(8,128)(2,1)S(1)}, u32[]{:S(2)}, u32[]{:S(2)}) collective-permute-start(bf16[128,768]{1,0:T(8,128)(2,1)S(1)} %get-tuple-element.54), channel_id=1, source_target_pairs={{0,2},{1,3},{2,0},{3,1},{4,6},{5,7},{6,4},{7,5},{8,10},{9,11},{10,... | collective-permute-start | bytes 589832 | tf_op jit(solution)/shard_map/ppermute | solution.py:329
  20.9 8.4 %collective-permute-start.5 = (bf16[128,768]{1,0:T(8,128)(2,1)S(1)}, bf16[128,768]{1,0:T(8,128)(2,1)S(1)}, u32[]{:S(2)}, u32[]{:S(2)}) collective-permute-start(bf16[128,768]{1,0:T(8,128)(2,1)S(1)} %get-tuple-element.53), channel_id=1, source_target_pairs={{0,2},{1,3},{2,0},{3,1},{4,6},{5,7},{6,4},{7,5},{8,10},{9,11},{10,... | collective-permute-start | bytes 589832 | tf_op jit(solution)/shard_map/ppermute | solution.py:329
  21.5 9.6 %collective-permute-start.9 = (bf16[128,768]{1,0:T(8,128)(2,1)S(1)}, bf16[128,768]{1,0:T(8,128)(2,1)S(1)}, u32[]{:S(2)}, u32[]{:S(2)}) collective-permute-start(bf16[128,768]{1,0:T(8,128)(2,1)S(1)} %get-tuple-element.56), channel_id=1, source_target_pairs={{0,8},{1,9},{2,10},{3,11},{4,12},{5,13},{6,14},{7,15},{8,0},{9,1},... | collective-permute-start | bytes 589832 | tf_op jit(solution)/shard_map/ppermute | solution.py:329
  24.1 12.3 %collective-permute-start.14 = (bf16[512,1024]{1,0:T(8,128)(2,1)S(1)}, bf16[512,1024]{1,0:T(8,128)(2,1)S(1)}, u32[]{:S(2)}, u32[]{:S(2)}) collective-permute-start(bf16[512,1024]{1,0:T(8,128)(2,1)S(1)} %get-tuple-element.65), channel_id=1, source_target_pairs={{0,1},{1,0},{2,3},{3,2},{4,5},{5,4},{6,7},{7,6},{8,9},{9,8},{10,11... | collective-permute-start | bytes 3145736 | tf_op jit(solution)/shard_map/ppermute | solution.py:329
  27.2 5.7 %collective-permute-start.8 = (bf16[128,768]{1,0:T(8,128)(2,1)S(1)}, bf16[128,768]{1,0:T(8,128)(2,1)S(1)}, u32[]{:S(2)}, u32[]{:S(2)}) collective-permute-start(bf16[128,768]{1,0:T(8,128)(2,1)S(1)} %get-tuple-element.55), channel_id=1, source_target_pairs={{0,16},{1,17},{2,18},{3,19},{4,20},{5,21},{6,22},{7,23},{8,24},{9,... | collective-permute-start | bytes 589832 | tf_op jit(solution)/shard_map/ppermute | solution.py:329
  29.4 9.6 %collective-permute-start.13 = (bf16[128,768]{1,0:T(8,128)(2,1)S(1)}, bf16[128,768]{1,0:T(8,128)(2,1)S(1)}, u32[]{:S(2)}, u32[]{:S(2)}) collective-permute-start(bf16[128,768]{1,0:T(8,128)(2,1)S(1)} %get-tuple-element.63), channel_id=1, source_target_pairs={{0,4},{1,5},{2,6},{3,7},{4,0},{5,1},{6,2},{7,3},{8,12},{9,13},{10,... | collective-permute-start | bytes 589832 | tf_op jit(solution)/shard_map/ppermute | solution.py:329
  33.0 6.0 %collective-permute-start.12 = (bf16[128,768]{1,0:T(8,128)(2,1)S(1)}, bf16[128,768]{1,0:T(8,128)(2,1)S(1)}, u32[]{:S(2)}, u32[]{:S(2)}) collective-permute-start(bf16[128,768]{1,0:T(8,128)(2,1)S(1)} %get-tuple-element.62), channel_id=1, source_target_pairs={{0,2},{1,3},{2,0},{3,1},{4,6},{5,7},{6,4},{7,5},{8,10},{9,11},{10,... | collective-permute-start | bytes 589832 | tf_op jit(solution)/shard_map/ppermute | solution.py:329
  34.7 5.7 %collective-permute-start.15 = (bf16[128,768]{1,0:T(8,128)(2,1)S(1)}, bf16[128,768]{1,0:T(8,128)(2,1)S(1)}, u32[]{:S(2)}, u32[]{:S(2)}) collective-permute-start(bf16[128,768]{1,0:T(8,128)(2,1)S(1)} %get-tuple-element.62), channel_id=1, source_target_pairs={{0,16},{1,17},{2,18},{3,19},{4,20},{5,21},{6,22},{7,23},{8,24},{9,... | collective-permute-start | bytes 589832 | tf_op jit(solution)/shard_map/ppermute | solution.py:329
  35.0 7.3 %collective-permute-start.11 = (bf16[128,512]{1,0:T(8,128)(2,1)S(1)}, bf16[128,512]{1,0:T(8,128)(2,1)S(1)}, u32[]{:S(2)}, u32[]{:S(2)}) collective-permute-start(bf16[128,512]{1,0:T(8,128)(2,1)S(1)} %get-tuple-element.61), channel_id=1, source_target_pairs={{0,8},{1,9},{2,10},{3,11},{4,12},{5,13},{6,14},{7,15},{8,0},{9,1},... | collective-permute-start | bytes 393224 | tf_op jit(solution)/shard_map/ppermute | solution.py:329
  40.4 8.5 %collective-permute-start.22 = (bf16[128,512]{1,0:T(8,128)(2,1)S(1)}, bf16[128,512]{1,0:T(8,128)(2,1)S(1)}, u32[]{:S(2)}, u32[]{:S(2)}) collective-permute-start(bf16[128,512]{1,0:T(8,128)(2,1)S(1)} %get-tuple-element.73), channel_id=1, source_target_pairs={{0,2},{1,3},{2,0},{3,1},{4,6},{5,7},{6,4},{7,5},{8,10},{9,11},{10,... | collective-permute-start | bytes 393224 | tf_op jit(solution)/shard_map/ppermute | solution.py:329
  41.5 7.6 %collective-permute-start.19 = (bf16[128,512]{1,0:T(8,128)(2,1)S(1)}, bf16[128,512]{1,0:T(8,128)(2,1)S(1)}, u32[]{:S(2)}, u32[]{:S(2)}) collective-permute-start(bf16[128,512]{1,0:T(8,128)(2,1)S(1)} %get-tuple-element.73), channel_id=1, source_target_pairs={{0,4},{1,5},{2,6},{3,7},{4,0},{5,1},{6,2},{7,3},{8,12},{9,13},{10,... | collective-permute-start | bytes 393224 | tf_op jit(solution)/shard_map/ppermute | solution.py:329
  42.3 6.8 %collective-permute-start.18 = (bf16[128,512]{1,0:T(8,128)(2,1)S(1)}, bf16[128,512]{1,0:T(8,128)(2,1)S(1)}, u32[]{:S(2)}, u32[]{:S(2)}) collective-permute-start(bf16[128,512]{1,0:T(8,128)(2,1)S(1)} %get-tuple-element.72), channel_id=1, source_target_pairs={{0,2},{1,3},{2,0},{3,1},{4,6},{5,7},{6,4},{7,5},{8,10},{9,11},{10,... | collective-permute-start | bytes 393224 | tf_op jit(solution)/shard_map/ppermute | solution.py:329
  43.1 15.6 %collective-permute-start.24 = (bf16[128,512]{1,0:T(8,128)(2,1)S(1)}, bf16[128,512]{1,0:T(8,128)(2,1)S(1)}, u32[]{:S(2)}, u32[]{:S(2)}) collective-permute-start(bf16[128,512]{1,0:T(8,128)(2,1)S(1)} %get-tuple-element.72), channel_id=1, source_target_pairs={{0,16},{1,17},{2,18},{3,19},{4,20},{5,21},{6,22},{7,23},{8,24},{9,... | collective-permute-start | bytes 393224 | tf_op jit(solution)/shard_map/ppermute | solution.py:329
  45.2 5.7 %collective-permute-start.16 = (bf16[128,768]{1,0:T(8,128)(2,1)S(1)}, bf16[128,768]{1,0:T(8,128)(2,1)S(1)}, u32[]{:S(2)}, u32[]{:S(2)}) collective-permute-start(bf16[128,768]{1,0:T(8,128)(2,1)S(1)} %get-tuple-element.70), channel_id=1, source_target_pairs={{0,2},{1,3},{2,0},{3,1},{4,6},{5,7},{6,4},{7,5},{8,10},{9,11},{10,... | collective-permute-start | bytes 589832 | tf_op jit(solution)/shard_map/ppermute | solution.py:329
  48.9 7.1 %collective-permute-start.17 = (bf16[128,768]{1,0:T(8,128)(2,1)S(1)}, bf16[128,768]{1,0:T(8,128)(2,1)S(1)}, u32[]{:S(2)}, u32[]{:S(2)}) collective-permute-start(bf16[128,768]{1,0:T(8,128)(2,1)S(1)} %get-tuple-element.71), channel_id=1, source_target_pairs={{0,16},{1,17},{2,18},{3,19},{4,20},{5,21},{6,22},{7,23},{8,24},{9,... | collective-permute-start | bytes 589832 | tf_op jit(solution)/shard_map/ppermute | solution.py:329
  49.1 13.0 %collective-permute-start.26 = (bf16[640,512]{1,0:T(8,128)(2,1)S(1)}, bf16[640,512]{1,0:T(8,128)(2,1)S(1)}, u32[]{:S(2)}, u32[]{:S(2)}) collective-permute-start(bf16[640,512]{1,0:T(8,128)(2,1)S(1)} %constant_dynamic-update-slice_fusion.16.refs_6_), channel_id=1, source_target_pairs={{0,1},{1,0},{2,3},{3,2},{4,5},{5,4},{6,7},{7,6},{8,9},{9,8},{10,11... | collective-permute-start | bytes 1966088 | tf_op jit(solution)/shard_map/ppermute | solution.py:329
  50.9 7.7 %collective-permute-start.25 = (bf16[128,512]{1,0:T(8,128)(2,1)S(1)}, bf16[128,512]{1,0:T(8,128)(2,1)S(1)}, u32[]{:S(2)}, u32[]{:S(2)}) collective-permute-start(bf16[128,512]{1,0:T(8,128)(2,1)S(1)} %get-tuple-element.79), channel_id=1, source_target_pairs={{0,16},{1,17},{2,18},{3,19},{4,20},{5,21},{6,22},{7,23},{8,24},{9,... | collective-permute-start | bytes 393224 | tf_op jit(solution)/shard_map/ppermute | solution.py:329
  51.5 7.2 %collective-permute-start.23 = (bf16[128,512]{1,0:T(8,128)(2,1)S(1)}, bf16[128,512]{1,0:T(8,128)(2,1)S(1)}, u32[]{:S(2)}, u32[]{:S(2)}) collective-permute-start(bf16[128,512]{1,0:T(8,128)(2,1)S(1)} %get-tuple-element.78), channel_id=1, source_target_pairs={{0,2},{1,3},{2,0},{3,1},{4,6},{5,7},{6,4},{7,5},{8,10},{9,11},{10,... | collective-permute-start | bytes 393224 | tf_op jit(solution)/shard_map/ppermute | solution.py:329
  58.7 3.4 %collective-permute-start.27 = (bf16[400,512]{1,0:T(8,128)(2,1)S(1)}, bf16[400,512]{1,0:T(8,128)(2,1)S(1)}, u32[]{:S(2)}, u32[]{:S(2)}) collective-permute-start(bf16[400,512]{1,0:T(8,128)(2,1)S(1)} %maximum_maximum_fusion.refs_7_), channel_id=1, source_target_pairs={{0,1},{1,0},{2,3},{3,2},{4,5},{5,4},{6,7},{7,6},{8,9},{9,8},{10,11... | collective-permute-start | bytes 1228808 | tf_op jit(solution)/shard_map/ppermute | solution.py:329
  (11 other events, 63.7 us)
